TPU v7x, 512 devices: a whole 4x4x16 slice. The times are simulated.
512 devices in a mesh: gx: 32 (over x, y, core), gy: 16 (over z).
Axes of the slice: x: 4, y: 4, z: 16, core: 2. Of those that a mesh axis runs over, the one named last changes fastest.
Arguments:
- hidden_states: bfloat16 [16, 256, 2048], P('gy', 'gx'), may hold values from -500 to 500
- norm_gain: float32 [2048], replicated, may hold values from 0.1 to 1.9
- norm_bias: float32 [2048], replicated, may hold values from -3 to 3
- query_weight: bfloat16 [2048, 2048], P('gy', 'gx'), may hold values from -0.125 to 0.125
- keyvalue_weight: bfloat16 [2048, 256], P('gy', 'gx'), may hold values from -0.125 to 0.125
- out_weight: bfloat16 [2048, 2048], P('gx', 'gy'), may hold values from -0.75 to 0.75
- key_cache: bfloat16 [16, 2304, 128], P('gy', 'gx'), may hold values from -400 to 400
- value_cache: bfloat16 [16, 2304, 128], P('gy', 'gx'), may hold values from -6 to 6
- cache_length: int32 [16], P('gy'), may hold values from 0 to 2048, as said below
Outputs:
- attention_out: bfloat16 [16, 256, 2048], P('gy', 'gx')
- new_key_cache: bfloat16 [16, 2304, 128], P('gy', 'gx')
- new_value_cache: bfloat16 [16, 2304, 128], P('gy', 'gx')
Inputs may be any that keep to these rules, and one draw needn't show every extreme that they name: Request r holds cache_length[r] earlier tokens; its new tokens take positions cache_length[r] to cache_length[r] + 255. Some request holds exactly 2048.
All inputs are finite; a program needn't handle non-finite values.
Results may differ from a plain program's by a relative error of at most 0.012.
The roundings to bfloat16 on the way count: a program that leaves them out, or rounds other values in their place, can miss the bound.
Values may be sent and summed in bfloat16 or wider, within the bound.
No kernel may reach another device: no remote copies, remote signals or barrier semaphores. Data moves between devices by JAX's collectives and lax.ppermute only.
A program may use at most 192 MiB of HBM per device.

v0:
```python
import jax
import jax.numpy as jnp
from jax import lax
from jax.sharding import PartitionSpec as P

HEADS = 16


NEGATIVE = -1e30


def normalize(hidden_states, norm_gain, norm_bias):
    values = hidden_states.astype(jnp.float32)
    average = jnp.mean(values, axis=-1, keepdims=True)
    centred = values - average
    spread = jnp.mean(centred * centred, axis=-1, keepdims=True)
    return (centred * lax.rsqrt(spread + 1e-05) * norm_gain + norm_bias).astype(jnp.bfloat16)


def page_terms(query_rows, query_pos, key_rows, value_rows, page_size):
    row_count = query_rows.shape[0]
    head_dim = key_rows.shape[1]
    page_count = key_rows.shape[0] // page_size
    scores = lax.dot_general(
        query_rows, key_rows, (((1,), (1,)), ((), ())), preferred_element_type=jnp.float32
    )
    scores = (scores * head_dim ** (-0.5)).reshape(row_count, page_count, page_size)
    key_pos = jnp.arange(page_count * page_size, dtype=jnp.int32).reshape(page_count, page_size)
    allowed = key_pos[None, :, :] <= query_pos[:, None, None]
    maxima = jnp.max(jnp.where(allowed, scores, NEGATIVE), axis=2)
    weights = jnp.where(allowed, jnp.exp(scores - maxima[:, :, None]), 0.0)
    totals = jnp.sum(weights, axis=2)
    weighted = jnp.einsum(
        "rnp,npd->rnd",
        weights.astype(jnp.bfloat16),
        value_rows.reshape(page_count, page_size, head_dim),
        preferred_element_type=jnp.float32,
    )
    return (maxima, totals, weighted)


def reduce_pages(maxima, totals, weighted):
    largest = jnp.max(maxima, axis=1)
    factor = jnp.exp(maxima - largest[:, None])
    return (
        largest,
        jnp.sum(totals * factor, axis=1),
        jnp.sum(weighted * factor[:, :, None], axis=1),
    )


def join_pages(first, second):
    larger = jnp.maximum(first[0], second[0])
    second_factor = jnp.exp(second[0] - larger)
    return (larger, second[1] * second_factor, second[2] * second_factor[:, None])


def body(
    hidden_states,
    norm_gain,
    norm_bias,
    query_weight,
    keyvalue_weight,
    out_weight,
    key_cache,
    value_cache,
    cache_length,
):
    own_tokens = hidden_states.shape[1]
    groups = lax.axis_size("gx")
    column_index = lax.axis_index("gx")
    span_len = own_tokens * groups
    page_size = key_cache.shape[1]
    head_dim = key_cache.shape[2]
    head_count = HEADS
    head_width = head_count * head_dim
    normed = normalize(hidden_states[0], norm_gain, norm_bias)
    full_rows = lax.all_gather(normed, "gx", axis=0, tiled=True)
    pieces = (
        lax.all_gather(query_weight, "gy", axis=0, tiled=True),
        lax.all_gather(keyvalue_weight, "gy", axis=0, tiled=True),
    )
    query_part = jnp.dot(full_rows, pieces[0], preferred_element_type=jnp.float32)
    keyvalue_part = jnp.dot(full_rows, pieces[1], preferred_element_type=jnp.float32)
    query_local = query_part.astype(jnp.bfloat16)
    keyvalue_local = keyvalue_part.astype(jnp.bfloat16)
    queries, new_keyvalue = (
        lax.all_gather(query_local, "gx", axis=1, tiled=True),
        lax.all_gather(keyvalue_local, "gx", axis=1, tiled=True),
    )
    length = cache_length[0]
    page_base = column_index * page_size
    offsets = page_base + jnp.arange(page_size, dtype=jnp.int32) - length
    inside = (offsets >= 0) & (offsets < span_len)
    picked = jnp.take(new_keyvalue, jnp.clip(offsets, 0, span_len - 1), axis=0)
    key_page = jnp.where(inside[:, None], picked[:, :head_dim], key_cache[0])
    value_page = jnp.where(inside[:, None], picked[:, head_dim:], value_cache[0])
    own_rows = lax.dynamic_slice_in_dim(queries, column_index * own_tokens, own_tokens, 0)
    own_rows = own_rows.reshape(own_tokens * head_count, head_dim)
    own_pos = (
        length
        + column_index * own_tokens
        + jnp.arange(own_tokens * head_count, dtype=jnp.int32) // head_count
    )
    own_total = own_tokens * head_count
    empty = (
        jnp.full((own_total,), NEGATIVE, jnp.float32),
        jnp.zeros((own_total,), jnp.float32),
        jnp.zeros((own_total, head_dim), jnp.float32),
    )
    pieces = (
        lax.all_gather(key_page, "gx", axis=0, tiled=True),
        lax.all_gather(value_page, "gx", axis=0, tiled=True),
    )
    maxima, totals, weighted = page_terms(own_rows, own_pos, pieces[0], pieces[1], page_size)
    maxima, totals, weighted = join_pages(empty, reduce_pages(maxima, totals, weighted))
    own_out = (weighted / totals[:, None]).reshape(own_tokens, head_width).astype(jnp.bfloat16)
    attended = lax.all_to_all(own_out, "gx", split_axis=1, concat_axis=0, tiled=True)
    out_full = lax.all_gather(out_weight, "gy", axis=1, tiled=True)
    hidden_part = lax.psum_scatter(
        jnp.dot(attended, out_full, preferred_element_type=jnp.float32),
        "gx",
        scatter_dimension=0,
        tiled=True,
    )
    return (hidden_part.astype(jnp.bfloat16)[None], key_page[None], value_page[None])


def solution(mesh):
    return jax.shard_map(
        body,
        mesh=mesh,
        in_specs=(
            P("gy", "gx", None),
            P(),
            P(),
            P("gy", "gx"),
            P("gy", "gx"),
            P("gx", "gy"),
            P("gy", "gx", None),
            P("gy", "gx", None),
            P("gy"),
        ),
        out_specs=(P("gy", "gx", None), P("gy", "gx", None), P("gy", "gx", None)),
        check_vma=False,
    )
```

profile of v0, /device:TPU:1, one launch (start us, length us, event | category | flops | bytes accessed | tf_op | source)
XLA Modules:
  0.0 328.2 jit_solution(9037517060432647469)
XLA Ops:
  7.2 0.0 all-gather.3.cloned.1.call-start
  7.2 0.9 convert_reduce_fusion
  8.1 1.0 fusion.12
  9.1 1.5 fusion.15
  10.6 0.0 all-gather.3.cloned.1.call-update
  10.6 0.0 all-gather.5.cloned.1.call-start
  10.6 30.7 %all_gather.28 = bf16[2048,64]{0,1:T(8,128)(2,1)S(1)} all-gather(bf16[128,64]{0,1:T(8,128)(2,1)} %param.12), channel_id=1, replica_groups=mesh['gx'=32,'gy'=16] {'gy'}, dimensions={0}, use_global_device_ids=true | all-gather | bytes 278528 | tf_op jit(solution)/shard_map/all_gather | solution.py:80
  41.3 34.3 %all-gather.3.cloned.1.call-done = bf16[256,2048]{1,0:T(8,128)(2,1)} async-done(((bf16[8,2048]{1,0:T(8,128)(2,1)}), bf16[256,2048]{1,0:T(8,128)(2,1)}) %all-gather.3.cloned.1.call-update) | async-done | bytes 1048592 | tf_op jit(solution)/shard_map/all_gather | solution.py:78
  75.6 2.4 convolution_convert_fusion
  78.0 0.0 all-gather.5.cloned.1.call-update
  78.7 0.1 broadcast_in_dim_reshape.16
  78.8 23.8 %all_gather.25 = bf16[2048,8]{0,1:T(8,128)(2,1)S(1)} all-gather(bf16[128,8]{0,1:T(8,128)(2,1)S(1)} %copy-done.6), channel_id=1, replica_groups=mesh['gx'=32,'gy'=16] {'gy'}, dimensions={0}, use_global_device_ids=true | all-gather | bytes 34816 | tf_op jit(solution)/shard_map/all_gather | solution.py:81
  102.7 0.4 convolution_convert_fusion.1
  103.0 30.5 %all_gather.26 = bf16[256,256]{0,1:T(8,128)(2,1)S(1)} all-gather(bf16[256,8]{0,1:T(8,128)(2,1)S(1)} %convolution_convert_fusion.1), channel_id=1, replica_groups=mesh['gx'=32,'gy'=16] {'gx'}, dimensions={1}, use_global_device_ids=true | all-gather | bytes 135168 | tf_op jit(solution)/shard_map/all_gather | solution.py:89
  133.5 0.1 copy.28
  133.6 0.7 gather_fusion
  134.3 0.1 broadcast_select_fusion
  134.4 0.1 slice_select_fusion
  134.5 0.0 copy-start.1
  134.5 0.0 copy-start.2
  134.6 22.7 %all_gather.30 = bf16[2304,128]{1,0:T(8,128)(2,1)S(1)} all-gather(bf16[72,128]{1,0:T(8,128)(2,1)S(1)} %get-tuple-element.5), channel_id=1, replica_groups=mesh['gx'=32,'gy'=16] {'gx'}, dimensions={0}, use_global_device_ids=true | all-gather | bytes 608256 | tf_op jit(solution)/shard_map/all_gather | solution.py:112
  157.2 24.1 %all_gather.27 = bf16[2304,128]{1,0:T(8,128)(2,1)S(1)} all-gather(bf16[72,128]{1,0:T(8,128)(2,1)S(1)} %get-tuple-element.6), channel_id=1, replica_groups=mesh['gx'=32,'gy'=16] {'gx'}, dimensions={0}, use_global_device_ids=true | all-gather | bytes 608256 | tf_op jit(solution)/shard_map/all_gather | solution.py:113
  181.3 1.3 constant_dynamic-slice_fusion
  182.6 0.2 copy.29
  182.8 0.4 select_reduce_fusion
  183.2 0.4 copy.30
  183.6 0.5 fusion.1
  184.1 0.5 fusion.2
  184.6 0.1 reduce_max.22
  184.7 0.1 reduce_sum.55
  184.8 0.1 copy.32
  184.8 0.1 copy.33
  184.9 0.1 copy.34
  185.0 0.1 copy.35
  185.1 1.1 fusion
  186.2 0.1 copy.31
  186.3 0.1 reduce_sum.52
  186.4 0.1 divide_convert_fusion
  186.6 0.7 reshape.153
  187.3 4.2 %all-to-all-start = ((bf16[32,2,256]{2,1,0:T(2,128)(2,1)}), bf16[32,2,256]{2,1,0:T(2,128)(2,1)S(1)}, u32[]{:S(2)}, u32[]{:S(2)}) async-start(bf16[32,2,256]{2,1,0:T(2,128)(2,1)} %reshape.153), calls=%async_computation | async-start | bytes 65536 | tf_op jit(solution)/shard_map/all_to_all | solution.py:118
  191.6 0.0 reduce-scatter.2.cloned.1.call-start
  191.6 22.0 %all_gather.31 = bf16[64,2048]{1,0:T(8,128)(2,1)S(1)} all-gather(bf16[64,128]{1,0:T(8,128)(2,1)S(1)} %copy-done.5), channel_id=1, replica_groups=mesh['gx'=32,'gy'=16] {'gy'}, dimensions={1}, use_global_device_ids=true | all-gather | bytes 278528 | tf_op jit(solution)/shard_map/all_gather | solution.py:119
  213.6 0.0 all-to-all-done
  213.6 0.1 reshape.154
  213.7 1.8 fusion.16
  215.5 0.0 reduce-scatter.2.cloned.1.call-update
  215.5 104.7 %reduce-scatter.2.cloned.1.call-done = f32[8,2048]{1,0:T(8,128)} async-done(((f32[256,2048]{1,0:T(8,128)}), f32[8,2048]{1,0:T(8,128)}) %reduce-scatter.2.cloned.1.call-update) | async-done | bytes 65552 | tf_op jit(solution)/shard_map/reduce_scatter | solution.py:120
  320.2 1.5 convert_bitcast_fusion.1
  (27 shorter events, 0.2 us)
Async XLA Ops:
  7.2 71.6 %copy-start.6 = (bf16[128,8]{0,1:T(8,128)(2,1)S(1)}, bf16[128,8]{0,1:T(8,128)(2,1)}, u32[]{:S(2)}) copy-start(bf16[128,8]{0,1:T(8,128)(2,1)} %param.13) | copy-start | bytes 6148
  7.2 68.4 %all-gather.3.cloned.1.call-start = ((), (), s32[]{:S(2)}) async-start(), calls=%async_computation.2 | async-start | bytes 1081344 | tf_op jit(solution)/shard_map/all_gather | solution.py:78
  10.6 170.7 %all-gather.5.cloned.1.call-start = ((), (), s32[]{:S(2)}) async-start(), calls=%async_computation.3 | async-start | bytes 1081344 | tf_op jit(solution)/shard_map/all_gather | solution.py:88
  75.6 27.1 %copy-start = (bf16[256,2048]{1,0:T(8,128)(2,1)S(1)}, bf16[256,2048]{1,0:T(8,128)(2,1)}, u32[]{:S(2)}) copy-start(bf16[256,2048]{1,0:T(8,128)(2,1)} %all-gather.3.cloned.1.call-done) | copy-start | bytes 3145732
  78.0 56.4 %copy-start.3 = (bf16[1,72,128]{2,1,0:T(8,128)(2,1)S(1)}, bf16[1,72,128]{2,1,0:T(8,128)(2,1)}, u32[]{:S(2)}) copy-start(bf16[1,72,128]{2,1,0:T(8,128)(2,1)} %param.15) | copy-start | bytes 55300
  78.0 56.5 %copy-start.4 = (bf16[1,72,128]{2,1,0:T(8,128)(2,1)S(1)}, bf16[1,72,128]{2,1,0:T(8,128)(2,1)}, u32[]{:S(2)}) copy-start(bf16[1,72,128]{2,1,0:T(8,128)(2,1)} %param.16) | copy-start | bytes 55300
  134.5 48.2 %copy-start.1 = (bf16[72,128]{1,0:T(8,128)(2,1)}, bf16[72,128]{1,0:T(8,128)(2,1)S(1)}, u32[]{:S(2)}) copy-start(bf16[72,128]{1,0:T(8,128)(2,1)S(1)} %get-tuple-element.5) | copy-start | bytes 55300
  134.5 48.2 %copy-start.2 = (bf16[72,128]{1,0:T(8,128)(2,1)}, bf16[72,128]{1,0:T(8,128)(2,1)S(1)}, u32[]{:S(2)}) copy-start(bf16[72,128]{1,0:T(8,128)(2,1)S(1)} %get-tuple-element.6) | copy-start | bytes 55300
  185.1 6.5 %copy-start.5 = (bf16[64,128]{1,0:T(8,128)(2,1)S(1)}, bf16[64,128]{1,0:T(8,128)(2,1)}, u32[]{:S(2)}) copy-start(bf16[64,128]{1,0:T(8,128)(2,1)} %param.14) | copy-start | bytes 49156
  187.3 26.3 %all-to-all-start = ((bf16[32,2,256]{2,1,0:T(2,128)(2,1)}), bf16[32,2,256]{2,1,0:T(2,128)(2,1)S(1)}, u32[]{:S(2)}, u32[]{:S(2)}) async-start(bf16[32,2,256]{2,1,0:T(2,128)(2,1)} %reshape.153), calls=%async_computation | async-start | bytes 65536 | tf_op jit(solution)/shard_map/all_to_all | solution.py:118
  191.6 128.7 %reduce-scatter.2.cloned.1.call-start = ((), (), s32[]{:S(2)}) async-start(), calls=%async_computation.4 | async-start | bytes 2162688 | tf_op jit(solution)/shard_map/reduce_scatter | solution.py:120
Sparse Core Ops, SparseCore 0:
  11.7 63.8 all-gather.2
  79.3 57.5 all-gather.4
  215.7 104.5 reduce-scatter.1
where the time goes:
time: 329 us; the launch traced here: 328 us
  blocking collectives  154 us (47%)
  waiting for transfers between devices  139 us (42%)
  between operations  14.6 us (4%)
  other arithmetic  6.12 us (2%)
  matrix products  6.05 us (2%)
  starting transfers between devices  4.37 us (1%)
  local copies, waits for them, and re-layouts  4.27 us (1%)
    reduce_scatter x1, waiting for transfers between devices, body(): lax.psum_scatter(jnp.dot(attended, out_full, preferred_element_type=jnp.f...  105 us
    all_gather x1, waiting for transfers between devices, body(): full_rows = lax.all_gather(normed, 'gx', axis=0, tiled=True)  34.3 us
    all_gather x1, blocking collectives, body(): lax.all_gather(query_weight, 'gy', axis=0, tiled=True)  30.7 us
    all_gather x1, blocking collectives, body(): lax.all_gather(keyvalue_local, 'gx', axis=1, tiled=True)  30.5 us
    all_gather x1, blocking collectives, body(): lax.all_gather(value_page, 'gx', axis=0, tiled=True)  24.1 us
    all_gather x1, blocking collectives, body(): lax.all_gather(keyvalue_weight, 'gy', axis=0, tiled=True)  23.8 us
    all_gather x1, blocking collectives, body(): lax.all_gather(key_page, 'gx', axis=0, tiled=True)  22.7 us
    all_gather x1, blocking collectives, body(): out_full = lax.all_gather(out_weight, 'gy', axis=1, tiled=True)  22 us
  transfers between devices with their start and end apart: 4, of which 2 were waited for; matrix products, arithmetic and copies ran while one was open for 0% of the time, Pallas kernels for 0%

commit v1 on v0

v1 whole, which is shorter than its diff:
```python
import jax
import jax.numpy as jnp
from jax import lax
from jax.experimental import pallas as pl
from jax.experimental.pallas import tpu as pltpu
from jax.sharding import PartitionSpec as P

CHIPS = 16
CORES = 2
LANES = 128
HALF = 64
PAGE = 72
OWN = 8
FEATURES = 2048
CHUNKS = FEATURES // LANES
KV_ROWS = 2 * PAGE
SEND_ROWS = KV_ROWS + OWN * CHUNKS
WEIGHT_ROWS = HALF + OWN
NEW = 256
NEGATIVE = -1e30

SAME_CORE = [[CORES * chip + core for chip in range(CHIPS)] for core in range(CORES)]
ONE_CHIP = [[CORES * chip + core for core in range(CORES)] for chip in range(CHIPS)]
SWAP = [(place, place ^ 1) for place in range(CHIPS * CORES)]

F32 = jnp.float32
BF16 = jnp.bfloat16


def dot(a, b):
    return lax.dot_general(a, b, (((1,), (0,)), ((), ())), preferred_element_type=F32)


def dot_nt(a, b):
    return lax.dot_general(a, b, (((1,), (1,)), ((), ())), preferred_element_type=F32)


def iota(shape, dim):
    return lax.broadcasted_iota(jnp.int32, shape, dim)


def eye(rows, columns, shift):
    return (iota((rows, columns), 0) + shift == iota((rows, columns), 1)).astype(F32).astype(BF16)


def prepare(hidden, gain, bias, query_w, keyvalue_w, out_w, key_page, value_page, send, weights):
    values = hidden[...].astype(F32)
    average = jnp.mean(values, axis=-1, keepdims=True)
    centred = values - average
    spread = jnp.mean(centred * centred, axis=-1, keepdims=True)
    normed = (centred * lax.rsqrt(spread + 1e-05) * gain[...] + bias[...]).astype(BF16)
    key_rows = key_page[...]
    value_rows = value_page[...]
    for chip in range(CHIPS):
        send[chip, 0:PAGE, :] = key_rows
        send[chip, PAGE:KV_ROWS, :] = value_rows
        for chunk in range(CHUNKS):
            send[chip, KV_ROWS + OWN * chunk : KV_ROWS + OWN * (chunk + 1), :] = normed[
                :, LANES * chunk : LANES * (chunk + 1)
            ]
    packed = dot(query_w[0:HALF, :], eye(HALF, LANES, 0)) + dot(query_w[HALF:LANES, :], eye(HALF, LANES, HALF))
    weights[0:HALF, :] = packed.astype(BF16)
    weights[HALF:WEIGHT_ROWS, :] = dot_nt(eye(OWN, OWN, 0), keyvalue_w[...]).astype(BF16)
    weights[WEIGHT_ROWS : WEIGHT_ROWS + HALF, :] = out_w[...]


def project(tokens, weights, queries, keyvalue):
    low = iota((HALF, LANES), 1) < HALF
    query_sum = jnp.zeros((LANES, LANES), F32)
    keyvalue_sum = jnp.zeros((CORES * OWN, LANES), F32)
    for chunk in range(CHUNKS):
        first = KV_ROWS + OWN * chunk
        rows = tokens[:, first : first + OWN, :].astype(F32).reshape(LANES, LANES).astype(BF16)
        left = weights[0, chunk, 0:HALF, :].astype(F32)
        right = weights[1, chunk, 0:HALF, :].astype(F32)
        upper = jnp.where(low, left, pltpu.roll(right, HALF, 1))
        lower = jnp.where(low, pltpu.roll(left, HALF, 1), right)
        square = jnp.concatenate([upper, lower], axis=0).astype(BF16)
        query_sum = query_sum + dot(rows, square)
        narrow = jnp.concatenate(
            [
                weights[0, chunk, HALF:WEIGHT_ROWS, :].astype(F32),
                weights[1, chunk, HALF:WEIGHT_ROWS, :].astype(F32),
            ],
            axis=0,
        ).astype(BF16)
        keyvalue_sum = keyvalue_sum + dot_nt(narrow, rows)
    queries[...] = query_sum.astype(BF16)
    rounded = keyvalue_sum.astype(BF16)
    for place in range(CHIPS * CORES):
        keyvalue[place] = rounded


def new_columns(keyvalue, core, first):
    return jnp.concatenate([keyvalue[CORES * chip + core] for chip in range(first, first + CHIPS // 2)], axis=0)


def token_of(index, core):
    return ((index >> 3) << 4) + OWN * core + (index & 7)


def attend(length_ref, core_ref, queries, own, peer, keyvalue, out_w, result):
    length = length_ref[0]
    core = core_ref[0]
    scale = float(LANES) ** (-0.5)
    query_rows = queries[...]
    places = CHIPS * PAGE
    lane = iota((1, places), 1)
    start = lane + PAGE * ((lane * 911) >> 16)
    scored = []
    value_sets = []
    for source, side in ((own, core), (peer, 1 - core)):
        keys = source[:, 0:PAGE, :].astype(F32).reshape(places, LANES).astype(BF16)
        value_sets.append(source[:, PAGE:KV_ROWS, :].astype(F32).reshape(places, LANES).astype(BF16))
        scores = dot_nt(query_rows, keys) * scale
        scored.append(jnp.where(start + PAGE * side < length, scores, NEGATIVE))
    own_token = token_of(iota((LANES, LANES), 0), core)
    for side in range(CORES):
        scores = dot(query_rows, new_columns(keyvalue, side, 0)) * scale
        scored.append(jnp.where(token_of(iota((LANES, LANES), 1), side) <= own_token, scores, NEGATIVE))
    largest = jnp.max(scored[0], axis=1, keepdims=True)
    for scores in scored[1:]:
        largest = jnp.maximum(largest, jnp.max(scores, axis=1, keepdims=True))
    total = jnp.zeros((LANES, 1), F32)
    summed = jnp.zeros((LANES, LANES), F32)
    for which, scores in enumerate(scored):
        terms = jnp.exp(scores - largest)
        total = total + jnp.sum(terms, axis=1, keepdims=True)
        if which < 2:
            summed = summed + dot(terms.astype(BF16), value_sets[which])
        else:
            summed = summed + dot_nt(terms.astype(BF16), new_columns(keyvalue, which - 2, CHIPS // 2))
    attended = (summed / total).astype(BF16)
    for chunk in range(CHUNKS):
        square = jnp.concatenate([out_w[0, chunk], out_w[1, chunk]], axis=0)
        part = dot(attended, square)
        result[:, OWN * chunk : OWN * (chunk + 1), :] = part.reshape(CHIPS, OWN, LANES)


def add_heads(parts, result):
    total = parts[0]
    for chip in range(1, CHIPS):
        total = total + parts[chip]
    for chunk in range(CHUNKS):
        result[:, LANES * chunk : LANES * (chunk + 1)] = total[OWN * chunk : OWN * (chunk + 1), :].astype(BF16)


def write_pages(length_ref, place_ref, keyvalue, key_page, value_page, new_key, new_value):
    length = length_ref[0]
    base = place_ref[0] * PAGE - length
    offset = iota((PAGE, LANES), 0) + base
    inside = (offset >= 0) & (offset < NEW)
    key_rows = jnp.zeros((PAGE, LANES), F32)
    value_rows = jnp.zeros((PAGE, LANES), F32)
    for side in range(CORES):
        chosen = (offset == token_of(iota((PAGE, LANES), 1), side)).astype(F32).astype(BF16)
        key_rows = key_rows + dot_nt(chosen, new_columns(keyvalue, side, 0))
        value_rows = value_rows + dot_nt(chosen, new_columns(keyvalue, side, CHIPS // 2))
    new_key[...] = jnp.where(inside, key_rows, key_page[...].astype(F32)).astype(BF16)
    new_value[...] = jnp.where(inside, value_rows, value_page[...].astype(F32)).astype(BF16)


def call(kernel, shapes, arguments, scalars=0):
    specs = [
        pl.BlockSpec(memory_space=pltpu.SMEM if at < scalars else pltpu.VMEM) for at in range(len(arguments))
    ]
    return pl.pallas_call(
        kernel,
        out_shape=[jax.ShapeDtypeStruct(shape, dtype) for shape, dtype in shapes],
        in_specs=specs,
        out_specs=[pl.BlockSpec(memory_space=pltpu.VMEM)] * len(shapes),
        compiler_params=pltpu.CompilerParams(vmem_limit_bytes=48 * 1024 * 1024),
    )(*arguments)


def body(
    hidden_states,
    norm_gain,
    norm_bias,
    query_weight,
    keyvalue_weight,
    out_weight,
    key_cache,
    value_cache,
    cache_length,
):
    place = lax.axis_index("gx").astype(jnp.int32).reshape(1)
    core = place & 1
    send, weights = call(
        prepare,
        [((CHIPS, SEND_ROWS, LANES), BF16), ((WEIGHT_ROWS + HALF, LANES), BF16)],
        (
            hidden_states[0],
            norm_gain.reshape(1, FEATURES),
            norm_bias.reshape(1, FEATURES),
            query_weight,
            keyvalue_weight,
            out_weight,
            key_cache[0],
            value_cache[0],
        ),
    )
    own = lax.all_to_all(send, "gx", 0, 0, tiled=True, axis_index_groups=SAME_CORE)
    planes = lax.all_gather(weights, "gy", axis=0, tiled=False)
    inner = lax.all_gather(planes[:, :WEIGHT_ROWS], "gx", axis=0, tiled=False, axis_index_groups=ONE_CHIP)
    queries, rows = call(
        project,
        [((LANES, LANES), BF16), ((CHIPS * CORES, CORES * OWN, LANES), BF16)],
        (own, inner),
    )
    keyvalue = lax.all_to_all(rows, "gx", 0, 0, tiled=True)
    peer = lax.ppermute(own[:, :KV_ROWS], "gx", SWAP)
    outer = lax.all_gather(planes[:, WEIGHT_ROWS:], "gx", axis=0, tiled=False, axis_index_groups=ONE_CHIP)
    (parts,) = call(
        attend,
        [((CHIPS, LANES, LANES), F32)],
        (cache_length, core, queries, own, peer, keyvalue, outer),
        scalars=2,
    )
    collected = lax.all_to_all(parts, "gx", 0, 0, tiled=True, axis_index_groups=SAME_CORE)
    new_key, new_value = call(
        write_pages,
        [((PAGE, LANES), BF16), ((PAGE, LANES), BF16)],
        (cache_length, place, keyvalue, key_cache[0], value_cache[0]),
        scalars=2,
    )
    (out,) = call(add_heads, [((OWN, FEATURES), BF16)], (collected,))
    return (out[None], new_key[None], new_value[None])


def solution(mesh):
    return jax.shard_map(
        body,
        mesh=mesh,
        in_specs=(
            P("gy", "gx", None),
            P(),
            P(),
            P("gy", "gx"),
            P("gy", "gx"),
            P("gx", "gy"),
            P("gy", "gx", None),
            P("gy", "gx", None),
            P("gy"),
        ),
        out_specs=(P("gy", "gx", None), P("gy", "gx", None), P("gy", "gx", None)),
        check_vma=False,
    )
```

time: 329 us -> 113 us (0.34)
  waiting for transfers between devices: 139 us -> 21.2 us
  blocking collectives: 154 us -> 65.5 us
  between operations: 14.6 us -> 1.36 us
  starting transfers between devices: 4.37 us -> 13 us
  other arithmetic: 6.12 us -> 0 us
  matrix products: 6.05 us -> 0 us
  Pallas kernels: 0 us -> 5.25 us
    all_gather x6 -> x3, blocking collectives: 154 us -> 42.7 us  [the longest x1 31.5 us: body(): planes = lax.all_gather(weights, 'gy', axis=0, tiled=False)]
    reduce_scatter x1 -> x0, waiting for transfers between devices: 105 us -> none  [body(): lax.psum_scatter(jnp.dot(attended, out_full, preferred_element_type=jnp.f...]
    all_gather x2 -> x0, waiting for transfers between devices: 34.3 us -> none  [the longest x1 34.3 us: body(): full_rows = lax.all_gather(normed, 'gx', axis=0, tiled=True)]
    all_to_all x0 -> x1, blocking collectives: none -> 22.8 us  [body(): lax.all_to_all(send, 'gx', 0, 0, tiled=True, axis_index_groups=SAME_CORE)]
    all_to_all x1 -> x2, waiting for transfers between devices: 0.01 us -> 21.2 us  [the longest x1 15.6 us: body(): lax.all_to_all(parts, 'gx', 0, 0, tiled=True, axis_index_groups=SAME_CORE)]
    dot_general x5 -> x0, matrix products: 6.05 us -> none  [the longest x1 2.38 us: body(): jnp.dot(full_rows, pieces[0], preferred_element_type=jnp.float32)]
    ppermute x0 -> x1, starting transfers between devices: none -> 5.31 us  [body(): peer = lax.ppermute(own[:, :KV_ROWS], 'gx', SWAP)]
    pallas_call x0 -> x5, Pallas kernels: none -> 5.25 us  [call(): pl.pallas_call(kernel, out_shape=[jax.ShapeDtypeStruct(shape, dtype) for...]
  transfers between devices with their start and end apart: 4 -> 3, of which waited for: 2 -> 2; matrix products, arithmetic and copies ran while one was open for 0% -> 0% of each run, Pallas kernels for 0% -> 2%
where the time goes in v1:
time: 113 us; the launch traced here: 112 us
  blocking collectives  65.5 us (58%)
  waiting for transfers between devices  21.2 us (19%)
  starting transfers between devices  13 us (12%)
  local copies, waits for them, and re-layouts  6.03 us (5%)
  Pallas kernels  5.25 us (5%)
  between operations  1.36 us (1%)
    all_gather x1, blocking collectives, body(): planes = lax.all_gather(weights, 'gy', axis=0, tiled=False)  31.5 us
    all_to_all x1, blocking collectives, body(): lax.all_to_all(send, 'gx', 0, 0, tiled=True, axis_index_groups=SAME_CORE)  22.8 us
    all_to_all x1, waiting for transfers between devices, body(): lax.all_to_all(parts, 'gx', 0, 0, tiled=True, axis_index_groups=SAME_CORE)  15.6 us
    all_gather x1, blocking collectives, body(): lax.all_gather(planes[:, :WEIGHT_ROWS], 'gx', axis=0, tiled=False, axis_i...  9.03 us
    unnamed x18, local copies, waits for them, and re-layouts  5.95 us
    all_to_all x1, waiting for transfers between devices, body(): keyvalue = lax.all_to_all(rows, 'gx', 0, 0, tiled=True)  5.62 us
    ppermute x1, starting transfers between devices, body(): peer = lax.ppermute(own[:, :KV_ROWS], 'gx', SWAP)  5.31 us
    pallas_call x5, Pallas kernels, call(): pl.pallas_call(kernel, out_shape=[jax.ShapeDtypeStruct(shape, dtype) for...  5.25 us
  transfers between devices with their start and end apart: 3, of which 2 were waited for; matrix products, arithmetic and copies ran while one was open for 0% of the time, Pallas kernels for 2%

profile of v1, /device:TPU:1, one launch (start us, length us, event | category | flops | bytes accessed | tf_op | source)
XLA Modules:
  0.0 112.4 jit_solution(7604391784156295525)
XLA Ops:
  0.6 0.8 copy.14.query_w
  1.5 0.8 copy.15.keyvalue_w
  2.3 0.0 copy-start
  2.3 0.7 copy-done
  3.0 0.0 copy-start.2
  3.0 0.7 copy-done.2
  3.7 0.0 copy-start.4
  3.7 0.8 copy-done.4
  4.5 0.0 copy-start.5
  4.5 0.7 copy-done.5
  5.2 0.0 copy-start.6
  5.2 0.7 copy-done.6
  5.9 0.0 copy-start.7
  5.9 0.7 copy-done.7
  6.6 0.2 shard_map.112
  6.8 22.8 %all_to_all.15.tokens.own = bf16[16,272,128]{2,1,0:T(8,128)(2,1)S(1)} all-to-all(bf16[16,272,128]{2,1,0:T(8,128)(2,1)S(1)} %get-tuple-element.9), channel_id=1, replica_groups={{0,32,64,96,128,160,192,224,256,288,320,352,384,416,448,480},{16,48,80,..., dimensions={0} | all-to-all | bytes 2228224 | tf_op jit(solution)/shard_map/all_to_all | solution.py:203
  29.6 5.3 %collective-permute-start = (bf16[16,144,128]{2,1,0:T(8,128)(2,1)S(1)}, bf16[16,144,128]{2,1,0:T(8,128)(2,1)S(1)}, u32[]{:S(2)}, u32[]{:S(2)}) collective-permute-start(bf16[16,144,128]{2,1,0:T(8,128)(2,1)S(1)} %slice.13), channel_id=1, source_target_pairs={{0,16},{16,0},{32,48},{48,32},{64,80},{80,64},{96,112},{112,96},{1... | collective-permute-start | bytes 1769480 | tf_op jit(solution)/shard_map/ppermute | solution.py:212
  35.0 31.5 %all-gather = bf16[2176,128]{1,0:T(8,128)(2,1)S(1)} all-gather(bf16[136,128]{1,0:T(8,128)(2,1)S(1)} %get-tuple-element.10), channel_id=2, replica_groups=mesh['gx'=32,'gy'=16] {'gy'}, dimensions={0}, use_global_device_ids=true | all-gather | bytes 591872 | tf_op jit(solution)/shard_map/all_gather | solution.py:204
  67.2 9.0 %all-gather.1 = bf16[32,72,128]{2,1,0:T(8,128)(2,1)S(1)} all-gather(bf16[16,72,128]{2,1,0:T(8,128)(2,1)S(1)} %slice.12), channel_id=3, replica_groups={{0,16},{32,48},{64,80},{96,112},{128,144},{160,176},{192,208},{224,240}..., dimensions={0}, use_global_device_ids=true | all-gather | bytes 884736 | tf_op jit(solution)/shard_map/all_gather | solution.py:205
  76.2 1.3 %shard_map.113 = (bf16[128,128]{1,0:T(8,128)(2,1)S(1)}, bf16[32,16,128]{2,1,0:T(8,128)(2,1)}) custom-call(bf16[16,272,128]{2,1,0:T(8,128)(2,1)S(1)} %all_to_all.15.tokens.own, bf16[2,16,72,128]{3,2,1,0:T(8,128)(2,1)S(1)} %bitcast.12), custom_call_target="tpu_custom_call" | custom-call | tf_op jit(solution)/shard_map/pallas_call | solution.py:167
  77.5 3.9 %all-to-all-start.1 = ((bf16[32,16,128]{2,1,0:T(8,128)(2,1)}), bf16[32,16,128]{2,1,0:T(8,128)(2,1)S(1)}, u32[]{:S(2)}, u32[]{:S(2)}) async-start(bf16[32,16,128]{2,1,0:T(8,128)(2,1)} %get-tuple-element.12), calls=%async_computation.1 | async-start | bytes 262144 | tf_op jit(solution)/shard_map/all_to_all | solution.py:211
  81.4 2.2 %all-gather.2 = bf16[32,64,128]{2,1,0:T(8,128)(2,1)S(1)} all-gather(bf16[16,64,128]{2,1,0:T(8,128)(2,1)S(1)} %slice.14), channel_id=4, replica_groups={{0,16},{32,48},{64,80},{96,112},{128,144},{160,176},{192,208},{224,240}..., dimensions={0}, use_global_device_ids=true | all-gather | bytes 786432 | tf_op jit(solution)/shard_map/all_gather | solution.py:213
  83.6 5.6 %all-to-all-done.1.keyvalue = bf16[32,16,128]{2,1,0:T(8,128)(2,1)S(1)} async-done(((bf16[32,16,128]{2,1,0:T(8,128)(2,1)}), bf16[32,16,128]{2,1,0:T(8,128)(2,1)S(1)}, u32[]{:S(2)}, u32[]{:S(2)}) %all-to-all-start.1) | async-done | bytes 131104 | tf_op jit(solution)/shard_map/all_to_all | solution.py:211
  89.2 0.0 collective-permute-done.peer
  89.2 2.2 %shard_map.114 = f32[16,128,128]{2,1,0:T(8,128)} custom-call(s32[1]{0:T(128)S(6)} %copy.16.length_ref, s32[1]{0:T(128)S(6)} %and.4.core_ref, bf16[128,128]{1,0:T(8,128)(2,1)S(1)} %get-tuple-element.11.queries, bf16[16,272,128]{2,1,0:T(8,128)(2,1)S(1)} %all_to_all.15.tokens.own, bf16[16,144,128]{2,1,0:T(8,128)(2,1)S(1)} %collective-permute-done.peer, ...), custom_call_target="tpu_custom_call" | custom-call | tf_op jit(solution)/shard_map/pallas_call | solution.py:167
  91.4 0.0 copy-start.1
  91.4 0.0 copy-start.3
  91.4 3.8 %all-to-all-start.2 = ((f32[16,128,128]{2,1,0:T(8,128)}), f32[16,128,128]{2,1,0:T(8,128)S(1)}, u32[]{:S(2)}, u32[]{:S(2)}) async-start(f32[16,128,128]{2,1,0:T(8,128)} %shard_map.114), calls=%async_computation.2 | async-start | bytes 2097152 | tf_op jit(solution)/shard_map/all_to_all | solution.py:220
  95.2 0.0 copy-done.1
  95.2 0.0 copy-done.3
  95.2 0.8 shard_map.116
  96.1 15.6 %all-to-all-done.2.parts = f32[16,128,128]{2,1,0:T(8,128)S(1)} async-done(((f32[16,128,128]{2,1,0:T(8,128)}), f32[16,128,128]{2,1,0:T(8,128)S(1)}, u32[]{:S(2)}, u32[]{:S(2)}) %all-to-all-start.2) | async-done | bytes 1048608 | tf_op jit(solution)/shard_map/all_to_all | solution.py:220
  111.7 0.7 shard_map.115
  (3 shorter events, 0.1 us)
Async XLA Ops:
  2.3 0.7 copy-start
  3.0 0.7 copy-start.2
  3.7 0.8 copy-start.4
  4.5 0.7 copy-start.5
  5.2 0.7 copy-start.6
  5.9 0.7 copy-start.7
  29.6 59.5 %collective-permute-start = (bf16[16,144,128]{2,1,0:T(8,128)(2,1)S(1)}, bf16[16,144,128]{2,1,0:T(8,128)(2,1)S(1)}, u32[]{:S(2)}, u32[]{:S(2)}) collective-permute-start(bf16[16,144,128]{2,1,0:T(8,128)(2,1)S(1)} %slice.13), channel_id=1, source_target_pairs={{0,16},{16,0},{32,48},{48,32},{64,80},{80,64},{96,112},{112,96},{1... | collective-permute-start | bytes 1769480 | tf_op jit(solution)/shard_map/ppermute | solution.py:212
  77.5 11.7 %all-to-all-start.1 = ((bf16[32,16,128]{2,1,0:T(8,128)(2,1)}), bf16[32,16,128]{2,1,0:T(8,128)(2,1)S(1)}, u32[]{:S(2)}, u32[]{:S(2)}) async-start(bf16[32,16,128]{2,1,0:T(8,128)(2,1)} %get-tuple-element.12), calls=%async_computation.1 | async-start | bytes 262144 | tf_op jit(solution)/shard_map/all_to_all | solution.py:211
  91.4 3.8 %copy-start.1 = (bf16[1,72,128]{2,1,0:T(8,128)(2,1)S(1)}, bf16[1,72,128]{2,1,0:T(8,128)(2,1)}, u32[]{:S(2)}) copy-start(bf16[1,72,128]{2,1,0:T(8,128)(2,1)} %param.15) | copy-start | bytes 55300
  91.4 3.8 %copy-start.3 = (bf16[1,72,128]{2,1,0:T(8,128)(2,1)S(1)}, bf16[1,72,128]{2,1,0:T(8,128)(2,1)}, u32[]{:S(2)}) copy-start(bf16[1,72,128]{2,1,0:T(8,128)(2,1)} %param.16) | copy-start | bytes 55300
  91.4 20.3 %all-to-all-start.2 = ((f32[16,128,128]{2,1,0:T(8,128)}), f32[16,128,128]{2,1,0:T(8,128)S(1)}, u32[]{:S(2)}, u32[]{:S(2)}) async-start(f32[16,128,128]{2,1,0:T(8,128)} %shard_map.114), calls=%async_computation.2 | async-start | bytes 2097152 | tf_op jit(solution)/shard_map/all_to_all | solution.py:220

commit v2 on v1

--- a/solution.py
+++ b/solution.py
@@ -39,18 +39,29 @@
     return lax.broadcasted_iota(jnp.int32, shape, dim)
 
 
-def eye(rows, columns, shift):
-    return (iota((rows, columns), 0) + shift == iota((rows, columns), 1)).astype(F32).astype(BF16)
-
-
-def prepare(hidden, gain, bias, query_w, keyvalue_w, out_w, key_page, value_page, send, weights):
-    values = hidden[...].astype(F32)
+def prepare(hidden, gain, bias, query_w, keyvalue_w, out_w, key_page, value_page, send, weights, *scratch):
+    held, done = scratch[:-1], scratch[-1]
+    targets = held + (
+        weights.at[0:HALF],
+        weights.at[HALF:WEIGHT_ROWS],
+        weights.at[WEIGHT_ROWS : WEIGHT_ROWS + HALF],
+    )
+    sources = (hidden, gain, bias, key_page, value_page, query_w, keyvalue_w, out_w)
+    copies = [
+        pltpu.make_async_copy(source, target, done.at[at])
+        for at, (source, target) in enumerate(zip(sources, targets))
+    ]
+    for copy in copies:
+        copy.start()
+    for copy in copies:
+        copy.wait()
+    values = held[0][...].astype(F32)
     average = jnp.mean(values, axis=-1, keepdims=True)
     centred = values - average
     spread = jnp.mean(centred * centred, axis=-1, keepdims=True)
-    normed = (centred * lax.rsqrt(spread + 1e-05) * gain[...] + bias[...]).astype(BF16)
-    key_rows = key_page[...]
-    value_rows = value_page[...]
+    normed = (centred * lax.rsqrt(spread + 1e-05) * held[1][...] + held[2][...]).astype(BF16)
+    key_rows = held[3][...]
+    value_rows = held[4][...]
     for chip in range(CHIPS):
         send[chip, 0:PAGE, :] = key_rows
         send[chip, PAGE:KV_ROWS, :] = value_rows
@@ -58,25 +69,16 @@
             send[chip, KV_ROWS + OWN * chunk : KV_ROWS + OWN * (chunk + 1), :] = normed[
                 :, LANES * chunk : LANES * (chunk + 1)
             ]
-    packed = dot(query_w[0:HALF, :], eye(HALF, LANES, 0)) + dot(query_w[HALF:LANES, :], eye(HALF, LANES, HALF))
-    weights[0:HALF, :] = packed.astype(BF16)
-    weights[HALF:WEIGHT_ROWS, :] = dot_nt(eye(OWN, OWN, 0), keyvalue_w[...]).astype(BF16)
-    weights[WEIGHT_ROWS : WEIGHT_ROWS + HALF, :] = out_w[...]
 
 
 def project(tokens, weights, queries, keyvalue):
-    low = iota((HALF, LANES), 1) < HALF
     query_sum = jnp.zeros((LANES, LANES), F32)
     keyvalue_sum = jnp.zeros((CORES * OWN, LANES), F32)
     for chunk in range(CHUNKS):
         first = KV_ROWS + OWN * chunk
         rows = tokens[:, first : first + OWN, :].astype(F32).reshape(LANES, LANES).astype(BF16)
-        left = weights[0, chunk, 0:HALF, :].astype(F32)
-        right = weights[1, chunk, 0:HALF, :].astype(F32)
-        upper = jnp.where(low, left, pltpu.roll(right, HALF, 1))
-        lower = jnp.where(low, pltpu.roll(left, HALF, 1), right)
-        square = jnp.concatenate([upper, lower], axis=0).astype(BF16)
-        query_sum = query_sum + dot(rows, square)
+        square = jnp.concatenate([weights[0, chunk, 0:HALF, :], weights[1, chunk, 0:HALF, :]], axis=0)
+        query_sum = query_sum + dot_nt(rows, square)
         narrow = jnp.concatenate(
             [
                 weights[0, chunk, HALF:WEIGHT_ROWS, :].astype(F32),
@@ -134,13 +136,13 @@
     for chunk in range(CHUNKS):
         square = jnp.concatenate([out_w[0, chunk], out_w[1, chunk]], axis=0)
         part = dot(attended, square)
-        result[:, OWN * chunk : OWN * (chunk + 1), :] = part.reshape(CHIPS, OWN, LANES)
+        result[:, OWN * chunk : OWN * (chunk + 1), :] = part.reshape(CHIPS, OWN, LANES).astype(BF16)
 
 
 def add_heads(parts, result):
-    total = parts[0]
+    total = parts[0].astype(F32)
     for chip in range(1, CHIPS):
-        total = total + parts[chip]
+        total = total + parts[chip].astype(F32)
     for chunk in range(CHUNKS):
         result[:, LANES * chunk : LANES * (chunk + 1)] = total[OWN * chunk : OWN * (chunk + 1), :].astype(BF16)
 
@@ -160,15 +162,21 @@
     new_value[...] = jnp.where(inside, value_rows, value_page[...].astype(F32)).astype(BF16)
 
 
-def call(kernel, shapes, arguments, scalars=0):
+def call(kernel, shapes, arguments, scalars=0, held=None):
+    space = pltpu.VMEM if held is None else pltpu.HBM
     specs = [
-        pl.BlockSpec(memory_space=pltpu.SMEM if at < scalars else pltpu.VMEM) for at in range(len(arguments))
+        pl.BlockSpec(memory_space=pltpu.SMEM if at < scalars else space) for at in range(len(arguments))
     ]
+    scratch = []
+    if held is not None:
+        scratch = [pltpu.VMEM(shape, dtype) for shape, dtype in held]
+        scratch.append(pltpu.SemaphoreType.DMA((len(arguments),)))
     return pl.pallas_call(
         kernel,
         out_shape=[jax.ShapeDtypeStruct(shape, dtype) for shape, dtype in shapes],
         in_specs=specs,
         out_specs=[pl.BlockSpec(memory_space=pltpu.VMEM)] * len(shapes),
+        scratch_shapes=scratch,
         compiler_params=pltpu.CompilerParams(vmem_limit_bytes=48 * 1024 * 1024),
     )(*arguments)
 
@@ -193,15 +201,23 @@
             hidden_states[0],
             norm_gain.reshape(1, FEATURES),
             norm_bias.reshape(1, FEATURES),
-            query_weight,
-            keyvalue_weight,
+            query_weight.T,
+            keyvalue_weight.T,
             out_weight,
             key_cache[0],
             value_cache[0],
         ),
+        held=[
+            ((OWN, FEATURES), BF16),
+            ((1, FEATURES), F32),
+            ((1, FEATURES), F32),
+            ((PAGE, LANES), BF16),
+            ((PAGE, LANES), BF16),
+        ],
     )
     own = lax.all_to_all(send, "gx", 0, 0, tiled=True, axis_index_groups=SAME_CORE)
     planes = lax.all_gather(weights, "gy", axis=0, tiled=False)
+    own, planes = lax.optimization_barrier((own, planes))
     inner = lax.all_gather(planes[:, :WEIGHT_ROWS], "gx", axis=0, tiled=False, axis_index_groups=ONE_CHIP)
     queries, rows = call(
         project,
@@ -213,7 +229,7 @@
     outer = lax.all_gather(planes[:, WEIGHT_ROWS:], "gx", axis=0, tiled=False, axis_index_groups=ONE_CHIP)
     (parts,) = call(
         attend,
-        [((CHIPS, LANES, LANES), F32)],
+        [((CHIPS, LANES, LANES), BF16)],
         (cache_length, core, queries, own, peer, keyvalue, outer),
         scalars=2,
     )

time: 113 us -> 94 us (0.83)
  blocking collectives: 65.5 us -> 36.6 us
  starting transfers between devices: 13 us -> 28 us
  waiting for transfers between devices: 21.2 us -> 14.9 us
  Pallas kernels: 5.25 us -> 6.43 us
    all_to_all x1 -> x0, blocking collectives: 22.8 us -> none  [body(): lax.all_to_all(send, 'gx', 0, 0, tiled=True, axis_index_groups=SAME_CORE)]
    all_to_all x0 -> x1, starting transfers between devices: none -> 7.6 us  [body(): lax.all_to_all(send, 'gx', 0, 0, tiled=True, axis_index_groups=SAME_CORE)]
    all_gather x1, blocking collectives: 9.03 us -> 2.23 us  [body(): lax.all_gather(planes[:, :WEIGHT_ROWS], 'gx', axis=0, tiled=False, axis_i...]
    all_to_all x1, waiting for transfers between devices: 15.6 us -> 9.39 us  [body(): lax.all_to_all(parts, 'gx', 0, 0, tiled=True, axis_index_groups=SAME_CORE)]
    ppermute x1, starting transfers between devices: 5.31 us -> 9.18 us  [body(): peer = lax.ppermute(own[:, :KV_ROWS], 'gx', SWAP)]
    all_to_all x1, starting transfers between devices: 3.88 us -> 7.66 us  [body(): keyvalue = lax.all_to_all(rows, 'gx', 0, 0, tiled=True)]
    pallas_call x5, Pallas kernels: 5.25 us -> 6.43 us  [call(): pl.pallas_call(kernel, out_shape=[jax.ShapeDtypeStruct(shape, dtype) for...]
    unnamed x18 -> x20, local copies, waits for them, and re-layouts: 5.95 us -> 5.71 us
  transfers between devices with their start and end apart: 3 -> 4, of which waited for: 2 -> 2; matrix products, arithmetic and copies ran while one was open for 0% -> 0% of each run, Pallas kernels for 2% -> 2%
where the time goes in v2:
time: 94 us; the launch traced here: 93.2 us
  blocking collectives  36.6 us (39%)
  starting transfers between devices  28 us (30%)
  waiting for transfers between devices  14.9 us (16%)
  Pallas kernels  6.43 us (7%)
  local copies, waits for them, and re-layouts  5.79 us (6%)
  between operations  1.38 us (1%)
    all_gather x1, blocking collectives, body(): planes = lax.all_gather(weights, 'gy', axis=0, tiled=False)  32.2 us
    all_to_all x1, waiting for transfers between devices, body(): lax.all_to_all(parts, 'gx', 0, 0, tiled=True, axis_index_groups=SAME_CORE)  9.39 us
    ppermute x1, starting transfers between devices, body(): peer = lax.ppermute(own[:, :KV_ROWS], 'gx', SWAP)  9.18 us
    all_to_all x1, starting transfers between devices, body(): keyvalue = lax.all_to_all(rows, 'gx', 0, 0, tiled=True)  7.66 us
    all_to_all x1, starting transfers between devices, body(): lax.all_to_all(send, 'gx', 0, 0, tiled=True, axis_index_groups=SAME_CORE)  7.6 us
    pallas_call x5, Pallas kernels, call(): pl.pallas_call(kernel, out_shape=[jax.ShapeDtypeStruct(shape, dtype) for...  6.43 us
    unnamed x20, local copies, waits for them, and re-layouts  5.71 us
    all_to_all x1, waiting for transfers between devices, body(): keyvalue = lax.all_to_all(rows, 'gx', 0, 0, tiled=True)  5.52 us
  transfers between devices with their start and end apart: 4, of which 2 were waited for; matrix products, arithmetic and copies ran while one was open for 0% of the time, Pallas kernels for 2%

profile of v2, /device:TPU:1, one launch (start us, length us, event | category | flops | bytes accessed | tf_op | source)
XLA Modules:
  0.0 93.2 jit_solution(15820672922949094574)
XLA Ops:
  0.6 0.0 copy-start
  0.6 0.7 copy-done
  1.4 0.0 copy-start.2
  1.4 0.7 copy-done.2
  2.1 0.0 copy-start.4
  2.1 0.8 copy-done.4
  2.8 0.0 copy-start.5
  2.8 0.7 copy-done.5
  3.6 0.0 copy-start.6
  3.6 0.7 copy-done.6
  4.3 0.0 copy-start.7
  4.3 0.7 copy-done.7
  5.0 0.0 copy-start.8
  5.0 0.7 copy-done.8
  5.7 0.0 copy-start.9
  5.7 0.7 copy-done.9
  6.4 1.4 %shard_map.112 = (bf16[16,272,128]{2,1,0:T(8,128)(2,1)}, bf16[136,128]{1,0:T(8,128)(2,1)S(1)}) custom-call(bf16[8,2048]{1,0:T(8,128)(2,1)S(1)} %bitcast.20, f32[1,2048]{1,0:T(1,128)S(1)} %bitcast.22, f32[1,2048]{1,0:T(1,128)S(1)} %bitcast.23, bf16[64,128]{1,0:T(8,128)(2,1)S(1)} %bitcast.21, bf16[8,128]{1,0:T(8,128)(2,1)S(1)} %bitcast.24, ...), custom_call_target="tpu_custom_call" | custom-call | tf_op jit(solution)/shard_map/pallas_call | solution.py:174
  7.8 7.6 %all-to-all-start = ((bf16[16,272,128]{2,1,0:T(8,128)(2,1)}), bf16[16,272,128]{2,1,0:T(8,128)(2,1)S(1)}, u32[]{:S(2)}, u32[]{:S(2)}) async-start(bf16[16,272,128]{2,1,0:T(8,128)(2,1)} %get-tuple-element.11), calls=%async_computation | async-start | bytes 2228224 | tf_op jit(solution)/shard_map/all_to_all | solution.py:218
  15.4 32.2 %all-gather = bf16[2176,128]{1,0:T(8,128)(2,1)S(1)} all-gather(bf16[136,128]{1,0:T(8,128)(2,1)S(1)} %get-tuple-element.12), channel_id=2, replica_groups=mesh['gx'=32,'gy'=16] {'gy'}, dimensions={0}, use_global_device_ids=true | all-gather | bytes 591872 | tf_op jit(solution)/shard_map/all_gather | solution.py:219
  47.6 0.0 all-to-all-done.tokens.own
  47.7 9.2 %collective-permute-start = (bf16[16,144,128]{2,1,0:T(8,128)(2,1)S(1)}, bf16[16,144,128]{2,1,0:T(8,128)(2,1)S(1)}, u32[]{:S(2)}, u32[]{:S(2)}) collective-permute-start(bf16[16,144,128]{2,1,0:T(8,128)(2,1)S(1)} %slice.10), channel_id=1, source_target_pairs={{0,16},{16,0},{32,48},{48,32},{64,80},{80,64},{96,112},{112,96},{1... | collective-permute-start | bytes 1769480 | tf_op jit(solution)/shard_map/ppermute | solution.py:228
  57.6 2.2 %all-gather.1 = bf16[32,72,128]{2,1,0:T(8,128)(2,1)S(1)} all-gather(bf16[16,72,128]{2,1,0:T(8,128)(2,1)S(1)} %slice.9), channel_id=3, replica_groups={{0,16},{32,48},{64,80},{96,112},{128,144},{160,176},{192,208},{224,240}..., dimensions={0}, use_global_device_ids=true | all-gather | bytes 884736 | tf_op jit(solution)/shard_map/all_gather | solution.py:221
  59.8 1.4 %shard_map.113 = (bf16[128,128]{1,0:T(8,128)(2,1)S(1)}, bf16[32,16,128]{2,1,0:T(8,128)(2,1)}) custom-call(bf16[16,272,128]{2,1,0:T(8,128)(2,1)S(1)} %all-to-all-done.tokens.own, bf16[2,16,72,128]{3,2,1,0:T(8,128)(2,1)S(1)} %bitcast.14), custom_call_target="tpu_custom_call" | custom-call | tf_op jit(solution)/shard_map/pallas_call | solution.py:174
  61.2 7.7 %all-to-all-start.1 = ((bf16[32,16,128]{2,1,0:T(8,128)(2,1)}), bf16[32,16,128]{2,1,0:T(8,128)(2,1)S(1)}, u32[]{:S(2)}, u32[]{:S(2)}) async-start(bf16[32,16,128]{2,1,0:T(8,128)(2,1)} %get-tuple-element.16), calls=%async_computation.1 | async-start | bytes 262144 | tf_op jit(solution)/shard_map/all_to_all | solution.py:227
  68.9 2.2 %all-gather.2 = bf16[32,64,128]{2,1,0:T(8,128)(2,1)S(1)} all-gather(bf16[16,64,128]{2,1,0:T(8,128)(2,1)S(1)} %slice.11), channel_id=4, replica_groups={{0,16},{32,48},{64,80},{96,112},{128,144},{160,176},{192,208},{224,240}..., dimensions={0}, use_global_device_ids=true | all-gather | bytes 786432 | tf_op jit(solution)/shard_map/all_gather | solution.py:229
  71.1 5.5 %all-to-all-done.1.keyvalue = bf16[32,16,128]{2,1,0:T(8,128)(2,1)S(1)} async-done(((bf16[32,16,128]{2,1,0:T(8,128)(2,1)}), bf16[32,16,128]{2,1,0:T(8,128)(2,1)S(1)}, u32[]{:S(2)}, u32[]{:S(2)}) %all-to-all-start.1) | async-done | bytes 131104 | tf_op jit(solution)/shard_map/all_to_all | solution.py:227
  76.6 0.0 collective-permute-done.peer
  76.6 0.0 copy-start.1
  76.6 0.0 copy-start.3
  76.6 2.1 %shard_map.114 = bf16[16,128,128]{2,1,0:T(8,128)(2,1)} custom-call(s32[1]{0:T(128)S(6)} %copy.12.length_ref, s32[1]{0:T(128)S(6)} %and.4.core_ref, bf16[128,128]{1,0:T(8,128)(2,1)S(1)} %get-tuple-element.15.queries, bf16[16,272,128]{2,1,0:T(8,128)(2,1)S(1)} %all-to-all-done.tokens.own, bf16[16,144,128]{2,1,0:T(8,128)(2,1)S(1)} %collective-permute-done.peer, ...), custom_call_target="tpu_custom_call" | custom-call | tf_op jit(solution)/shard_map/pallas_call | solution.py:174
  78.7 3.6 %all-to-all-start.2 = ((bf16[16,128,128]{2,1,0:T(8,128)(2,1)}), bf16[16,128,128]{2,1,0:T(8,128)(2,1)S(1)}, u32[]{:S(2)}, u32[]{:S(2)}) async-start(bf16[16,128,128]{2,1,0:T(8,128)(2,1)} %shard_map.114), calls=%async_computation.2 | async-start | bytes 1048576 | tf_op jit(solution)/shard_map/all_to_all | solution.py:236
  82.2 0.0 copy-done.1
  82.2 0.0 copy-done.3
  82.3 0.8 shard_map.116
  83.1 9.4 %all-to-all-done.2.parts = bf16[16,128,128]{2,1,0:T(8,128)(2,1)S(1)} async-done(((bf16[16,128,128]{2,1,0:T(8,128)(2,1)}), bf16[16,128,128]{2,1,0:T(8,128)(2,1)S(1)}, u32[]{:S(2)}, u32[]{:S(2)}) %all-to-all-start.2) | async-done | bytes 524320 | tf_op jit(solution)/shard_map/all_to_all | solution.py:236
  92.5 0.7 shard_map.115
  (3 shorter events, 0.1 us)
Async XLA Ops:
  0.6 0.7 copy-start
  1.4 0.7 copy-start.2
  2.1 0.8 copy-start.4
  2.8 0.7 copy-start.5
  3.6 0.7 copy-start.6
  4.3 0.7 copy-start.7
  5.0 0.7 copy-start.8
  5.7 0.7 copy-start.9
  7.8 39.8 %all-to-all-start = ((bf16[16,272,128]{2,1,0:T(8,128)(2,1)}), bf16[16,272,128]{2,1,0:T(8,128)(2,1)S(1)}, u32[]{:S(2)}, u32[]{:S(2)}) async-start(bf16[16,272,128]{2,1,0:T(8,128)(2,1)} %get-tuple-element.11), calls=%async_computation | async-start | bytes 2228224 | tf_op jit(solution)/shard_map/all_to_all | solution.py:218
  47.7 28.9 %collective-permute-start = (bf16[16,144,128]{2,1,0:T(8,128)(2,1)S(1)}, bf16[16,144,128]{2,1,0:T(8,128)(2,1)S(1)}, u32[]{:S(2)}, u32[]{:S(2)}) collective-permute-start(bf16[16,144,128]{2,1,0:T(8,128)(2,1)S(1)} %slice.10), channel_id=1, source_target_pairs={{0,16},{16,0},{32,48},{48,32},{64,80},{80,64},{96,112},{112,96},{1... | collective-permute-start | bytes 1769480 | tf_op jit(solution)/shard_map/ppermute | solution.py:228
  61.2 15.4 %all-to-all-start.1 = ((bf16[32,16,128]{2,1,0:T(8,128)(2,1)}), bf16[32,16,128]{2,1,0:T(8,128)(2,1)S(1)}, u32[]{:S(2)}, u32[]{:S(2)}) async-start(bf16[32,16,128]{2,1,0:T(8,128)(2,1)} %get-tuple-element.16), calls=%async_computation.1 | async-start | bytes 262144 | tf_op jit(solution)/shard_map/all_to_all | solution.py:227
  76.6 5.7 %copy-start.1 = (bf16[1,72,128]{2,1,0:T(8,128)(2,1)S(1)}, bf16[1,72,128]{2,1,0:T(8,128)(2,1)}, u32[]{:S(2)}) copy-start(bf16[1,72,128]{2,1,0:T(8,128)(2,1)} %param.15) | copy-start | bytes 55300
  76.6 5.7 %copy-start.3 = (bf16[1,72,128]{2,1,0:T(8,128)(2,1)S(1)}, bf16[1,72,128]{2,1,0:T(8,128)(2,1)}, u32[]{:S(2)}) copy-start(bf16[1,72,128]{2,1,0:T(8,128)(2,1)} %param.16) | copy-start | bytes 55300
  78.7 13.8 %all-to-all-start.2 = ((bf16[16,128,128]{2,1,0:T(8,128)(2,1)}), bf16[16,128,128]{2,1,0:T(8,128)(2,1)S(1)}, u32[]{:S(2)}, u32[]{:S(2)}) async-start(bf16[16,128,128]{2,1,0:T(8,128)(2,1)} %shard_map.114), calls=%async_computation.2 | async-start | bytes 1048576 | tf_op jit(solution)/shard_map/all_to_all | solution.py:236

commit v3 on v2

--- a/solution.py
+++ b/solution.py
@@ -71,28 +71,38 @@
             ]
 
 
-def project(tokens, weights, queries, keyvalue):
-    query_sum = jnp.zeros((LANES, LANES), F32)
-    keyvalue_sum = jnp.zeros((CORES * OWN, LANES), F32)
+def gathered_tokens(tokens):
+    pieces = []
     for chunk in range(CHUNKS):
         first = KV_ROWS + OWN * chunk
-        rows = tokens[:, first : first + OWN, :].astype(F32).reshape(LANES, LANES).astype(BF16)
-        square = jnp.concatenate([weights[0, chunk, 0:HALF, :], weights[1, chunk, 0:HALF, :]], axis=0)
-        query_sum = query_sum + dot_nt(rows, square)
-        narrow = jnp.concatenate(
-            [
-                weights[0, chunk, HALF:WEIGHT_ROWS, :].astype(F32),
-                weights[1, chunk, HALF:WEIGHT_ROWS, :].astype(F32),
-            ],
-            axis=0,
-        ).astype(BF16)
-        keyvalue_sum = keyvalue_sum + dot_nt(narrow, rows)
-    queries[...] = query_sum.astype(BF16)
-    rounded = keyvalue_sum.astype(BF16)
+        pieces.append(tokens[:, first : first + OWN, :].astype(F32).reshape(LANES, LANES).astype(BF16))
+    return jnp.concatenate(pieces, axis=1)
+
+
+def project_keyvalue(tokens, weights, keyvalue):
+    narrow = jnp.concatenate(
+        [
+            jnp.concatenate([weights[core, chunk, HALF:WEIGHT_ROWS, :].astype(F32) for core in range(CORES)], axis=0)
+            for chunk in range(CHUNKS)
+        ],
+        axis=1,
+    ).astype(BF16)
+    rounded = dot_nt(narrow, gathered_tokens(tokens)).astype(BF16)
     for place in range(CHIPS * CORES):
         keyvalue[place] = rounded
 
 
+def project_queries(tokens, weights, queries):
+    square = jnp.concatenate(
+        [
+            jnp.concatenate([weights[core, chunk, 0:HALF, :] for core in range(CORES)], axis=0)
+            for chunk in range(CHUNKS)
+        ],
+        axis=1,
+    )
+    queries[...] = dot_nt(gathered_tokens(tokens), square).astype(BF16)
+
+
 def new_columns(keyvalue, core, first):
     return jnp.concatenate([keyvalue[CORES * chip + core] for chip in range(first, first + CHIPS // 2)], axis=0)
 
@@ -101,7 +111,7 @@
     return ((index >> 3) << 4) + OWN * core + (index & 7)
 
 
-def attend(length_ref, core_ref, queries, own, peer, keyvalue, out_w, result):
+def attend_cached(length_ref, core_ref, queries, own, peer, largest_out, total_out, summed_out):
     length = length_ref[0]
     core = core_ref[0]
     scale = float(LANES) ** (-0.5)
@@ -116,25 +126,44 @@
         value_sets.append(source[:, PAGE:KV_ROWS, :].astype(F32).reshape(places, LANES).astype(BF16))
         scores = dot_nt(query_rows, keys) * scale
         scored.append(jnp.where(start + PAGE * side < length, scores, NEGATIVE))
+    largest = jnp.maximum(
+        jnp.max(scored[0], axis=1, keepdims=True), jnp.max(scored[1], axis=1, keepdims=True)
+    )
+    total = jnp.zeros((LANES, 1), F32)
+    summed = jnp.zeros((LANES, LANES), F32)
+    for scores, values in zip(scored, value_sets):
+        terms = jnp.where(scores > 0.5 * NEGATIVE, jnp.exp(scores - largest), 0.0)
+        total = total + jnp.sum(terms, axis=1, keepdims=True)
+        summed = summed + dot(terms.astype(BF16), values)
+    largest_out[...] = jnp.broadcast_to(largest, (LANES, LANES))
+    total_out[...] = jnp.broadcast_to(total, (LANES, LANES))
+    summed_out[...] = summed
+
+
+def attend_new(core_ref, queries, old_largest, old_total, old_summed, keyvalue, planes, peer, result):
+    core = core_ref[0]
+    scale = float(LANES) ** (-0.5)
+    query_rows = queries[...]
     own_token = token_of(iota((LANES, LANES), 0), core)
+    scored = []
     for side in range(CORES):
         scores = dot(query_rows, new_columns(keyvalue, side, 0)) * scale
         scored.append(jnp.where(token_of(iota((LANES, LANES), 1), side) <= own_token, scores, NEGATIVE))
-    largest = jnp.max(scored[0], axis=1, keepdims=True)
-    for scores in scored[1:]:
-        largest = jnp.maximum(largest, jnp.max(scores, axis=1, keepdims=True))
-    total = jnp.zeros((LANES, 1), F32)
-    summed = jnp.zeros((LANES, LANES), F32)
-    for which, scores in enumerate(scored):
-        terms = jnp.exp(scores - largest)
-        total = total + jnp.sum(terms, axis=1, keepdims=True)
-        if which < 2:
-            summed = summed + dot(terms.astype(BF16), value_sets[which])
-        else:
-            summed = summed + dot_nt(terms.astype(BF16), new_columns(keyvalue, which - 2, CHIPS // 2))
+    largest = jnp.max(jnp.maximum(scored[0], scored[1]), axis=1, keepdims=True)
+    largest = jnp.maximum(old_largest[...], jnp.broadcast_to(largest, (LANES, LANES)))
+    factor = jnp.exp(old_largest[...] - largest)
+    terms = [jnp.exp(scores - largest) for scores in scored]
+    total = old_total[...] * factor + jnp.sum(terms[0] + terms[1], axis=1, keepdims=True)
+    summed = old_summed[...] * factor
+    for side in range(CORES):
+        summed = summed + dot_nt(terms[side].astype(BF16), new_columns(keyvalue, side, CHIPS // 2))
+    turned = pltpu.roll(summed, HALF, 1)
+    summed = jnp.where(core == 0, summed, turned)
     attended = (summed / total).astype(BF16)
     for chunk in range(CHUNKS):
-        square = jnp.concatenate([out_w[0, chunk], out_w[1, chunk]], axis=0)
+        square = jnp.concatenate(
+            [planes[chunk, WEIGHT_ROWS : WEIGHT_ROWS + HALF, :], peer[chunk, KV_ROWS : KV_ROWS + HALF, :]], axis=0
+        )
         part = dot(attended, square)
         result[:, OWN * chunk : OWN * (chunk + 1), :] = part.reshape(CHIPS, OWN, LANES).astype(BF16)
 
@@ -171,6 +200,8 @@
     if held is not None:
         scratch = [pltpu.VMEM(shape, dtype) for shape, dtype in held]
         scratch.append(pltpu.SemaphoreType.DMA((len(arguments),)))
+    if held is not None:
+        arguments = [pltpu.with_memory_space_constraint(argument, pltpu.HBM) for argument in arguments]
     return pl.pallas_call(
         kernel,
         out_shape=[jax.ShapeDtypeStruct(shape, dtype) for shape, dtype in shapes],
@@ -219,19 +250,26 @@
     planes = lax.all_gather(weights, "gy", axis=0, tiled=False)
     own, planes = lax.optimization_barrier((own, planes))
     inner = lax.all_gather(planes[:, :WEIGHT_ROWS], "gx", axis=0, tiled=False, axis_index_groups=ONE_CHIP)
-    queries, rows = call(
-        project,
-        [((LANES, LANES), BF16), ((CHIPS * CORES, CORES * OWN, LANES), BF16)],
+    (rows,) = call(
+        project_keyvalue,
+        [((CHIPS * CORES, CORES * OWN, LANES), BF16)],
         (own, inner),
     )
     keyvalue = lax.all_to_all(rows, "gx", 0, 0, tiled=True)
-    peer = lax.ppermute(own[:, :KV_ROWS], "gx", SWAP)
-    outer = lax.all_gather(planes[:, WEIGHT_ROWS:], "gx", axis=0, tiled=False, axis_index_groups=ONE_CHIP)
+    swapped = jnp.concatenate([own[:, :KV_ROWS], planes[:, WEIGHT_ROWS:]], axis=1)
+    peer = lax.ppermute(swapped, "gx", SWAP)
+    (queries,) = call(project_queries, [((LANES, LANES), BF16)], (own, inner))
+    largest, total, summed = call(
+        attend_cached,
+        [((LANES, LANES), F32)] * 3,
+        (cache_length, core, queries, own, peer),
+        scalars=2,
+    )
     (parts,) = call(
-        attend,
+        attend_new,
         [((CHIPS, LANES, LANES), BF16)],
-        (cache_length, core, queries, own, peer, keyvalue, outer),
-        scalars=2,
+        (core, queries, largest, total, summed, keyvalue, planes, peer),
+        scalars=1,
     )
     collected = lax.all_to_all(parts, "gx", 0, 0, tiled=True, axis_index_groups=SAME_CORE)
     new_key, new_value = call(

time: 94 us -> 88.3 us (0.939)
  local copies, waits for them, and re-layouts: 5.79 us -> 0.09 us
  blocking collectives: 36.6 us -> 34.6 us
  other arithmetic: 0 us -> 0.98 us
    unnamed x20 -> x4, local copies, waits for them, and re-layouts: 5.71 us -> 0.01 us
    all_gather x1 -> x0, blocking collectives: 2.18 us -> none  [body(): lax.all_gather(planes[:, WEIGHT_ROWS:], 'gx', axis=0, tiled=False, axis_i...]
    concatenate x0 -> x1, other arithmetic: none -> 0.98 us  [body(): jnp.concatenate([own[:, :KV_ROWS], planes[:, WEIGHT_ROWS:]], axis=1)]
    pallas_call x5 -> x7, Pallas kernels: 6.43 us -> 7.36 us  [call(): pl.pallas_call(kernel, out_shape=[jax.ShapeDtypeStruct(shape, dtype) for...]
  transfers between devices with their start and end apart: 4 -> 4, of which waited for: 2 -> 2; matrix products, arithmetic and copies ran while one was open for 0% -> 0% of each run, Pallas kernels for 2% -> 3%
where the time goes in v3:
time: 88.3 us; the launch traced here: 87.8 us
  blocking collectives  34.6 us (39%)
  starting transfers between devices  28.2 us (32%)
  waiting for transfers between devices  15.2 us (17%)
  Pallas kernels  7.36 us (8%)
  between operations  1.39 us (2%)
  other arithmetic  0.98 us (1%)
    all_gather x1, blocking collectives, body(): planes = lax.all_gather(weights, 'gy', axis=0, tiled=False)  32.2 us
    all_to_all x1, waiting for transfers between devices, body(): lax.all_to_all(parts, 'gx', 0, 0, tiled=True, axis_index_groups=SAME_CORE)  9.4 us
    ppermute x1, starting transfers between devices, body(): peer = lax.ppermute(swapped, 'gx', SWAP)  9.17 us
    all_to_all x1, starting transfers between devices, body(): keyvalue = lax.all_to_all(rows, 'gx', 0, 0, tiled=True)  7.89 us
    all_to_all x1, starting transfers between devices, body(): lax.all_to_all(send, 'gx', 0, 0, tiled=True, axis_index_groups=SAME_CORE)  7.6 us
    pallas_call x7, Pallas kernels, call(): pl.pallas_call(kernel, out_shape=[jax.ShapeDtypeStruct(shape, dtype) for...  7.36 us
    all_to_all x1, waiting for transfers between devices, body(): keyvalue = lax.all_to_all(rows, 'gx', 0, 0, tiled=True)  5.79 us
    all_to_all x1, starting transfers between devices, body(): lax.all_to_all(parts, 'gx', 0, 0, tiled=True, axis_index_groups=SAME_CORE)  3.57 us
  transfers between devices with their start and end apart: 4, of which 2 were waited for; matrix products, arithmetic and copies ran while one was open for 0% of the time, Pallas kernels for 3%

profile of v3, /device:TPU:1, one launch (start us, length us, event | category | flops | bytes accessed | tf_op | source)
XLA Modules:
  0.0 87.8 jit_solution(786409120961153082)
XLA Ops:
  0.6 2.1 %shard_map.112 = (bf16[16,272,128]{2,1,0:T(8,128)(2,1)}, bf16[136,128]{1,0:T(8,128)(2,1)S(1)}) custom-call(bf16[8,2048]{1,0:T(8,128)(2,1)} %bitcast.23, f32[1,2048]{1,0:T(1,128)} %bitcast.25, f32[1,2048]{1,0:T(1,128)} %bitcast.26, bf16[64,128]{1,0:T(8,128)(2,1)} %bitcast.24, bf16[8,128]{1,0:T(8,128)(2,1)} %bitcast.27, bf16[64,128]{1,0:T(8,128)(2,1)} %out_w.1, ...), custom_call_target="tpu_custom_call" | custom-call | tf_op jit(solution)/shard_map/pallas_call | solution.py:205
  2.8 7.6 %all-to-all-start = ((bf16[16,272,128]{2,1,0:T(8,128)(2,1)}), bf16[16,272,128]{2,1,0:T(8,128)(2,1)S(1)}, u32[]{:S(2)}, u32[]{:S(2)}) async-start(bf16[16,272,128]{2,1,0:T(8,128)(2,1)} %get-tuple-element.12), calls=%async_computation | async-start | bytes 2228224 | tf_op jit(solution)/shard_map/all_to_all | solution.py:249
  10.4 32.2 %all-gather = bf16[2176,128]{1,0:T(8,128)(2,1)S(1)} all-gather(bf16[136,128]{1,0:T(8,128)(2,1)S(1)} %get-tuple-element.13), channel_id=2, replica_groups=mesh['gx'=32,'gy'=16] {'gy'}, dimensions={0}, use_global_device_ids=true | all-gather | bytes 591872 | tf_op jit(solution)/shard_map/all_gather | solution.py:250
  42.6 0.0 all-to-all-done.tokens.own
  42.7 1.0 %pad_maximum_fusion = bf16[16,208,128]{2,1,0:T(8,128)(2,1)} fusion(bf16[16,64,128]{2,1,0:T(8,128)(2,1)S(1)} %slice.11, bf16[16,144,128]{2,1,0:T(8,128)(2,1)S(1)} %slice.10), kind=kLoop, calls=%fused_computation | loop fusion | flops 1703936 | bytes 1703936 | tf_op jit(solution)/shard_map/concatenate | solution.py:259
  43.7 9.2 %collective-permute-start = (bf16[16,208,128]{2,1,0:T(8,128)(2,1)}, bf16[16,208,128]{2,1,0:T(8,128)(2,1)S(1)}, u32[]{:S(2)}, u32[]{:S(2)}) collective-permute-start(bf16[16,208,128]{2,1,0:T(8,128)(2,1)} %pad_maximum_fusion), channel_id=1, source_target_pairs={{0,16},{16,0},{32,48},{48,32},{64,80},{80,64},{96,112},{112,96},{1... | collective-permute-start | bytes 2555912 | tf_op jit(solution)/shard_map/ppermute | solution.py:260
  52.9 2.4 %all-gather.1 = bf16[32,72,128]{2,1,0:T(8,128)(2,1)S(1)} all-gather(bf16[16,72,128]{2,1,0:T(8,128)(2,1)S(1)} %slice.9), channel_id=3, replica_groups={{0,16},{32,48},{64,80},{96,112},{128,144},{160,176},{192,208},{224,240}..., dimensions={0}, use_global_device_ids=true | all-gather | bytes 884736 | tf_op jit(solution)/shard_map/all_gather | solution.py:252
  55.2 0.9 %shard_map.115 = bf16[32,16,128]{2,1,0:T(8,128)(2,1)} custom-call(bf16[16,272,128]{2,1,0:T(8,128)(2,1)S(1)} %all-to-all-done.tokens.own, bf16[2,16,72,128]{3,2,1,0:T(8,128)(2,1)S(1)} %bitcast.13), custom_call_target="tpu_custom_call" | custom-call | tf_op jit(solution)/shard_map/pallas_call | solution.py:205
  56.2 7.9 %all-to-all-start.1 = ((bf16[32,16,128]{2,1,0:T(8,128)(2,1)}), bf16[32,16,128]{2,1,0:T(8,128)(2,1)S(1)}, u32[]{:S(2)}, u32[]{:S(2)}) async-start(bf16[32,16,128]{2,1,0:T(8,128)(2,1)} %shard_map.115), calls=%async_computation.1 | async-start | bytes 262144 | tf_op jit(solution)/shard_map/all_to_all | solution.py:258
  64.7 0.3 shard_map.113.queries
  65.0 0.0 collective-permute-done.peer
  65.0 0.9 %shard_map.114 = (f32[128,128]{1,0:T(8,128)S(1)}, f32[128,128]{1,0:T(8,128)S(1)}, f32[128,128]{1,0:T(8,128)S(1)}) custom-call(s32[1]{0:T(128)S(6)} %copy.12.length_ref, s32[1]{0:T(128)S(6)} %and.4.core_ref, bf16[128,128]{1,0:T(8,128)(2,1)S(1)} %shard_map.113.queries, bf16[16,272,128]{2,1,0:T(8,128)(2,1)S(1)} %all-to-all-done.tokens.own, ...), custom_call_target="tpu_custom_call" | custom-call | tf_op jit(solution)/shard_map/pallas_call | solution.py:205
  66.0 5.8 %all-to-all-done.1.keyvalue = bf16[32,16,128]{2,1,0:T(8,128)(2,1)S(1)} async-done(((bf16[32,16,128]{2,1,0:T(8,128)(2,1)}), bf16[32,16,128]{2,1,0:T(8,128)(2,1)S(1)}, u32[]{:S(2)}, u32[]{:S(2)}) %all-to-all-start.1) | async-done | bytes 131104 | tf_op jit(solution)/shard_map/all_to_all | solution.py:258
  71.8 0.0 copy-start
  71.8 0.0 copy-start.1
  71.8 1.6 %shard_map.116 = bf16[16,128,128]{2,1,0:T(8,128)(2,1)} custom-call(s32[1]{0:T(128)S(6)} %and.4.core_ref, bf16[128,128]{1,0:T(8,128)(2,1)S(1)} %shard_map.113.queries, f32[128,128]{1,0:T(8,128)S(1)} %get-tuple-element.16.old_largest, f32[128,128]{1,0:T(8,128)S(1)} %get-tuple-element.17.old_total, f32[128,128]{1,0:T(8,128)S(1)} %get-tuple-element.18.old_summed, ...), custom_call_target="tpu_custom_call" | custom-call | tf_op jit(solution)/shard_map/pallas_call | solution.py:205
  73.3 3.6 %all-to-all-start.2 = ((bf16[16,128,128]{2,1,0:T(8,128)(2,1)}), bf16[16,128,128]{2,1,0:T(8,128)(2,1)S(1)}, u32[]{:S(2)}, u32[]{:S(2)}) async-start(bf16[16,128,128]{2,1,0:T(8,128)(2,1)} %shard_map.116), calls=%async_computation.2 | async-start | bytes 1048576 | tf_op jit(solution)/shard_map/all_to_all | solution.py:274
  76.9 0.0 copy-done
  76.9 0.0 copy-done.1
  76.9 0.8 shard_map.118
  77.7 9.4 %all-to-all-done.2.parts = bf16[16,128,128]{2,1,0:T(8,128)(2,1)S(1)} async-done(((bf16[16,128,128]{2,1,0:T(8,128)(2,1)}), bf16[16,128,128]{2,1,0:T(8,128)(2,1)S(1)}, u32[]{:S(2)}, u32[]{:S(2)}) %all-to-all-start.2) | async-done | bytes 524320 | tf_op jit(solution)/shard_map/all_to_all | solution.py:274
  87.1 0.7 shard_map.117
  (3 shorter events, 0.1 us)
Async XLA Ops:
  2.8 39.8 %all-to-all-start = ((bf16[16,272,128]{2,1,0:T(8,128)(2,1)}), bf16[16,272,128]{2,1,0:T(8,128)(2,1)S(1)}, u32[]{:S(2)}, u32[]{:S(2)}) async-start(bf16[16,272,128]{2,1,0:T(8,128)(2,1)} %get-tuple-element.12), calls=%async_computation | async-start | bytes 2228224 | tf_op jit(solution)/shard_map/all_to_all | solution.py:249
  43.7 21.3 %collective-permute-start = (bf16[16,208,128]{2,1,0:T(8,128)(2,1)}, bf16[16,208,128]{2,1,0:T(8,128)(2,1)S(1)}, u32[]{:S(2)}, u32[]{:S(2)}) collective-permute-start(bf16[16,208,128]{2,1,0:T(8,128)(2,1)} %pad_maximum_fusion), channel_id=1, source_target_pairs={{0,16},{16,0},{32,48},{48,32},{64,80},{80,64},{96,112},{112,96},{1... | collective-permute-start | bytes 2555912 | tf_op jit(solution)/shard_map/ppermute | solution.py:260
  56.2 15.6 %all-to-all-start.1 = ((bf16[32,16,128]{2,1,0:T(8,128)(2,1)}), bf16[32,16,128]{2,1,0:T(8,128)(2,1)S(1)}, u32[]{:S(2)}, u32[]{:S(2)}) async-start(bf16[32,16,128]{2,1,0:T(8,128)(2,1)} %shard_map.115), calls=%async_computation.1 | async-start | bytes 262144 | tf_op jit(solution)/shard_map/all_to_all | solution.py:258
  71.8 5.2 %copy-start = (bf16[1,72,128]{2,1,0:T(8,128)(2,1)S(1)}, bf16[1,72,128]{2,1,0:T(8,128)(2,1)}, u32[]{:S(2)}) copy-start(bf16[1,72,128]{2,1,0:T(8,128)(2,1)} %param.15) | copy-start | bytes 55300
  71.8 5.2 %copy-start.1 = (bf16[1,72,128]{2,1,0:T(8,128)(2,1)S(1)}, bf16[1,72,128]{2,1,0:T(8,128)(2,1)}, u32[]{:S(2)}) copy-start(bf16[1,72,128]{2,1,0:T(8,128)(2,1)} %param.16) | copy-start | bytes 55300
  73.3 13.8 %all-to-all-start.2 = ((bf16[16,128,128]{2,1,0:T(8,128)(2,1)}), bf16[16,128,128]{2,1,0:T(8,128)(2,1)S(1)}, u32[]{:S(2)}, u32[]{:S(2)}) async-start(bf16[16,128,128]{2,1,0:T(8,128)(2,1)} %shard_map.116), calls=%async_computation.2 | async-start | bytes 1048576 | tf_op jit(solution)/shard_map/all_to_all | solution.py:274

commit v4 on v3

--- a/solution.py
+++ b/solution.py
@@ -88,11 +88,11 @@
         axis=1,
     ).astype(BF16)
     rounded = dot_nt(narrow, gathered_tokens(tokens)).astype(BF16)
-    for place in range(CHIPS * CORES):
-        keyvalue[place] = rounded
-
-
-def project_queries(tokens, weights, queries):
+    for chip in range(CHIPS):
+        keyvalue[chip] = rounded
+
+
+def project_queries(tokens, weights):
     square = jnp.concatenate(
         [
             jnp.concatenate([weights[core, chunk, 0:HALF, :] for core in range(CORES)], axis=0)
@@ -100,47 +100,47 @@
         ],
         axis=1,
     )
-    queries[...] = dot_nt(gathered_tokens(tokens), square).astype(BF16)
+    return dot_nt(gathered_tokens(tokens), square).astype(BF16)
 
 
 def new_columns(keyvalue, core, first):
-    return jnp.concatenate([keyvalue[CORES * chip + core] for chip in range(first, first + CHIPS // 2)], axis=0)
+    return jnp.concatenate([keyvalue[core, chip] for chip in range(first, first + CHIPS // 2)], axis=0)
 
 
 def token_of(index, core):
     return ((index >> 3) << 4) + OWN * core + (index & 7)
 
 
-def attend_cached(length_ref, core_ref, queries, own, peer, largest_out, total_out, summed_out):
+def attend_cached(length_ref, own, weights, keys, values, queries, largest_out, total_out, summed_out):
     length = length_ref[0]
-    core = core_ref[0]
     scale = float(LANES) ** (-0.5)
-    query_rows = queries[...]
+    query_rows = project_queries(own, weights)
+    queries[...] = query_rows
     places = CHIPS * PAGE
     lane = iota((1, places), 1)
     start = lane + PAGE * ((lane * 911) >> 16)
     scored = []
     value_sets = []
-    for source, side in ((own, core), (peer, 1 - core)):
-        keys = source[:, 0:PAGE, :].astype(F32).reshape(places, LANES).astype(BF16)
-        value_sets.append(source[:, PAGE:KV_ROWS, :].astype(F32).reshape(places, LANES).astype(BF16))
-        scores = dot_nt(query_rows, keys) * scale
+    for side in range(CORES):
+        key_rows = keys[side].astype(F32).reshape(places, LANES).astype(BF16)
+        value_sets.append(values[side].astype(F32).reshape(places, LANES).astype(BF16))
+        scores = dot_nt(query_rows, key_rows) * scale
         scored.append(jnp.where(start + PAGE * side < length, scores, NEGATIVE))
     largest = jnp.maximum(
         jnp.max(scored[0], axis=1, keepdims=True), jnp.max(scored[1], axis=1, keepdims=True)
     )
     total = jnp.zeros((LANES, 1), F32)
     summed = jnp.zeros((LANES, LANES), F32)
-    for scores, values in zip(scored, value_sets):
+    for scores, value_rows in zip(scored, value_sets):
         terms = jnp.where(scores > 0.5 * NEGATIVE, jnp.exp(scores - largest), 0.0)
         total = total + jnp.sum(terms, axis=1, keepdims=True)
-        summed = summed + dot(terms.astype(BF16), values)
+        summed = summed + dot(terms.astype(BF16), value_rows)
     largest_out[...] = jnp.broadcast_to(largest, (LANES, LANES))
     total_out[...] = jnp.broadcast_to(total, (LANES, LANES))
     summed_out[...] = summed
 
 
-def attend_new(core_ref, queries, old_largest, old_total, old_summed, keyvalue, planes, peer, result):
+def attend_new(core_ref, queries, old_largest, old_total, old_summed, keyvalue, out_w, result):
     core = core_ref[0]
     scale = float(LANES) ** (-0.5)
     query_rows = queries[...]
@@ -157,13 +157,9 @@
     summed = old_summed[...] * factor
     for side in range(CORES):
         summed = summed + dot_nt(terms[side].astype(BF16), new_columns(keyvalue, side, CHIPS // 2))
-    turned = pltpu.roll(summed, HALF, 1)
-    summed = jnp.where(core == 0, summed, turned)
     attended = (summed / total).astype(BF16)
     for chunk in range(CHUNKS):
-        square = jnp.concatenate(
-            [planes[chunk, WEIGHT_ROWS : WEIGHT_ROWS + HALF, :], peer[chunk, KV_ROWS : KV_ROWS + HALF, :]], axis=0
-        )
+        square = jnp.concatenate([out_w[0, chunk], out_w[1, chunk]], axis=0)
         part = dot(attended, square)
         result[:, OWN * chunk : OWN * (chunk + 1), :] = part.reshape(CHIPS, OWN, LANES).astype(BF16)
 
@@ -250,25 +246,24 @@
     planes = lax.all_gather(weights, "gy", axis=0, tiled=False)
     own, planes = lax.optimization_barrier((own, planes))
     inner = lax.all_gather(planes[:, :WEIGHT_ROWS], "gx", axis=0, tiled=False, axis_index_groups=ONE_CHIP)
-    (rows,) = call(
-        project_keyvalue,
-        [((CHIPS * CORES, CORES * OWN, LANES), BF16)],
-        (own, inner),
-    )
-    keyvalue = lax.all_to_all(rows, "gx", 0, 0, tiled=True)
-    swapped = jnp.concatenate([own[:, :KV_ROWS], planes[:, WEIGHT_ROWS:]], axis=1)
-    peer = lax.ppermute(swapped, "gx", SWAP)
-    (queries,) = call(project_queries, [((LANES, LANES), BF16)], (own, inner))
-    largest, total, summed = call(
+    (rows,) = call(project_keyvalue, [((CHIPS, CORES * OWN, LANES), BF16)], (own, inner))
+    own, inner, planes, rows = lax.optimization_barrier((own, inner, planes, rows))
+    columns = lax.all_to_all(rows, "gx", 0, 0, tiled=True, axis_index_groups=SAME_CORE)
+    outer = lax.all_gather(planes[:, WEIGHT_ROWS:], "gx", axis=0, tiled=False, axis_index_groups=ONE_CHIP)
+    keys = lax.all_gather(own[:, :PAGE], "gx", axis=0, tiled=False, axis_index_groups=ONE_CHIP)
+    values = lax.all_gather(own[:, PAGE:KV_ROWS], "gx", axis=0, tiled=False, axis_index_groups=ONE_CHIP)
+    queries, largest, total, summed = call(
         attend_cached,
-        [((LANES, LANES), F32)] * 3,
-        (cache_length, core, queries, own, peer),
-        scalars=2,
-    )
+        [((LANES, LANES), BF16)] + [((LANES, LANES), F32)] * 3,
+        (cache_length, own, inner, keys, values),
+        scalars=1,
+    )
+    columns, outer, summed = lax.optimization_barrier((columns, outer, summed))
+    keyvalue = lax.all_gather(columns, "gx", axis=0, tiled=False, axis_index_groups=ONE_CHIP)
     (parts,) = call(
         attend_new,
         [((CHIPS, LANES, LANES), BF16)],
-        (core, queries, largest, total, summed, keyvalue, planes, peer),
+        (core, queries, largest, total, summed, keyvalue, outer),
         scalars=1,
     )
     collected = lax.all_to_all(parts, "gx", 0, 0, tiled=True, axis_index_groups=SAME_CORE)

time: 88.3 us -> 90.7 us (1.027)
  blocking collectives: 34.6 us -> 50.1 us
  starting transfers between devices: 28.2 us -> 21.8 us
  waiting for transfers between devices: 15.2 us -> 9.52 us
  other arithmetic: 0.98 us -> 0 us
    ppermute x1 -> x0, starting transfers between devices: 9.17 us -> none  [body(): peer = lax.ppermute(swapped, 'gx', SWAP)]
    all_gather x0 -> x4, blocking collectives: none -> 8.82 us  [the longest x1 2.51 us: body(): lax.all_gather(own[:, PAGE:KV_ROWS], 'gx', axis=0, tiled=False, axis_inde...]
    all_gather x1, blocking collectives: 2.37 us -> 8.73 us  [body(): lax.all_gather(planes[:, :WEIGHT_ROWS], 'gx', axis=0, tiled=False, axis_i...]
    all_to_all x1, waiting for transfers between devices: 5.79 us -> 0.01 us  [body(): lax.all_to_all(rows, 'gx', 0, 0, tiled=True, axis_index_groups=SAME_CORE)]
    all_to_all x1, starting transfers between devices: 3.57 us -> 6.93 us  [body(): lax.all_to_all(parts, 'gx', 0, 0, tiled=True, axis_index_groups=SAME_CORE)]
    concatenate x1 -> x0, other arithmetic: 0.98 us -> none  [body(): jnp.concatenate([own[:, :KV_ROWS], planes[:, WEIGHT_ROWS:]], axis=1)]
    pallas_call x7 -> x6, Pallas kernels: 7.36 us -> 7.35 us  [call(): pl.pallas_call(kernel, out_shape=[jax.ShapeDtypeStruct(shape, dtype) for...]
  transfers between devices with their start and end apart: 4 -> 3, of which waited for: 2 -> 1; matrix products, arithmetic and copies ran while one was open for 0% -> 0% of each run, Pallas kernels for 3% -> 2%
where the time goes in v4:
time: 90.7 us; the launch traced here: 90.2 us
  blocking collectives  50.1 us (55%)
  starting transfers between devices  21.8 us (24%)
  waiting for transfers between devices  9.52 us (10%)
  Pallas kernels  7.35 us (8%)
  between operations  1.37 us (2%)
    all_gather x1, blocking collectives, body(): planes = lax.all_gather(weights, 'gy', axis=0, tiled=False)  32.6 us
    all_to_all x1, waiting for transfers between devices, body(): lax.all_to_all(parts, 'gx', 0, 0, tiled=True, axis_index_groups=SAME_CORE)  9.51 us
    all_gather x1, blocking collectives, body(): lax.all_gather(planes[:, :WEIGHT_ROWS], 'gx', axis=0, tiled=False, axis_i...  8.73 us
    all_to_all x1, starting transfers between devices, body(): lax.all_to_all(send, 'gx', 0, 0, tiled=True, axis_index_groups=SAME_CORE)  7.6 us
    pallas_call x6, Pallas kernels, call(): pl.pallas_call(kernel, out_shape=[jax.ShapeDtypeStruct(shape, dtype) for...  7.35 us
    all_to_all x1, starting transfers between devices, body(): lax.all_to_all(rows, 'gx', 0, 0, tiled=True, axis_index_groups=SAME_CORE)  7.26 us
    all_to_all x1, starting transfers between devices, body(): lax.all_to_all(parts, 'gx', 0, 0, tiled=True, axis_index_groups=SAME_CORE)  6.93 us
    all_gather x1, blocking collectives, body(): lax.all_gather(own[:, PAGE:KV_ROWS], 'gx', axis=0, tiled=False, axis_inde...  2.51 us
  transfers between devices with their start and end apart: 3, of which 1 were waited for; matrix products, arithmetic and copies ran while one was open for 0% of the time, Pallas kernels for 2%

profile of v4, /device:TPU:1, one launch (start us, length us, event | category | flops | bytes accessed | tf_op | source)
XLA Modules:
  0.0 90.2 jit_solution(2553761987601874761)
XLA Ops:
  0.6 2.1 %shard_map.112 = (bf16[16,272,128]{2,1,0:T(8,128)(2,1)}, bf16[136,128]{1,0:T(8,128)(2,1)S(1)}) custom-call(bf16[8,2048]{1,0:T(8,128)(2,1)} %bitcast.31, f32[1,2048]{1,0:T(1,128)} %bitcast.33, f32[1,2048]{1,0:T(1,128)} %bitcast.34, bf16[64,128]{1,0:T(8,128)(2,1)} %bitcast.32, bf16[8,128]{1,0:T(8,128)(2,1)} %bitcast.35, bf16[64,128]{1,0:T(8,128)(2,1)} %out_w.1, ...), custom_call_target="tpu_custom_call" | custom-call | tf_op jit(solution)/shard_map/pallas_call | solution.py:201
  2.8 7.6 %all-to-all-start = ((bf16[16,272,128]{2,1,0:T(8,128)(2,1)}), bf16[16,272,128]{2,1,0:T(8,128)(2,1)S(1)}, u32[]{:S(2)}, u32[]{:S(2)}) async-start(bf16[16,272,128]{2,1,0:T(8,128)(2,1)} %get-tuple-element.20), calls=%async_computation | async-start | bytes 2228224 | tf_op jit(solution)/shard_map/all_to_all | solution.py:245
  11.0 32.6 %all-gather = bf16[2176,128]{1,0:T(8,128)(2,1)S(1)} all-gather(bf16[136,128]{1,0:T(8,128)(2,1)S(1)} %get-tuple-element.21), channel_id=2, replica_groups=mesh['gx'=32,'gy'=16] {'gy'}, dimensions={0}, use_global_device_ids=true | all-gather | bytes 591872 | tf_op jit(solution)/shard_map/all_gather | solution.py:246
  43.6 0.0 all-to-all-done.tokens.own
  43.6 8.7 %all-gather.1 = bf16[32,72,128]{2,1,0:T(8,128)(2,1)S(1)} all-gather(bf16[16,72,128]{2,1,0:T(8,128)(2,1)S(1)} %slice.12), channel_id=3, replica_groups={{0,16},{32,48},{64,80},{96,112},{128,144},{160,176},{192,208},{224,240}..., dimensions={0}, use_global_device_ids=true | all-gather | bytes 884736 | tf_op jit(solution)/shard_map/all_gather | solution.py:248
  52.4 0.9 shard_map.113
  53.2 7.3 %all-to-all-start.1 = ((bf16[16,16,128]{2,1,0:T(8,128)(2,1)}), bf16[16,16,128]{2,1,0:T(8,128)(2,1)S(1)}, u32[]{:S(2)}, u32[]{:S(2)}) async-start(bf16[16,16,128]{2,1,0:T(8,128)(2,1)} %shard_map.113), calls=%async_computation.1 | async-start | bytes 131072 | tf_op jit(solution)/shard_map/all_to_all | solution.py:251
  60.6 2.5 %all-gather.3 = bf16[32,72,128]{2,1,0:T(8,128)(2,1)S(1)} all-gather(bf16[16,72,128]{2,1,0:T(8,128)(2,1)S(1)} %get-tuple-element.37), channel_id=5, replica_groups={{0,16},{32,48},{64,80},{96,112},{128,144},{160,176},{192,208},{224,240}..., dimensions={0}, use_global_device_ids=true | all-gather | bytes 884736 | tf_op jit(solution)/shard_map/all_gather | solution.py:254
  63.1 2.2 %all-gather.2 = bf16[32,72,128]{2,1,0:T(8,128)(2,1)S(1)} all-gather(bf16[16,72,128]{2,1,0:T(8,128)(2,1)S(1)} %get-tuple-element.38), channel_id=4, replica_groups={{0,16},{32,48},{64,80},{96,112},{128,144},{160,176},{192,208},{224,240}..., dimensions={0}, use_global_device_ids=true | all-gather | bytes 884736 | tf_op jit(solution)/shard_map/all_gather | solution.py:253
  65.3 2.2 %all-gather.4 = bf16[32,64,128]{2,1,0:T(8,128)(2,1)S(1)} all-gather(bf16[16,64,128]{2,1,0:T(8,128)(2,1)S(1)} %slice.15), channel_id=6, replica_groups={{0,16},{32,48},{64,80},{96,112},{128,144},{160,176},{192,208},{224,240}..., dimensions={0}, use_global_device_ids=true | all-gather | bytes 786432 | tf_op jit(solution)/shard_map/all_gather | solution.py:252
  67.5 1.3 %shard_map.114 = (bf16[128,128]{1,0:T(8,128)(2,1)S(1)}, f32[128,128]{1,0:T(8,128)S(1)}, f32[128,128]{1,0:T(8,128)S(1)}, f32[128,128]{1,0:T(8,128)S(1)}) custom-call(s32[1]{0:T(128)S(6)} %copy.12.length_ref, bf16[16,272,128]{2,1,0:T(8,128)(2,1)S(1)} %all-to-all-done.tokens.own, bf16[2,16,72,128]{3,2,1,0:T(8,128)(2,1)S(1)} %bitcast.18, ...), custom_call_target="tpu_custom_call" | custom-call | tf_op jit(solution)/shard_map/pallas_call | solution.py:201
  68.8 0.0 all-to-all-done.1
  68.8 1.9 %all-gather.5 = bf16[32,16,128]{2,1,0:T(8,128)(2,1)S(1)} all-gather(bf16[16,16,128]{2,1,0:T(8,128)(2,1)S(1)} %all-to-all-done.1), channel_id=7, replica_groups={{0,16},{32,48},{64,80},{96,112},{128,144},{160,176},{192,208},{224,240}..., dimensions={0}, use_global_device_ids=true | all-gather | bytes 196608 | tf_op jit(solution)/shard_map/all_gather | solution.py:262
  70.8 0.0 copy-start
  70.8 0.0 copy-start.1
  70.8 1.5 %shard_map.115 = bf16[16,128,128]{2,1,0:T(8,128)(2,1)} custom-call(s32[1]{0:T(128)S(6)} %and.4.core_ref, bf16[128,128]{1,0:T(8,128)(2,1)S(1)} %get-tuple-element.26.queries, f32[128,128]{1,0:T(8,128)S(1)} %get-tuple-element.27.old_largest, f32[128,128]{1,0:T(8,128)S(1)} %get-tuple-element.28.old_total, f32[128,128]{1,0:T(8,128)S(1)} %get-tuple-element.32.old_summed, ...), custom_call_target="tpu_custom_call" | custom-call | tf_op jit(solution)/shard_map/pallas_call | solution.py:201
  72.2 6.9 %all-to-all-start.2 = ((bf16[16,128,128]{2,1,0:T(8,128)(2,1)}), bf16[16,128,128]{2,1,0:T(8,128)(2,1)S(1)}, u32[]{:S(2)}, u32[]{:S(2)}) async-start(bf16[16,128,128]{2,1,0:T(8,128)(2,1)} %shard_map.115), calls=%async_computation.2 | async-start | bytes 1048576 | tf_op jit(solution)/shard_map/all_to_all | solution.py:269
  79.2 0.0 copy-done
  79.2 0.0 copy-done.1
  79.2 0.8 shard_map.117
  80.0 9.5 %all-to-all-done.2.parts = bf16[16,128,128]{2,1,0:T(8,128)(2,1)S(1)} async-done(((bf16[16,128,128]{2,1,0:T(8,128)(2,1)}), bf16[16,128,128]{2,1,0:T(8,128)(2,1)S(1)}, u32[]{:S(2)}, u32[]{:S(2)}) %all-to-all-start.2) | async-done | bytes 524320 | tf_op jit(solution)/shard_map/all_to_all | solution.py:269
  89.5 0.7 shard_map.116
  (3 shorter events, 0.1 us)
Async XLA Ops:
  2.8 40.8 %all-to-all-start = ((bf16[16,272,128]{2,1,0:T(8,128)(2,1)}), bf16[16,272,128]{2,1,0:T(8,128)(2,1)S(1)}, u32[]{:S(2)}, u32[]{:S(2)}) async-start(bf16[16,272,128]{2,1,0:T(8,128)(2,1)} %get-tuple-element.20), calls=%async_computation | async-start | bytes 2228224 | tf_op jit(solution)/shard_map/all_to_all | solution.py:245
  53.2 15.6 %all-to-all-start.1 = ((bf16[16,16,128]{2,1,0:T(8,128)(2,1)}), bf16[16,16,128]{2,1,0:T(8,128)(2,1)S(1)}, u32[]{:S(2)}, u32[]{:S(2)}) async-start(bf16[16,16,128]{2,1,0:T(8,128)(2,1)} %shard_map.113), calls=%async_computation.1 | async-start | bytes 131072 | tf_op jit(solution)/shard_map/all_to_all | solution.py:251
  70.8 8.4 %copy-start = (bf16[1,72,128]{2,1,0:T(8,128)(2,1)S(1)}, bf16[1,72,128]{2,1,0:T(8,128)(2,1)}, u32[]{:S(2)}) copy-start(bf16[1,72,128]{2,1,0:T(8,128)(2,1)} %param.15) | copy-start | bytes 55300
  70.8 8.4 %copy-start.1 = (bf16[1,72,128]{2,1,0:T(8,128)(2,1)S(1)}, bf16[1,72,128]{2,1,0:T(8,128)(2,1)}, u32[]{:S(2)}) copy-start(bf16[1,72,128]{2,1,0:T(8,128)(2,1)} %param.16) | copy-start | bytes 55300
  72.2 17.3 %all-to-all-start.2 = ((bf16[16,128,128]{2,1,0:T(8,128)(2,1)}), bf16[16,128,128]{2,1,0:T(8,128)(2,1)S(1)}, u32[]{:S(2)}, u32[]{:S(2)}) async-start(bf16[16,128,128]{2,1,0:T(8,128)(2,1)} %shard_map.115), calls=%async_computation.2 | async-start | bytes 1048576 | tf_op jit(solution)/shard_map/all_to_all | solution.py:269

commit v5 on v4

--- a/solution.py
+++ b/solution.py
@@ -111,8 +111,9 @@
     return ((index >> 3) << 4) + OWN * core + (index & 7)
 
 
-def attend_cached(length_ref, own, weights, keys, values, queries, largest_out, total_out, summed_out):
+def attend_cached(length_ref, core_ref, own, weights, peer, queries, largest_out, total_out, summed_out):
     length = length_ref[0]
+    core = core_ref[0]
     scale = float(LANES) ** (-0.5)
     query_rows = project_queries(own, weights)
     queries[...] = query_rows
@@ -121,20 +122,20 @@
     start = lane + PAGE * ((lane * 911) >> 16)
     scored = []
     value_sets = []
-    for side in range(CORES):
-        key_rows = keys[side].astype(F32).reshape(places, LANES).astype(BF16)
-        value_sets.append(values[side].astype(F32).reshape(places, LANES).astype(BF16))
-        scores = dot_nt(query_rows, key_rows) * scale
+    for source, side in ((own, core), (peer, 1 - core)):
+        keys = source[:, 0:PAGE, :].astype(F32).reshape(places, LANES).astype(BF16)
+        value_sets.append(source[:, PAGE:KV_ROWS, :].astype(F32).reshape(places, LANES).astype(BF16))
+        scores = dot_nt(query_rows, keys) * scale
         scored.append(jnp.where(start + PAGE * side < length, scores, NEGATIVE))
     largest = jnp.maximum(
         jnp.max(scored[0], axis=1, keepdims=True), jnp.max(scored[1], axis=1, keepdims=True)
     )
     total = jnp.zeros((LANES, 1), F32)
     summed = jnp.zeros((LANES, LANES), F32)
-    for scores, value_rows in zip(scored, value_sets):
+    for scores, values in zip(scored, value_sets):
         terms = jnp.where(scores > 0.5 * NEGATIVE, jnp.exp(scores - largest), 0.0)
         total = total + jnp.sum(terms, axis=1, keepdims=True)
-        summed = summed + dot(terms.astype(BF16), value_rows)
+        summed = summed + dot(terms.astype(BF16), values)
     largest_out[...] = jnp.broadcast_to(largest, (LANES, LANES))
     total_out[...] = jnp.broadcast_to(total, (LANES, LANES))
     summed_out[...] = summed
@@ -250,13 +251,12 @@
     own, inner, planes, rows = lax.optimization_barrier((own, inner, planes, rows))
     columns = lax.all_to_all(rows, "gx", 0, 0, tiled=True, axis_index_groups=SAME_CORE)
     outer = lax.all_gather(planes[:, WEIGHT_ROWS:], "gx", axis=0, tiled=False, axis_index_groups=ONE_CHIP)
-    keys = lax.all_gather(own[:, :PAGE], "gx", axis=0, tiled=False, axis_index_groups=ONE_CHIP)
-    values = lax.all_gather(own[:, PAGE:KV_ROWS], "gx", axis=0, tiled=False, axis_index_groups=ONE_CHIP)
+    peer = lax.ppermute(own[:, :KV_ROWS], "gx", SWAP)
     queries, largest, total, summed = call(
         attend_cached,
         [((LANES, LANES), BF16)] + [((LANES, LANES), F32)] * 3,
-        (cache_length, own, inner, keys, values),
-        scalars=1,
+        (cache_length, core, own, inner, peer),
+        scalars=2,
     )
     columns, outer, summed = lax.optimization_barrier((columns, outer, summed))
     keyvalue = lax.all_gather(columns, "gx", axis=0, tiled=False, axis_index_groups=ONE_CHIP)

time: 90.7 us -> 89.7 us (0.989)
  blocking collectives: 50.1 us -> 46.7 us
  waiting for transfers between devices: 9.52 us -> 12.2 us
  starting transfers between devices: 21.8 us -> 20.6 us
    all_gather x2 -> x0, blocking collectives: 4.72 us -> none  [the longest x1 2.51 us: body(): lax.all_gather(own[:, PAGE:KV_ROWS], 'gx', axis=0, tiled=False, axis_inde...]
    all_to_all x1, starting transfers between devices: 6.93 us -> 3.57 us  [body(): lax.all_to_all(parts, 'gx', 0, 0, tiled=True, axis_index_groups=SAME_CORE)]
    all_to_all x1, waiting for transfers between devices: 0.01 us -> 2.89 us  [body(): lax.all_to_all(rows, 'gx', 0, 0, tiled=True, axis_index_groups=SAME_CORE)]
    ppermute x0 -> x1, starting transfers between devices: none -> 2.27 us  [body(): peer = lax.ppermute(own[:, :KV_ROWS], 'gx', SWAP)]
    all_gather x1, blocking collectives: 1.93 us -> 3.12 us  [body(): lax.all_gather(columns, 'gx', axis=0, tiled=False, axis_index_groups=ONE_...]
  transfers between devices with their start and end apart: 3 -> 4, of which waited for: 1 -> 2; matrix products, arithmetic and copies ran while one was open for 0% -> 0% of each run, Pallas kernels for 2% -> 2%
where the time goes in v5:
time: 89.7 us; the launch traced here: 89.2 us
  blocking collectives  46.7 us (52%)
  starting transfers between devices  20.6 us (23%)
  waiting for transfers between devices  12.2 us (14%)
  Pallas kernels  7.35 us (8%)
  between operations  1.37 us (2%)
    all_gather x1, blocking collectives, body(): planes = lax.all_gather(weights, 'gy', axis=0, tiled=False)  32.2 us
    all_to_all x1, waiting for transfers between devices, body(): lax.all_to_all(parts, 'gx', 0, 0, tiled=True, axis_index_groups=SAME_CORE)  9.33 us
    all_gather x1, blocking collectives, body(): lax.all_gather(planes[:, :WEIGHT_ROWS], 'gx', axis=0, tiled=False, axis_i...  9.13 us
    all_to_all x1, starting transfers between devices, body(): lax.all_to_all(send, 'gx', 0, 0, tiled=True, axis_index_groups=SAME_CORE)  7.6 us
    pallas_call x6, Pallas kernels, call(): pl.pallas_call(kernel, out_shape=[jax.ShapeDtypeStruct(shape, dtype) for...  7.35 us
    all_to_all x1, starting transfers between devices, body(): lax.all_to_all(rows, 'gx', 0, 0, tiled=True, axis_index_groups=SAME_CORE)  7.19 us
    all_to_all x1, starting transfers between devices, body(): lax.all_to_all(parts, 'gx', 0, 0, tiled=True, axis_index_groups=SAME_CORE)  3.57 us
    all_gather x1, blocking collectives, body(): lax.all_gather(columns, 'gx', axis=0, tiled=False, axis_index_groups=ONE_...  3.12 us
  transfers between devices with their start and end apart: 4, of which 2 were waited for; matrix products, arithmetic and copies ran while one was open for 0% of the time, Pallas kernels for 2%

profile of v5, /device:TPU:1, one launch (start us, length us, event | category | flops | bytes accessed | tf_op | source)
XLA Modules:
  0.0 89.2 jit_solution(7152103434048467792)
XLA Ops:
  0.6 2.1 %shard_map.112 = (bf16[16,272,128]{2,1,0:T(8,128)(2,1)}, bf16[136,128]{1,0:T(8,128)(2,1)S(1)}) custom-call(bf16[8,2048]{1,0:T(8,128)(2,1)} %bitcast.27, f32[1,2048]{1,0:T(1,128)} %bitcast.29, f32[1,2048]{1,0:T(1,128)} %bitcast.30, bf16[64,128]{1,0:T(8,128)(2,1)} %bitcast.28, bf16[8,128]{1,0:T(8,128)(2,1)} %bitcast.31, bf16[64,128]{1,0:T(8,128)(2,1)} %out_w.1, ...), custom_call_target="tpu_custom_call" | custom-call | tf_op jit(solution)/shard_map/pallas_call | solution.py:202
  2.8 7.6 %all-to-all-start = ((bf16[16,272,128]{2,1,0:T(8,128)(2,1)}), bf16[16,272,128]{2,1,0:T(8,128)(2,1)S(1)}, u32[]{:S(2)}, u32[]{:S(2)}) async-start(bf16[16,272,128]{2,1,0:T(8,128)(2,1)} %get-tuple-element.20), calls=%async_computation | async-start | bytes 2228224 | tf_op jit(solution)/shard_map/all_to_all | solution.py:246
  10.4 32.2 %all-gather = bf16[2176,128]{1,0:T(8,128)(2,1)S(1)} all-gather(bf16[136,128]{1,0:T(8,128)(2,1)S(1)} %get-tuple-element.21), channel_id=2, replica_groups=mesh['gx'=32,'gy'=16] {'gy'}, dimensions={0}, use_global_device_ids=true | all-gather | bytes 591872 | tf_op jit(solution)/shard_map/all_gather | solution.py:247
  42.6 0.0 all-to-all-done.tokens.own
  42.6 9.1 %all-gather.1 = bf16[32,72,128]{2,1,0:T(8,128)(2,1)S(1)} all-gather(bf16[16,72,128]{2,1,0:T(8,128)(2,1)S(1)} %slice.9), channel_id=3, replica_groups={{0,16},{32,48},{64,80},{96,112},{128,144},{160,176},{192,208},{224,240}..., dimensions={0}, use_global_device_ids=true | all-gather | bytes 884736 | tf_op jit(solution)/shard_map/all_gather | solution.py:249
  51.8 0.9 shard_map.113
  52.6 0.8 slice.10
  53.5 2.3 %collective-permute-start = (bf16[16,144,128]{2,1,0:T(8,128)(2,1)}, bf16[16,144,128]{2,1,0:T(8,128)(2,1)S(1)}, u32[]{:S(2)}, u32[]{:S(2)}) collective-permute-start(bf16[16,144,128]{2,1,0:T(8,128)(2,1)} %slice.10), channel_id=1, source_target_pairs={{0,16},{16,0},{32,48},{48,32},{64,80},{80,64},{96,112},{112,96},{1... | collective-permute-start | bytes 1769480 | tf_op jit(solution)/shard_map/ppermute | solution.py:254
  56.4 7.2 %all-to-all-start.1 = ((bf16[16,16,128]{2,1,0:T(8,128)(2,1)}), bf16[16,16,128]{2,1,0:T(8,128)(2,1)S(1)}, u32[]{:S(2)}, u32[]{:S(2)}) async-start(bf16[16,16,128]{2,1,0:T(8,128)(2,1)} %shard_map.113), calls=%async_computation.1 | async-start | bytes 131072 | tf_op jit(solution)/shard_map/all_to_all | solution.py:252
  63.6 2.2 %all-gather.2 = bf16[32,64,128]{2,1,0:T(8,128)(2,1)S(1)} all-gather(bf16[16,64,128]{2,1,0:T(8,128)(2,1)S(1)} %slice.11), channel_id=4, replica_groups={{0,16},{32,48},{64,80},{96,112},{128,144},{160,176},{192,208},{224,240}..., dimensions={0}, use_global_device_ids=true | all-gather | bytes 786432 | tf_op jit(solution)/shard_map/all_gather | solution.py:253
  65.9 0.0 collective-permute-done.peer
  65.9 1.3 %shard_map.114 = (bf16[128,128]{1,0:T(8,128)(2,1)S(1)}, f32[128,128]{1,0:T(8,128)S(1)}, f32[128,128]{1,0:T(8,128)S(1)}, f32[128,128]{1,0:T(8,128)S(1)}) custom-call(s32[1]{0:T(128)S(6)} %copy.12.length_ref, s32[1]{0:T(128)S(6)} %and.4.core_ref, bf16[16,272,128]{2,1,0:T(8,128)(2,1)S(1)} %all-to-all-done.tokens.own, bf16[2,16,72,128]{3,2,1,0:T(8,128)(2,1)S(1)} %bitcast.16, ...), custom_call_target="tpu_custom_call" | custom-call | tf_op jit(solution)/shard_map/pallas_call | solution.py:202
  67.2 2.9 %all-to-all-done.1 = bf16[16,16,128]{2,1,0:T(8,128)(2,1)S(1)} async-done(((bf16[16,16,128]{2,1,0:T(8,128)(2,1)}), bf16[16,16,128]{2,1,0:T(8,128)(2,1)S(1)}, u32[]{:S(2)}, u32[]{:S(2)}) %all-to-all-start.1) | async-done | bytes 65568 | tf_op jit(solution)/shard_map/all_to_all | solution.py:252
  70.1 3.1 %all-gather.3 = bf16[32,16,128]{2,1,0:T(8,128)(2,1)S(1)} all-gather(bf16[16,16,128]{2,1,0:T(8,128)(2,1)S(1)} %all-to-all-done.1), channel_id=5, replica_groups={{0,16},{32,48},{64,80},{96,112},{128,144},{160,176},{192,208},{224,240}..., dimensions={0}, use_global_device_ids=true | all-gather | bytes 196608 | tf_op jit(solution)/shard_map/all_gather | solution.py:262
  73.2 0.0 copy-start
  73.2 0.0 copy-start.1
  73.3 1.5 %shard_map.115 = bf16[16,128,128]{2,1,0:T(8,128)(2,1)} custom-call(s32[1]{0:T(128)S(6)} %and.4.core_ref, bf16[128,128]{1,0:T(8,128)(2,1)S(1)} %get-tuple-element.26.queries, f32[128,128]{1,0:T(8,128)S(1)} %get-tuple-element.27.old_largest, f32[128,128]{1,0:T(8,128)S(1)} %get-tuple-element.28.old_total, f32[128,128]{1,0:T(8,128)S(1)} %get-tuple-element.32.old_summed, ...), custom_call_target="tpu_custom_call" | custom-call | tf_op jit(solution)/shard_map/pallas_call | solution.py:202
  74.7 3.6 %all-to-all-start.2 = ((bf16[16,128,128]{2,1,0:T(8,128)(2,1)}), bf16[16,128,128]{2,1,0:T(8,128)(2,1)S(1)}, u32[]{:S(2)}, u32[]{:S(2)}) async-start(bf16[16,128,128]{2,1,0:T(8,128)(2,1)} %shard_map.115), calls=%async_computation.2 | async-start | bytes 1048576 | tf_op jit(solution)/shard_map/all_to_all | solution.py:269
  78.3 0.0 copy-done
  78.3 0.0 copy-done.1
  78.3 0.8 shard_map.117
  79.2 9.3 %all-to-all-done.2.parts = bf16[16,128,128]{2,1,0:T(8,128)(2,1)S(1)} async-done(((bf16[16,128,128]{2,1,0:T(8,128)(2,1)}), bf16[16,128,128]{2,1,0:T(8,128)(2,1)S(1)}, u32[]{:S(2)}, u32[]{:S(2)}) %all-to-all-start.2) | async-done | bytes 524320 | tf_op jit(solution)/shard_map/all_to_all | solution.py:269
  88.5 0.7 shard_map.116
  (2 shorter events, 0.0 us)
Async XLA Ops:
  2.8 39.8 %all-to-all-start = ((bf16[16,272,128]{2,1,0:T(8,128)(2,1)}), bf16[16,272,128]{2,1,0:T(8,128)(2,1)S(1)}, u32[]{:S(2)}, u32[]{:S(2)}) async-start(bf16[16,272,128]{2,1,0:T(8,128)(2,1)} %get-tuple-element.20), calls=%async_computation | async-start | bytes 2228224 | tf_op jit(solution)/shard_map/all_to_all | solution.py:246
  53.5 12.4 %collective-permute-start = (bf16[16,144,128]{2,1,0:T(8,128)(2,1)}, bf16[16,144,128]{2,1,0:T(8,128)(2,1)S(1)}, u32[]{:S(2)}, u32[]{:S(2)}) collective-permute-start(bf16[16,144,128]{2,1,0:T(8,128)(2,1)} %slice.10), channel_id=1, source_target_pairs={{0,16},{16,0},{32,48},{48,32},{64,80},{80,64},{96,112},{112,96},{1... | collective-permute-start | bytes 1769480 | tf_op jit(solution)/shard_map/ppermute | solution.py:254
  56.4 13.7 %all-to-all-start.1 = ((bf16[16,16,128]{2,1,0:T(8,128)(2,1)}), bf16[16,16,128]{2,1,0:T(8,128)(2,1)S(1)}, u32[]{:S(2)}, u32[]{:S(2)}) async-start(bf16[16,16,128]{2,1,0:T(8,128)(2,1)} %shard_map.113), calls=%async_computation.1 | async-start | bytes 131072 | tf_op jit(solution)/shard_map/all_to_all | solution.py:252
  73.2 5.1 %copy-start = (bf16[1,72,128]{2,1,0:T(8,128)(2,1)S(1)}, bf16[1,72,128]{2,1,0:T(8,128)(2,1)}, u32[]{:S(2)}) copy-start(bf16[1,72,128]{2,1,0:T(8,128)(2,1)} %param.15) | copy-start | bytes 55300
  73.2 5.1 %copy-start.1 = (bf16[1,72,128]{2,1,0:T(8,128)(2,1)S(1)}, bf16[1,72,128]{2,1,0:T(8,128)(2,1)}, u32[]{:S(2)}) copy-start(bf16[1,72,128]{2,1,0:T(8,128)(2,1)} %param.16) | copy-start | bytes 55300
  74.7 13.8 %all-to-all-start.2 = ((bf16[16,128,128]{2,1,0:T(8,128)(2,1)}), bf16[16,128,128]{2,1,0:T(8,128)(2,1)S(1)}, u32[]{:S(2)}, u32[]{:S(2)}) async-start(bf16[16,128,128]{2,1,0:T(8,128)(2,1)} %shard_map.115), calls=%async_computation.2 | async-start | bytes 1048576 | tf_op jit(solution)/shard_map/all_to_all | solution.py:269

commit v6 on v3

--- a/solution.py
+++ b/solution.py
@@ -19,7 +19,8 @@
 NEW = 256
 NEGATIVE = -1e30
 
-SAME_CORE = [[CORES * chip + core for chip in range(CHIPS)] for core in range(CORES)]
+FIRST = 10
+SAME_CORE = [[CORES * ((at + FIRST) % CHIPS) + core for at in range(CHIPS)] for core in range(CORES)]
 ONE_CHIP = [[CORES * chip + core for core in range(CORES)] for chip in range(CHIPS)]
 SWAP = [(place, place ^ 1) for place in range(CHIPS * CORES)]
 
@@ -108,7 +109,8 @@
 
 
 def token_of(index, core):
-    return ((index >> 3) << 4) + OWN * core + (index & 7)
+    chip = ((index >> 3) + FIRST) & (CHIPS - 1)
+    return (chip << 4) + OWN * core + (index & 7)
 
 
 def attend_cached(length_ref, core_ref, queries, own, peer, largest_out, total_out, summed_out):
@@ -118,7 +120,9 @@
     query_rows = queries[...]
     places = CHIPS * PAGE
     lane = iota((1, places), 1)
-    start = lane + PAGE * ((lane * 911) >> 16)
+    at = (lane * 911) >> 16
+    chip = (at + FIRST) & (CHIPS - 1)
+    start = lane - PAGE * at + KV_ROWS * chip
     scored = []
     value_sets = []
     for source, side in ((own, core), (peer, 1 - core)):

time: 88.3 us -> 86.3 us (0.977)
  waiting for transfers between devices: 15.2 us -> 12 us
  starting transfers between devices: 28.2 us -> 29.4 us
    all_to_all x1, starting transfers between devices: 7.89 us -> 3.87 us  [body(): keyvalue = lax.all_to_all(rows, 'gx', 0, 0, tiled=True)]
    all_to_all x1, waiting for transfers between devices: 9.4 us -> 6.1 us  [body(): lax.all_to_all(parts, 'gx', 0, 0, tiled=True, axis_index_groups=SAME_CORE)]
    all_to_all x1, starting transfers between devices: 3.57 us -> 6.66 us  [body(): lax.all_to_all(parts, 'gx', 0, 0, tiled=True, axis_index_groups=SAME_CORE)]
    all_to_all x1, starting transfers between devices: 7.6 us -> 9.73 us  [body(): lax.all_to_all(send, 'gx', 0, 0, tiled=True, axis_index_groups=SAME_CORE)]
where the time goes in v6:
time: 86.3 us; the launch traced here: 85.8 us
  blocking collectives  34.6 us (40%)
  starting transfers between devices  29.4 us (34%)
  waiting for transfers between devices  12 us (14%)
  Pallas kernels  7.35 us (9%)
  between operations  1.37 us (2%)
  other arithmetic  0.98 us (1%)
    all_gather x1, blocking collectives, body(): planes = lax.all_gather(weights, 'gy', axis=0, tiled=False)  32.2 us
    all_to_all x1, starting transfers between devices, body(): lax.all_to_all(send, 'gx', 0, 0, tiled=True, axis_index_groups=SAME_CORE)  9.73 us
    ppermute x1, starting transfers between devices, body(): peer = lax.ppermute(swapped, 'gx', SWAP)  9.1 us
    pallas_call x7, Pallas kernels, call(): pl.pallas_call(kernel, out_shape=[jax.ShapeDtypeStruct(shape, dtype) for...  7.35 us
    all_to_all x1, starting transfers between devices, body(): lax.all_to_all(parts, 'gx', 0, 0, tiled=True, axis_index_groups=SAME_CORE)  6.66 us
    all_to_all x1, waiting for transfers between devices, body(): lax.all_to_all(parts, 'gx', 0, 0, tiled=True, axis_index_groups=SAME_CORE)  6.1 us
    all_to_all x1, waiting for transfers between devices, body(): keyvalue = lax.all_to_all(rows, 'gx', 0, 0, tiled=True)  5.91 us
    all_to_all x1, starting transfers between devices, body(): keyvalue = lax.all_to_all(rows, 'gx', 0, 0, tiled=True)  3.87 us
  transfers between devices with their start and end apart: 4, of which 2 were waited for; matrix products, arithmetic and copies ran while one was open for 0% of the time, Pallas kernels for 3%

profile of v6, /device:TPU:1, one launch (start us, length us, event | category | flops | bytes accessed | tf_op | source)
XLA Modules:
  0.0 85.8 jit_solution(17429097086460513349)
XLA Ops:
  0.6 2.1 %shard_map.112 = (bf16[16,272,128]{2,1,0:T(8,128)(2,1)}, bf16[136,128]{1,0:T(8,128)(2,1)S(1)}) custom-call(bf16[8,2048]{1,0:T(8,128)(2,1)} %bitcast.23, f32[1,2048]{1,0:T(1,128)} %bitcast.25, f32[1,2048]{1,0:T(1,128)} %bitcast.26, bf16[64,128]{1,0:T(8,128)(2,1)} %bitcast.24, bf16[8,128]{1,0:T(8,128)(2,1)} %bitcast.27, bf16[64,128]{1,0:T(8,128)(2,1)} %out_w.1, ...), custom_call_target="tpu_custom_call" | custom-call | tf_op jit(solution)/shard_map/pallas_call | solution.py:209
  2.8 9.7 %all-to-all-start = ((bf16[16,272,128]{2,1,0:T(8,128)(2,1)}), bf16[16,272,128]{2,1,0:T(8,128)(2,1)S(1)}, u32[]{:S(2)}, u32[]{:S(2)}) async-start(bf16[16,272,128]{2,1,0:T(8,128)(2,1)} %get-tuple-element.12), calls=%async_computation | async-start | bytes 2228224 | tf_op jit(solution)/shard_map/all_to_all | solution.py:253
  12.5 32.2 %all-gather = bf16[2176,128]{1,0:T(8,128)(2,1)S(1)} all-gather(bf16[136,128]{1,0:T(8,128)(2,1)S(1)} %get-tuple-element.13), channel_id=2, replica_groups=mesh['gx'=32,'gy'=16] {'gy'}, dimensions={0}, use_global_device_ids=true | all-gather | bytes 591872 | tf_op jit(solution)/shard_map/all_gather | solution.py:254
  44.7 0.0 all-to-all-done.tokens.own
  44.8 1.0 %pad_maximum_fusion = bf16[16,208,128]{2,1,0:T(8,128)(2,1)} fusion(bf16[16,64,128]{2,1,0:T(8,128)(2,1)S(1)} %slice.11, bf16[16,144,128]{2,1,0:T(8,128)(2,1)S(1)} %slice.10), kind=kLoop, calls=%fused_computation | loop fusion | flops 1703936 | bytes 1703936 | tf_op jit(solution)/shard_map/concatenate | solution.py:263
  45.8 9.1 %collective-permute-start = (bf16[16,208,128]{2,1,0:T(8,128)(2,1)}, bf16[16,208,128]{2,1,0:T(8,128)(2,1)S(1)}, u32[]{:S(2)}, u32[]{:S(2)}) collective-permute-start(bf16[16,208,128]{2,1,0:T(8,128)(2,1)} %pad_maximum_fusion), channel_id=1, source_target_pairs={{0,16},{16,0},{32,48},{48,32},{64,80},{80,64},{96,112},{112,96},{1... | collective-permute-start | bytes 2555912 | tf_op jit(solution)/shard_map/ppermute | solution.py:264
  54.9 2.4 %all-gather.1 = bf16[32,72,128]{2,1,0:T(8,128)(2,1)S(1)} all-gather(bf16[16,72,128]{2,1,0:T(8,128)(2,1)S(1)} %slice.9), channel_id=3, replica_groups={{0,16},{32,48},{64,80},{96,112},{128,144},{160,176},{192,208},{224,240}..., dimensions={0}, use_global_device_ids=true | all-gather | bytes 884736 | tf_op jit(solution)/shard_map/all_gather | solution.py:256
  57.3 0.9 %shard_map.115 = bf16[32,16,128]{2,1,0:T(8,128)(2,1)} custom-call(bf16[16,272,128]{2,1,0:T(8,128)(2,1)S(1)} %all-to-all-done.tokens.own, bf16[2,16,72,128]{3,2,1,0:T(8,128)(2,1)S(1)} %bitcast.13), custom_call_target="tpu_custom_call" | custom-call | tf_op jit(solution)/shard_map/pallas_call | solution.py:209
  58.2 3.9 %all-to-all-start.1 = ((bf16[32,16,128]{2,1,0:T(8,128)(2,1)}), bf16[32,16,128]{2,1,0:T(8,128)(2,1)S(1)}, u32[]{:S(2)}, u32[]{:S(2)}) async-start(bf16[32,16,128]{2,1,0:T(8,128)(2,1)} %shard_map.115), calls=%async_computation.1 | async-start | bytes 262144 | tf_op jit(solution)/shard_map/all_to_all | solution.py:262
  62.7 0.3 shard_map.113.queries
  63.0 0.0 collective-permute-done.peer
  63.1 0.9 %shard_map.114 = (f32[128,128]{1,0:T(8,128)S(1)}, f32[128,128]{1,0:T(8,128)S(1)}, f32[128,128]{1,0:T(8,128)S(1)}) custom-call(s32[1]{0:T(128)S(6)} %copy.12.length_ref, s32[1]{0:T(128)S(6)} %and.4.core_ref, bf16[128,128]{1,0:T(8,128)(2,1)S(1)} %shard_map.113.queries, bf16[16,272,128]{2,1,0:T(8,128)(2,1)S(1)} %all-to-all-done.tokens.own, ...), custom_call_target="tpu_custom_call" | custom-call | tf_op jit(solution)/shard_map/pallas_call | solution.py:209
  64.0 5.9 %all-to-all-done.1.keyvalue = bf16[32,16,128]{2,1,0:T(8,128)(2,1)S(1)} async-done(((bf16[32,16,128]{2,1,0:T(8,128)(2,1)}), bf16[32,16,128]{2,1,0:T(8,128)(2,1)S(1)}, u32[]{:S(2)}, u32[]{:S(2)}) %all-to-all-start.1) | async-done | bytes 131104 | tf_op jit(solution)/shard_map/all_to_all | solution.py:262
  69.9 0.0 copy-start
  69.9 0.0 copy-start.1
  69.9 1.6 %shard_map.116 = bf16[16,128,128]{2,1,0:T(8,128)(2,1)} custom-call(s32[1]{0:T(128)S(6)} %and.4.core_ref, bf16[128,128]{1,0:T(8,128)(2,1)S(1)} %shard_map.113.queries, f32[128,128]{1,0:T(8,128)S(1)} %get-tuple-element.16.old_largest, f32[128,128]{1,0:T(8,128)S(1)} %get-tuple-element.17.old_total, f32[128,128]{1,0:T(8,128)S(1)} %get-tuple-element.18.old_summed, ...), custom_call_target="tpu_custom_call" | custom-call | tf_op jit(solution)/shard_map/pallas_call | solution.py:209
  71.5 6.7 %all-to-all-start.2 = ((bf16[16,128,128]{2,1,0:T(8,128)(2,1)}), bf16[16,128,128]{2,1,0:T(8,128)(2,1)S(1)}, u32[]{:S(2)}, u32[]{:S(2)}) async-start(bf16[16,128,128]{2,1,0:T(8,128)(2,1)} %shard_map.116), calls=%async_computation.2 | async-start | bytes 1048576 | tf_op jit(solution)/shard_map/all_to_all | solution.py:278
  78.1 0.0 copy-done
  78.1 0.0 copy-done.1
  78.2 0.8 shard_map.118
  79.0 6.1 %all-to-all-done.2.parts = bf16[16,128,128]{2,1,0:T(8,128)(2,1)S(1)} async-done(((bf16[16,128,128]{2,1,0:T(8,128)(2,1)}), bf16[16,128,128]{2,1,0:T(8,128)(2,1)S(1)}, u32[]{:S(2)}, u32[]{:S(2)}) %all-to-all-start.2) | async-done | bytes 524320 | tf_op jit(solution)/shard_map/all_to_all | solution.py:278
  85.1 0.7 shard_map.117
  (3 shorter events, 0.1 us)
Async XLA Ops:
  2.8 42.0 %all-to-all-start = ((bf16[16,272,128]{2,1,0:T(8,128)(2,1)}), bf16[16,272,128]{2,1,0:T(8,128)(2,1)S(1)}, u32[]{:S(2)}, u32[]{:S(2)}) async-start(bf16[16,272,128]{2,1,0:T(8,128)(2,1)} %get-tuple-element.12), calls=%async_computation | async-start | bytes 2228224 | tf_op jit(solution)/shard_map/all_to_all | solution.py:253
  45.8 17.3 %collective-permute-start = (bf16[16,208,128]{2,1,0:T(8,128)(2,1)}, bf16[16,208,128]{2,1,0:T(8,128)(2,1)S(1)}, u32[]{:S(2)}, u32[]{:S(2)}) collective-permute-start(bf16[16,208,128]{2,1,0:T(8,128)(2,1)} %pad_maximum_fusion), channel_id=1, source_target_pairs={{0,16},{16,0},{32,48},{48,32},{64,80},{80,64},{96,112},{112,96},{1... | collective-permute-start | bytes 2555912 | tf_op jit(solution)/shard_map/ppermute | solution.py:264
  58.2 11.7 %all-to-all-start.1 = ((bf16[32,16,128]{2,1,0:T(8,128)(2,1)}), bf16[32,16,128]{2,1,0:T(8,128)(2,1)S(1)}, u32[]{:S(2)}, u32[]{:S(2)}) async-start(bf16[32,16,128]{2,1,0:T(8,128)(2,1)} %shard_map.115), calls=%async_computation.1 | async-start | bytes 262144 | tf_op jit(solution)/shard_map/all_to_all | solution.py:262
  69.9 8.2 %copy-start = (bf16[1,72,128]{2,1,0:T(8,128)(2,1)S(1)}, bf16[1,72,128]{2,1,0:T(8,128)(2,1)}, u32[]{:S(2)}) copy-start(bf16[1,72,128]{2,1,0:T(8,128)(2,1)} %param.15) | copy-start | bytes 55300
  69.9 8.2 %copy-start.1 = (bf16[1,72,128]{2,1,0:T(8,128)(2,1)S(1)}, bf16[1,72,128]{2,1,0:T(8,128)(2,1)}, u32[]{:S(2)}) copy-start(bf16[1,72,128]{2,1,0:T(8,128)(2,1)} %param.16) | copy-start | bytes 55300
  71.5 13.6 %all-to-all-start.2 = ((bf16[16,128,128]{2,1,0:T(8,128)(2,1)}), bf16[16,128,128]{2,1,0:T(8,128)(2,1)S(1)}, u32[]{:S(2)}, u32[]{:S(2)}) async-start(bf16[16,128,128]{2,1,0:T(8,128)(2,1)} %shard_map.116), calls=%async_computation.2 | async-start | bytes 1048576 | tf_op jit(solution)/shard_map/all_to_all | solution.py:278

commit v7 on v4

--- a/solution.py
+++ b/solution.py
@@ -19,7 +19,8 @@
 NEW = 256
 NEGATIVE = -1e30
 
-SAME_CORE = [[CORES * chip + core for chip in range(CHIPS)] for core in range(CORES)]
+FIRST = 10
+SAME_CORE = [[CORES * ((at + FIRST) % CHIPS) + core for at in range(CHIPS)] for core in range(CORES)]
 ONE_CHIP = [[CORES * chip + core for core in range(CORES)] for chip in range(CHIPS)]
 SWAP = [(place, place ^ 1) for place in range(CHIPS * CORES)]
 
@@ -88,8 +89,8 @@
         axis=1,
     ).astype(BF16)
     rounded = dot_nt(narrow, gathered_tokens(tokens)).astype(BF16)
-    for chip in range(CHIPS):
-        keyvalue[chip] = rounded
+    for place in range(CHIPS * CORES):
+        keyvalue[place] = rounded
 
 
 def project_queries(tokens, weights):
@@ -104,11 +105,12 @@
 
 
 def new_columns(keyvalue, core, first):
-    return jnp.concatenate([keyvalue[core, chip] for chip in range(first, first + CHIPS // 2)], axis=0)
+    return jnp.concatenate([keyvalue[CORES * chip + core] for chip in range(first, first + CHIPS // 2)], axis=0)
 
 
 def token_of(index, core):
-    return ((index >> 3) << 4) + OWN * core + (index & 7)
+    chip = ((index >> 3) + FIRST) & (CHIPS - 1)
+    return (chip << 4) + OWN * core + (index & 7)
 
 
 def attend_cached(length_ref, own, weights, keys, values, queries, largest_out, total_out, summed_out):
@@ -118,7 +120,9 @@
     queries[...] = query_rows
     places = CHIPS * PAGE
     lane = iota((1, places), 1)
-    start = lane + PAGE * ((lane * 911) >> 16)
+    at = (lane * 911) >> 16
+    chip = (at + FIRST) & (CHIPS - 1)
+    start = lane - PAGE * at + KV_ROWS * chip
     scored = []
     value_sets = []
     for side in range(CORES):
@@ -158,10 +162,15 @@
     for side in range(CORES):
         summed = summed + dot_nt(terms[side].astype(BF16), new_columns(keyvalue, side, CHIPS // 2))
     attended = (summed / total).astype(BF16)
-    for chunk in range(CHUNKS):
-        square = jnp.concatenate([out_w[0, chunk], out_w[1, chunk]], axis=0)
-        part = dot(attended, square)
-        result[:, OWN * chunk : OWN * (chunk + 1), :] = part.reshape(CHIPS, OWN, LANES).astype(BF16)
+    for chunk in range(0, CHUNKS, 2):
+        wide = jnp.concatenate(
+            [jnp.concatenate([out_w[0, at], out_w[1, at]], axis=0) for at in (chunk, chunk + 1)], axis=1
+        )
+        part = dot(attended, wide)
+        for at in range(2):
+            result[:, OWN * (chunk + at) : OWN * (chunk + at + 1), :] = (
+                part[:, LANES * at : LANES * (at + 1)].reshape(CHIPS, OWN, LANES).astype(BF16)
+            )
 
 
 def add_heads(parts, result):
@@ -246,20 +255,19 @@
     planes = lax.all_gather(weights, "gy", axis=0, tiled=False)
     own, planes = lax.optimization_barrier((own, planes))
     inner = lax.all_gather(planes[:, :WEIGHT_ROWS], "gx", axis=0, tiled=False, axis_index_groups=ONE_CHIP)
-    (rows,) = call(project_keyvalue, [((CHIPS, CORES * OWN, LANES), BF16)], (own, inner))
-    own, inner, planes, rows = lax.optimization_barrier((own, inner, planes, rows))
-    columns = lax.all_to_all(rows, "gx", 0, 0, tiled=True, axis_index_groups=SAME_CORE)
-    outer = lax.all_gather(planes[:, WEIGHT_ROWS:], "gx", axis=0, tiled=False, axis_index_groups=ONE_CHIP)
+    (rows,) = call(project_keyvalue, [((CHIPS * CORES, CORES * OWN, LANES), BF16)], (own, inner))
+    own, inner, planes, rows, length = lax.optimization_barrier((own, inner, planes, rows, cache_length))
+    keyvalue = lax.all_to_all(rows, "gx", 0, 0, tiled=True)
     keys = lax.all_gather(own[:, :PAGE], "gx", axis=0, tiled=False, axis_index_groups=ONE_CHIP)
     values = lax.all_gather(own[:, PAGE:KV_ROWS], "gx", axis=0, tiled=False, axis_index_groups=ONE_CHIP)
+    outer = lax.all_gather(planes[:, WEIGHT_ROWS:], "gx", axis=0, tiled=False, axis_index_groups=ONE_CHIP)
     queries, largest, total, summed = call(
         attend_cached,
         [((LANES, LANES), BF16)] + [((LANES, LANES), F32)] * 3,
-        (cache_length, own, inner, keys, values),
+        (length, own, inner, keys, values),
         scalars=1,
     )
-    columns, outer, summed = lax.optimization_barrier((columns, outer, summed))
-    keyvalue = lax.all_gather(columns, "gx", axis=0, tiled=False, axis_index_groups=ONE_CHIP)
+    keyvalue, outer, summed = lax.optimization_barrier((keyvalue, outer, summed))
     (parts,) = call(
         attend_new,
         [((CHIPS, LANES, LANES), BF16)],
@@ -270,7 +278,7 @@
     new_key, new_value = call(
         write_pages,
         [((PAGE, LANES), BF16), ((PAGE, LANES), BF16)],
-        (cache_length, place, keyvalue, key_cache[0], value_cache[0]),
+        (length, place, keyvalue, key_cache[0], value_cache[0]),
         scalars=2,
     )
     (out,) = call(add_heads, [((OWN, FEATURES), BF16)], (collected,))

time: 90.7 us -> 85.8 us (0.946)
  waiting for transfers between devices: 9.52 us -> 6.15 us
  blocking collectives: 50.1 us -> 47.9 us
    all_to_all x1, starting transfers between devices: 7.26 us -> 3.87 us  [body(): keyvalue = lax.all_to_all(rows, 'gx', 0, 0, tiled=True)]
    all_to_all x1, waiting for transfers between devices: 9.51 us -> 6.15 us  [body(): lax.all_to_all(parts, 'gx', 0, 0, tiled=True, axis_index_groups=SAME_CORE)]
    all_to_all x1, starting transfers between devices: 7.6 us -> 9.73 us  [body(): lax.all_to_all(send, 'gx', 0, 0, tiled=True, axis_index_groups=SAME_CORE)]
    all_gather x1 -> x0, blocking collectives: 1.93 us -> none  [body(): lax.all_gather(columns, 'gx', axis=0, tiled=False, axis_index_groups=ONE_...]
    all_to_all x1, starting transfers between devices: 6.93 us -> 8.82 us  [body(): lax.all_to_all(parts, 'gx', 0, 0, tiled=True, axis_index_groups=SAME_CORE)]
  transfers between devices with their start and end apart: 3 -> 3, of which waited for: 1 -> 1; matrix products, arithmetic and copies ran while one was open for 0% -> 0% of each run, Pallas kernels for 2% -> 3%
where the time goes in v7:
time: 85.8 us; the launch traced here: 85.3 us
  blocking collectives  47.9 us (56%)
  starting transfers between devices  22.4 us (26%)
  Pallas kernels  7.37 us (9%)
  waiting for transfers between devices  6.15 us (7%)
  between operations  1.35 us (2%)
    all_gather x1, blocking collectives, body(): planes = lax.all_gather(weights, 'gy', axis=0, tiled=False)  32.2 us
    all_to_all x1, starting transfers between devices, body(): lax.all_to_all(send, 'gx', 0, 0, tiled=True, axis_index_groups=SAME_CORE)  9.73 us
    all_gather x1, blocking collectives, body(): lax.all_gather(planes[:, :WEIGHT_ROWS], 'gx', axis=0, tiled=False, axis_i...  9.06 us
    all_to_all x1, starting transfers between devices, body(): lax.all_to_all(parts, 'gx', 0, 0, tiled=True, axis_index_groups=SAME_CORE)  8.82 us
    pallas_call x6, Pallas kernels, call(): pl.pallas_call(kernel, out_shape=[jax.ShapeDtypeStruct(shape, dtype) for...  7.37 us
    all_to_all x1, waiting for transfers between devices, body(): lax.all_to_all(parts, 'gx', 0, 0, tiled=True, axis_index_groups=SAME_CORE)  6.15 us
    all_to_all x1, starting transfers between devices, body(): keyvalue = lax.all_to_all(rows, 'gx', 0, 0, tiled=True)  3.87 us
    all_gather x1, blocking collectives, body(): lax.all_gather(own[:, PAGE:KV_ROWS], 'gx', axis=0, tiled=False, axis_inde...  2.23 us
  transfers between devices with their start and end apart: 3, of which 1 were waited for; matrix products, arithmetic and copies ran while one was open for 0% of the time, Pallas kernels for 3%

profile of v7, /device:TPU:1, one launch (start us, length us, event | category | flops | bytes accessed | tf_op | source)
XLA Modules:
  0.0 85.3 jit_solution(6213588749302586250)
XLA Ops:
  0.6 2.1 %shard_map.112 = (bf16[16,272,128]{2,1,0:T(8,128)(2,1)}, bf16[136,128]{1,0:T(8,128)(2,1)S(1)}) custom-call(bf16[8,2048]{1,0:T(8,128)(2,1)} %bitcast.28, f32[1,2048]{1,0:T(1,128)} %bitcast.30, f32[1,2048]{1,0:T(1,128)} %bitcast.31, bf16[64,128]{1,0:T(8,128)(2,1)} %bitcast.29, bf16[8,128]{1,0:T(8,128)(2,1)} %bitcast.32, bf16[64,128]{1,0:T(8,128)(2,1)} %out_w.1, ...), custom_call_target="tpu_custom_call" | custom-call | tf_op jit(solution)/shard_map/pallas_call | solution.py:210
  2.8 9.7 %all-to-all-start = ((bf16[16,272,128]{2,1,0:T(8,128)(2,1)}), bf16[16,272,128]{2,1,0:T(8,128)(2,1)S(1)}, u32[]{:S(2)}, u32[]{:S(2)}) async-start(bf16[16,272,128]{2,1,0:T(8,128)(2,1)} %get-tuple-element.21), calls=%async_computation | async-start | bytes 2228224 | tf_op jit(solution)/shard_map/all_to_all | solution.py:254
  13.2 32.2 %all-gather = bf16[2176,128]{1,0:T(8,128)(2,1)S(1)} all-gather(bf16[136,128]{1,0:T(8,128)(2,1)S(1)} %get-tuple-element.22), channel_id=2, replica_groups=mesh['gx'=32,'gy'=16] {'gy'}, dimensions={0}, use_global_device_ids=true | all-gather | bytes 591872 | tf_op jit(solution)/shard_map/all_gather | solution.py:255
  45.4 0.0 all-to-all-done.tokens.own
  45.4 9.1 %all-gather.1 = bf16[32,72,128]{2,1,0:T(8,128)(2,1)S(1)} all-gather(bf16[16,72,128]{2,1,0:T(8,128)(2,1)S(1)} %slice.12), channel_id=3, replica_groups={{0,16},{32,48},{64,80},{96,112},{128,144},{160,176},{192,208},{224,240}..., dimensions={0}, use_global_device_ids=true | all-gather | bytes 884736 | tf_op jit(solution)/shard_map/all_gather | solution.py:257
  54.5 0.9 %shard_map.113 = bf16[32,16,128]{2,1,0:T(8,128)(2,1)} custom-call(bf16[16,272,128]{2,1,0:T(8,128)(2,1)S(1)} %all-to-all-done.tokens.own, bf16[2,16,72,128]{3,2,1,0:T(8,128)(2,1)S(1)} %bitcast.16), custom_call_target="tpu_custom_call" | custom-call | tf_op jit(solution)/shard_map/pallas_call | solution.py:210
  55.4 3.9 %all-to-all-start.1 = ((bf16[32,16,128]{2,1,0:T(8,128)(2,1)}), bf16[32,16,128]{2,1,0:T(8,128)(2,1)S(1)}, u32[]{:S(2)}, u32[]{:S(2)}) async-start(bf16[32,16,128]{2,1,0:T(8,128)(2,1)} %shard_map.113), calls=%async_computation.1 | async-start | bytes 262144 | tf_op jit(solution)/shard_map/all_to_all | solution.py:260
  59.3 2.2 %all-gather.3 = bf16[32,72,128]{2,1,0:T(8,128)(2,1)S(1)} all-gather(bf16[16,72,128]{2,1,0:T(8,128)(2,1)S(1)} %get-tuple-element.39), channel_id=5, replica_groups={{0,16},{32,48},{64,80},{96,112},{128,144},{160,176},{192,208},{224,240}..., dimensions={0}, use_global_device_ids=true | all-gather | bytes 884736 | tf_op jit(solution)/shard_map/all_gather | solution.py:262
  61.6 2.2 %all-gather.2 = bf16[32,72,128]{2,1,0:T(8,128)(2,1)S(1)} all-gather(bf16[16,72,128]{2,1,0:T(8,128)(2,1)S(1)} %get-tuple-element.40), channel_id=4, replica_groups={{0,16},{32,48},{64,80},{96,112},{128,144},{160,176},{192,208},{224,240}..., dimensions={0}, use_global_device_ids=true | all-gather | bytes 884736 | tf_op jit(solution)/shard_map/all_gather | solution.py:261
  63.8 1.3 %shard_map.114 = (bf16[128,128]{1,0:T(8,128)(2,1)S(1)}, f32[128,128]{1,0:T(8,128)S(1)}, f32[128,128]{1,0:T(8,128)S(1)}, f32[128,128]{1,0:T(8,128)S(1)}) custom-call(s32[1]{0:T(128)S(6)} %copy.12.length_ref, bf16[16,272,128]{2,1,0:T(8,128)(2,1)S(1)} %all-to-all-done.tokens.own, bf16[2,16,72,128]{3,2,1,0:T(8,128)(2,1)S(1)} %bitcast.17, ...), custom_call_target="tpu_custom_call" | custom-call | tf_op jit(solution)/shard_map/pallas_call | solution.py:210
  65.1 2.2 %all-gather.4 = bf16[32,64,128]{2,1,0:T(8,128)(2,1)S(1)} all-gather(bf16[16,64,128]{2,1,0:T(8,128)(2,1)S(1)} %slice.15), channel_id=6, replica_groups={{0,16},{32,48},{64,80},{96,112},{128,144},{160,176},{192,208},{224,240}..., dimensions={0}, use_global_device_ids=true | all-gather | bytes 786432 | tf_op jit(solution)/shard_map/all_gather | solution.py:263
  67.3 0.0 all-to-all-done.1.keyvalue
  67.3 0.0 copy-start
  67.3 0.0 copy-start.1
  67.3 1.5 %shard_map.115 = bf16[16,128,128]{2,1,0:T(8,128)(2,1)} custom-call(s32[1]{0:T(128)S(6)} %and.4.core_ref, bf16[128,128]{1,0:T(8,128)(2,1)S(1)} %get-tuple-element.28.queries, f32[128,128]{1,0:T(8,128)S(1)} %get-tuple-element.29.old_largest, f32[128,128]{1,0:T(8,128)S(1)} %get-tuple-element.30.old_total, f32[128,128]{1,0:T(8,128)S(1)} %get-tuple-element.34.old_summed, ...), custom_call_target="tpu_custom_call" | custom-call | tf_op jit(solution)/shard_map/pallas_call | solution.py:210
  68.8 8.8 %all-to-all-start.2 = ((bf16[16,128,128]{2,1,0:T(8,128)(2,1)}), bf16[16,128,128]{2,1,0:T(8,128)(2,1)S(1)}, u32[]{:S(2)}, u32[]{:S(2)}) async-start(bf16[16,128,128]{2,1,0:T(8,128)(2,1)} %shard_map.115), calls=%async_computation.2 | async-start | bytes 1048576 | tf_op jit(solution)/shard_map/all_to_all | solution.py:277
  77.6 0.0 copy-done
  77.6 0.0 copy-done.1
  77.6 0.8 shard_map.117
  78.5 6.1 %all-to-all-done.2.parts = bf16[16,128,128]{2,1,0:T(8,128)(2,1)S(1)} async-done(((bf16[16,128,128]{2,1,0:T(8,128)(2,1)}), bf16[16,128,128]{2,1,0:T(8,128)(2,1)S(1)}, u32[]{:S(2)}, u32[]{:S(2)}) %all-to-all-start.2) | async-done | bytes 524320 | tf_op jit(solution)/shard_map/all_to_all | solution.py:277
  84.6 0.7 shard_map.116
  (3 shorter events, 0.1 us)
Async XLA Ops:
  2.8 42.6 %all-to-all-start = ((bf16[16,272,128]{2,1,0:T(8,128)(2,1)}), bf16[16,272,128]{2,1,0:T(8,128)(2,1)S(1)}, u32[]{:S(2)}, u32[]{:S(2)}) async-start(bf16[16,272,128]{2,1,0:T(8,128)(2,1)} %get-tuple-element.21), calls=%async_computation | async-start | bytes 2228224 | tf_op jit(solution)/shard_map/all_to_all | solution.py:254
  55.4 11.9 %all-to-all-start.1 = ((bf16[32,16,128]{2,1,0:T(8,128)(2,1)}), bf16[32,16,128]{2,1,0:T(8,128)(2,1)S(1)}, u32[]{:S(2)}, u32[]{:S(2)}) async-start(bf16[32,16,128]{2,1,0:T(8,128)(2,1)} %shard_map.113), calls=%async_computation.1 | async-start | bytes 262144 | tf_op jit(solution)/shard_map/all_to_all | solution.py:260
  67.3 10.3 %copy-start = (bf16[1,72,128]{2,1,0:T(8,128)(2,1)S(1)}, bf16[1,72,128]{2,1,0:T(8,128)(2,1)}, u32[]{:S(2)}) copy-start(bf16[1,72,128]{2,1,0:T(8,128)(2,1)} %param.15) | copy-start | bytes 55300
  67.3 10.3 %copy-start.1 = (bf16[1,72,128]{2,1,0:T(8,128)(2,1)S(1)}, bf16[1,72,128]{2,1,0:T(8,128)(2,1)}, u32[]{:S(2)}) copy-start(bf16[1,72,128]{2,1,0:T(8,128)(2,1)} %param.16) | copy-start | bytes 55300
  68.8 15.8 %all-to-all-start.2 = ((bf16[16,128,128]{2,1,0:T(8,128)(2,1)}), bf16[16,128,128]{2,1,0:T(8,128)(2,1)S(1)}, u32[]{:S(2)}, u32[]{:S(2)}) async-start(bf16[16,128,128]{2,1,0:T(8,128)(2,1)} %shard_map.115), calls=%async_computation.2 | async-start | bytes 1048576 | tf_op jit(solution)/shard_map/all_to_all | solution.py:277

commit v8 on v7

--- a/solution.py
+++ b/solution.py
@@ -21,6 +21,11 @@
 
 FIRST = 10
 SAME_CORE = [[CORES * ((at + FIRST) % CHIPS) + core for at in range(CHIPS)] for core in range(CORES)]
+COLUMNS = [
+    [(CORES * chip + (odd + plane) % CORES) * CHUNKS + plane for plane in reversed(range(CHUNKS))]
+    for chip in range(CHIPS)
+    for odd in range(CORES)
+]
 ONE_CHIP = [[CORES * chip + core for core in range(CORES)] for chip in range(CHIPS)]
 SWAP = [(place, place ^ 1) for place in range(CHIPS * CORES)]
 
@@ -72,6 +77,11 @@
             ]
 
 
+def part_of(gathered, odd, core, chunk):
+    side = odd if (core + chunk) % CORES == 0 else 1 - odd
+    return gathered.at[side, CHUNKS - 1 - chunk]
+
+
 def gathered_tokens(tokens):
     pieces = []
     for chunk in range(CHUNKS):
@@ -80,10 +90,13 @@
     return jnp.concatenate(pieces, axis=1)
 
 
-def project_keyvalue(tokens, weights, keyvalue):
+def project_keyvalue(odd_ref, tokens, weights, keyvalue):
+    odd = odd_ref[0]
     narrow = jnp.concatenate(
         [
-            jnp.concatenate([weights[core, chunk, HALF:WEIGHT_ROWS, :].astype(F32) for core in range(CORES)], axis=0)
+            jnp.concatenate(
+                [part_of(weights, odd, core, chunk)[HALF:WEIGHT_ROWS, :].astype(F32) for core in range(CORES)], axis=0
+            )
             for chunk in range(CHUNKS)
         ],
         axis=1,
@@ -93,10 +106,10 @@
         keyvalue[place] = rounded
 
 
-def project_queries(tokens, weights):
+def project_queries(odd, tokens, weights):
     square = jnp.concatenate(
         [
-            jnp.concatenate([weights[core, chunk, 0:HALF, :] for core in range(CORES)], axis=0)
+            jnp.concatenate([part_of(weights, odd, core, chunk)[0:HALF, :] for core in range(CORES)], axis=0)
             for chunk in range(CHUNKS)
         ],
         axis=1,
@@ -113,10 +126,10 @@
     return (chip << 4) + OWN * core + (index & 7)
 
 
-def attend_cached(length_ref, own, weights, keys, values, queries, largest_out, total_out, summed_out):
+def attend_cached(length_ref, odd_ref, own, weights, keys, values, queries, largest_out, total_out, summed_out):
     length = length_ref[0]
     scale = float(LANES) ** (-0.5)
-    query_rows = project_queries(own, weights)
+    query_rows = project_queries(odd_ref[0], own, weights)
     queries[...] = query_rows
     places = CHIPS * PAGE
     lane = iota((1, places), 1)
@@ -144,7 +157,7 @@
     summed_out[...] = summed
 
 
-def attend_new(core_ref, queries, old_largest, old_total, old_summed, keyvalue, out_w, result):
+def attend_new(core_ref, odd_ref, queries, old_largest, old_total, old_summed, keyvalue, out_w, result):
     core = core_ref[0]
     scale = float(LANES) ** (-0.5)
     query_rows = queries[...]
@@ -162,9 +175,14 @@
     for side in range(CORES):
         summed = summed + dot_nt(terms[side].astype(BF16), new_columns(keyvalue, side, CHIPS // 2))
     attended = (summed / total).astype(BF16)
+    odd = odd_ref[0]
     for chunk in range(0, CHUNKS, 2):
         wide = jnp.concatenate(
-            [jnp.concatenate([out_w[0, at], out_w[1, at]], axis=0) for at in (chunk, chunk + 1)], axis=1
+            [
+                jnp.concatenate([part_of(out_w, odd, half, at)[...] for half in range(CORES)], axis=0)
+                for at in (chunk, chunk + 1)
+            ],
+            axis=1,
         )
         part = dot(attended, wide)
         for at in range(2):
@@ -230,6 +248,7 @@
 ):
     place = lax.axis_index("gx").astype(jnp.int32).reshape(1)
     core = place & 1
+    odd = lax.axis_index("gy").astype(jnp.int32).reshape(1) & 1
     send, weights = call(
         prepare,
         [((CHIPS, SEND_ROWS, LANES), BF16), ((WEIGHT_ROWS + HALF, LANES), BF16)],
@@ -252,10 +271,10 @@
         ],
     )
     own = lax.all_to_all(send, "gx", 0, 0, tiled=True, axis_index_groups=SAME_CORE)
-    planes = lax.all_gather(weights, "gy", axis=0, tiled=False)
+    planes = lax.all_gather(weights, ("gx", "gy"), axis=0, tiled=False, axis_index_groups=COLUMNS)
     own, planes = lax.optimization_barrier((own, planes))
     inner = lax.all_gather(planes[:, :WEIGHT_ROWS], "gx", axis=0, tiled=False, axis_index_groups=ONE_CHIP)
-    (rows,) = call(project_keyvalue, [((CHIPS * CORES, CORES * OWN, LANES), BF16)], (own, inner))
+    (rows,) = call(project_keyvalue, [((CHIPS * CORES, CORES * OWN, LANES), BF16)], (odd, own, inner), scalars=1)
     own, inner, planes, rows, length = lax.optimization_barrier((own, inner, planes, rows, cache_length))
     keyvalue = lax.all_to_all(rows, "gx", 0, 0, tiled=True)
     keys = lax.all_gather(own[:, :PAGE], "gx", axis=0, tiled=False, axis_index_groups=ONE_CHIP)
@@ -264,15 +283,15 @@
     queries, largest, total, summed = call(
         attend_cached,
         [((LANES, LANES), BF16)] + [((LANES, LANES), F32)] * 3,
-        (length, own, inner, keys, values),
-        scalars=1,
+        (length, odd, own, inner, keys, values),
+        scalars=2,
     )
     keyvalue, outer, summed = lax.optimization_barrier((keyvalue, outer, summed))
     (parts,) = call(
         attend_new,
         [((CHIPS, LANES, LANES), BF16)],
-        (core, queries, largest, total, summed, keyvalue, outer),
-        scalars=1,
+        (core, odd, queries, largest, total, summed, keyvalue, outer),
+        scalars=2,
     )
     collected = lax.all_to_all(parts, "gx", 0, 0, tiled=True, axis_index_groups=SAME_CORE)
     new_key, new_value = call(

time: 85.8 us -> 81.3 us (0.948)
  blocking collectives: 47.9 us -> 43.6 us
    all_gather x1, blocking collectives: 9.06 us -> 2.23 us  [body(): lax.all_gather(planes[:, :WEIGHT_ROWS], 'gx', axis=0, tiled=False, axis_i...]
    all_gather x1, blocking collectives: 32.2 us -> 34.8 us  [body(): lax.all_gather(weights, ('gx', 'gy'), axis=0, tiled=False, axis_index_gro...]
where the time goes in v8:
time: 81.3 us; the launch traced here: 80.8 us
  blocking collectives  43.6 us (54%)
  starting transfers between devices  22.2 us (27%)
  Pallas kernels  7.39 us (9%)
  waiting for transfers between devices  6.15 us (8%)
  between operations  1.35 us (2%)
    all_gather x1, blocking collectives, body(): lax.all_gather(weights, ('gx', 'gy'), axis=0, tiled=False, axis_index_gro...  34.8 us
    all_to_all x1, starting transfers between devices, body(): lax.all_to_all(send, 'gx', 0, 0, tiled=True, axis_index_groups=SAME_CORE)  9.73 us
    all_to_all x1, starting transfers between devices, body(): lax.all_to_all(parts, 'gx', 0, 0, tiled=True, axis_index_groups=SAME_CORE)  8.83 us
    pallas_call x6, Pallas kernels, call(): pl.pallas_call(kernel, out_shape=[jax.ShapeDtypeStruct(shape, dtype) for...  7.39 us
    all_to_all x1, waiting for transfers between devices, body(): lax.all_to_all(parts, 'gx', 0, 0, tiled=True, axis_index_groups=SAME_CORE)  6.15 us
    all_to_all x1, starting transfers between devices, body(): keyvalue = lax.all_to_all(rows, 'gx', 0, 0, tiled=True)  3.65 us
    all_gather x1, blocking collectives, body(): lax.all_gather(planes[:, :WEIGHT_ROWS], 'gx', axis=0, tiled=False, axis_i...  2.23 us
    all_gather x1, blocking collectives, body(): lax.all_gather(own[:, PAGE:KV_ROWS], 'gx', axis=0, tiled=False, axis_inde...  2.23 us
  transfers between devices with their start and end apart: 3, of which 1 were waited for; matrix products, arithmetic and copies ran while one was open for 0% of the time, Pallas kernels for 3%

profile of v8, /device:TPU:1, one launch (start us, length us, event | category | flops | bytes accessed | tf_op | source)
XLA Modules:
  0.0 80.8 jit_solution(12649911967990724321)
XLA Ops:
  0.6 2.1 %shard_map.112 = (bf16[16,272,128]{2,1,0:T(8,128)(2,1)}, bf16[136,128]{1,0:T(8,128)(2,1)S(1)}) custom-call(bf16[8,2048]{1,0:T(8,128)(2,1)} %bitcast.29, f32[1,2048]{1,0:T(1,128)} %bitcast.31, f32[1,2048]{1,0:T(1,128)} %bitcast.32, bf16[64,128]{1,0:T(8,128)(2,1)} %bitcast.30, bf16[8,128]{1,0:T(8,128)(2,1)} %bitcast.33, bf16[64,128]{1,0:T(8,128)(2,1)} %out_w.1, ...), custom_call_target="tpu_custom_call" | custom-call | tf_op jit(solution)/shard_map/pallas_call | solution.py:228
  2.8 9.7 %all-to-all-start = ((bf16[16,272,128]{2,1,0:T(8,128)(2,1)}), bf16[16,272,128]{2,1,0:T(8,128)(2,1)S(1)}, u32[]{:S(2)}, u32[]{:S(2)}) async-start(bf16[16,272,128]{2,1,0:T(8,128)(2,1)} %get-tuple-element.21), calls=%async_computation | async-start | bytes 2228224 | tf_op jit(solution)/shard_map/all_to_all | solution.py:273
  13.2 34.8 %all-gather = bf16[2176,128]{1,0:T(8,128)(2,1)S(1)} all-gather(bf16[136,128]{1,0:T(8,128)(2,1)S(1)} %get-tuple-element.22), channel_id=2, replica_groups={{31,14,29,12,27,10,25,8,23,6,21,4,19,2,17,0},{15,30,13,28,11,26,9,24,7,..., dimensions={0}, use_global_device_ids=true | all-gather | bytes 591872 | tf_op jit(solution)/shard_map/all_gather | solution.py:274
  48.0 0.0 all-to-all-done.tokens.own
  48.0 2.2 %all-gather.1 = bf16[32,72,128]{2,1,0:T(8,128)(2,1)S(1)} all-gather(bf16[16,72,128]{2,1,0:T(8,128)(2,1)S(1)} %slice.12), channel_id=3, replica_groups={{0,16},{32,48},{64,80},{96,112},{128,144},{160,176},{192,208},{224,240}..., dimensions={0}, use_global_device_ids=true | all-gather | bytes 884736 | tf_op jit(solution)/shard_map/all_gather | solution.py:276
  50.2 0.9 %shard_map.113 = bf16[32,16,128]{2,1,0:T(8,128)(2,1)} custom-call(s32[1]{0:T(128)} %bitcast.1.odd_ref, bf16[16,272,128]{2,1,0:T(8,128)(2,1)S(1)} %all-to-all-done.tokens.own, bf16[2,16,72,128]{3,2,1,0:T(8,128)(2,1)S(1)} %bitcast.17), custom_call_target="tpu_custom_call" | custom-call | tf_op jit(solution)/shard_map/pallas_call | solution.py:228
  51.1 3.6 %all-to-all-start.1 = ((bf16[32,16,128]{2,1,0:T(8,128)(2,1)}), bf16[32,16,128]{2,1,0:T(8,128)(2,1)S(1)}, u32[]{:S(2)}, u32[]{:S(2)}) async-start(bf16[32,16,128]{2,1,0:T(8,128)(2,1)} %shard_map.113), calls=%async_computation.1 | async-start | bytes 262144 | tf_op jit(solution)/shard_map/all_to_all | solution.py:279
  54.9 2.2 %all-gather.3 = bf16[32,72,128]{2,1,0:T(8,128)(2,1)S(1)} all-gather(bf16[16,72,128]{2,1,0:T(8,128)(2,1)S(1)} %get-tuple-element.39), channel_id=5, replica_groups={{0,16},{32,48},{64,80},{96,112},{128,144},{160,176},{192,208},{224,240}..., dimensions={0}, use_global_device_ids=true | all-gather | bytes 884736 | tf_op jit(solution)/shard_map/all_gather | solution.py:281
  57.1 2.2 %all-gather.2 = bf16[32,72,128]{2,1,0:T(8,128)(2,1)S(1)} all-gather(bf16[16,72,128]{2,1,0:T(8,128)(2,1)S(1)} %get-tuple-element.40), channel_id=4, replica_groups={{0,16},{32,48},{64,80},{96,112},{128,144},{160,176},{192,208},{224,240}..., dimensions={0}, use_global_device_ids=true | all-gather | bytes 884736 | tf_op jit(solution)/shard_map/all_gather | solution.py:280
  59.3 1.4 %shard_map.114 = (bf16[128,128]{1,0:T(8,128)(2,1)S(1)}, f32[128,128]{1,0:T(8,128)S(1)}, f32[128,128]{1,0:T(8,128)S(1)}, f32[128,128]{1,0:T(8,128)S(1)}) custom-call(s32[1]{0:T(128)S(6)} %copy.12.length_ref, s32[1]{0:T(128)} %bitcast.1.odd_ref, bf16[16,272,128]{2,1,0:T(8,128)(2,1)S(1)} %all-to-all-done.tokens.own, bf16[2,16,72,128]{3,2,1,0:T(8,128)(2,1)S(1)} %bitcast.18, ...), custom_call_target="tpu_custom_call" | custom-call | tf_op jit(solution)/shard_map/pallas_call | solution.py:228
  60.7 2.2 %all-gather.4 = bf16[32,64,128]{2,1,0:T(8,128)(2,1)S(1)} all-gather(bf16[16,64,128]{2,1,0:T(8,128)(2,1)S(1)} %slice.15), channel_id=6, replica_groups={{0,16},{32,48},{64,80},{96,112},{128,144},{160,176},{192,208},{224,240}..., dimensions={0}, use_global_device_ids=true | all-gather | bytes 786432 | tf_op jit(solution)/shard_map/all_gather | solution.py:282
  62.9 0.0 all-to-all-done.1.keyvalue
  62.9 0.0 copy-start
  62.9 0.0 copy-start.1
  62.9 1.5 %shard_map.115 = bf16[16,128,128]{2,1,0:T(8,128)(2,1)} custom-call(s32[1]{0:T(128)S(6)} %and.10.core_ref, s32[1]{0:T(128)} %bitcast.1.odd_ref, bf16[128,128]{1,0:T(8,128)(2,1)S(1)} %get-tuple-element.28.queries, f32[128,128]{1,0:T(8,128)S(1)} %get-tuple-element.29.old_largest, f32[128,128]{1,0:T(8,128)S(1)} %get-tuple-element.30.old_total, ...), custom_call_target="tpu_custom_call" | custom-call | tf_op jit(solution)/shard_map/pallas_call | solution.py:228
  64.3 8.8 %all-to-all-start.2 = ((bf16[16,128,128]{2,1,0:T(8,128)(2,1)}), bf16[16,128,128]{2,1,0:T(8,128)(2,1)S(1)}, u32[]{:S(2)}, u32[]{:S(2)}) async-start(bf16[16,128,128]{2,1,0:T(8,128)(2,1)} %shard_map.115), calls=%async_computation.2 | async-start | bytes 1048576 | tf_op jit(solution)/shard_map/all_to_all | solution.py:296
  73.2 0.0 copy-done
  73.2 0.0 copy-done.1
  73.2 0.8 %shard_map.117 = (bf16[72,128]{1,0:T(8,128)(2,1)}, bf16[72,128]{1,0:T(8,128)(2,1)}) custom-call(s32[1]{0:T(128)S(6)} %copy.12.length_ref, s32[1]{0:T(128)} %bitcast.place_ref, bf16[32,16,128]{2,1,0:T(8,128)(2,1)S(1)} %all-to-all-done.1.keyvalue, bf16[72,128]{1,0:T(8,128)(2,1)S(1)} %bitcast.23, bf16[72,128]{1,0:T(8,128)(2,1)S(1)} %bitcast.25), custom_call_target="tpu_custom_call" | custom-call | tf_op jit(solution)/shard_map/pallas_call | solution.py:228
  74.0 6.1 %all-to-all-done.2.parts = bf16[16,128,128]{2,1,0:T(8,128)(2,1)S(1)} async-done(((bf16[16,128,128]{2,1,0:T(8,128)(2,1)}), bf16[16,128,128]{2,1,0:T(8,128)(2,1)S(1)}, u32[]{:S(2)}, u32[]{:S(2)}) %all-to-all-start.2) | async-done | bytes 524320 | tf_op jit(solution)/shard_map/all_to_all | solution.py:296
  80.2 0.7 shard_map.116
  (3 shorter events, 0.1 us)
Async XLA Ops:
  2.8 45.2 %all-to-all-start = ((bf16[16,272,128]{2,1,0:T(8,128)(2,1)}), bf16[16,272,128]{2,1,0:T(8,128)(2,1)S(1)}, u32[]{:S(2)}, u32[]{:S(2)}) async-start(bf16[16,272,128]{2,1,0:T(8,128)(2,1)} %get-tuple-element.21), calls=%async_computation | async-start | bytes 2228224 | tf_op jit(solution)/shard_map/all_to_all | solution.py:273
  51.1 11.7 %all-to-all-start.1 = ((bf16[32,16,128]{2,1,0:T(8,128)(2,1)}), bf16[32,16,128]{2,1,0:T(8,128)(2,1)S(1)}, u32[]{:S(2)}, u32[]{:S(2)}) async-start(bf16[32,16,128]{2,1,0:T(8,128)(2,1)} %shard_map.113), calls=%async_computation.1 | async-start | bytes 262144 | tf_op jit(solution)/shard_map/all_to_all | solution.py:279
  62.9 10.3 %copy-start = (bf16[1,72,128]{2,1,0:T(8,128)(2,1)S(1)}, bf16[1,72,128]{2,1,0:T(8,128)(2,1)}, u32[]{:S(2)}) copy-start(bf16[1,72,128]{2,1,0:T(8,128)(2,1)} %param.15) | copy-start | bytes 55300
  62.9 10.3 %copy-start.1 = (bf16[1,72,128]{2,1,0:T(8,128)(2,1)S(1)}, bf16[1,72,128]{2,1,0:T(8,128)(2,1)}, u32[]{:S(2)}) copy-start(bf16[1,72,128]{2,1,0:T(8,128)(2,1)} %param.16) | copy-start | bytes 55300
  64.3 15.8 %all-to-all-start.2 = ((bf16[16,128,128]{2,1,0:T(8,128)(2,1)}), bf16[16,128,128]{2,1,0:T(8,128)(2,1)S(1)}, u32[]{:S(2)}, u32[]{:S(2)}) async-start(bf16[16,128,128]{2,1,0:T(8,128)(2,1)} %shard_map.115), calls=%async_computation.2 | async-start | bytes 1048576 | tf_op jit(solution)/shard_map/all_to_all | solution.py:296

commit v9 on v8

--- a/solution.py
+++ b/solution.py
@@ -90,7 +90,7 @@
     return jnp.concatenate(pieces, axis=1)
 
 
-def project_keyvalue(odd_ref, tokens, weights, keyvalue):
+def project_keyvalue(odd_ref, tokens, weights, planes, keyvalue, swapped):
     odd = odd_ref[0]
     narrow = jnp.concatenate(
         [
@@ -104,6 +104,8 @@
     rounded = dot_nt(narrow, gathered_tokens(tokens)).astype(BF16)
     for place in range(CHIPS * CORES):
         keyvalue[place] = rounded
+    swapped[:, 0:KV_ROWS, :] = tokens[:, 0:KV_ROWS, :]
+    swapped[:, KV_ROWS : KV_ROWS + HALF, :] = planes[:, WEIGHT_ROWS : WEIGHT_ROWS + HALF, :]
 
 
 def project_queries(odd, tokens, weights):
@@ -126,8 +128,11 @@
     return (chip << 4) + OWN * core + (index & 7)
 
 
-def attend_cached(length_ref, odd_ref, own, weights, keys, values, queries, largest_out, total_out, summed_out):
+def attend_cached(
+    length_ref, odd_ref, core_ref, own, weights, peer, queries, largest_out, total_out, summed_out
+):
     length = length_ref[0]
+    core = core_ref[0]
     scale = float(LANES) ** (-0.5)
     query_rows = project_queries(odd_ref[0], own, weights)
     queries[...] = query_rows
@@ -138,9 +143,9 @@
     start = lane - PAGE * at + KV_ROWS * chip
     scored = []
     value_sets = []
-    for side in range(CORES):
-        key_rows = keys[side].astype(F32).reshape(places, LANES).astype(BF16)
-        value_sets.append(values[side].astype(F32).reshape(places, LANES).astype(BF16))
+    for source, side in ((own, core), (peer, 1 - core)):
+        key_rows = source[:, 0:PAGE, :].astype(F32).reshape(places, LANES).astype(BF16)
+        value_sets.append(source[:, PAGE:KV_ROWS, :].astype(F32).reshape(places, LANES).astype(BF16))
         scores = dot_nt(query_rows, key_rows) * scale
         scored.append(jnp.where(start + PAGE * side < length, scores, NEGATIVE))
     largest = jnp.maximum(
@@ -157,7 +162,7 @@
     summed_out[...] = summed
 
 
-def attend_new(core_ref, odd_ref, queries, old_largest, old_total, old_summed, keyvalue, out_w, result):
+def attend_new(core_ref, odd_ref, queries, old_largest, old_total, old_summed, keyvalue, planes, peer, result):
     core = core_ref[0]
     scale = float(LANES) ** (-0.5)
     query_rows = queries[...]
@@ -174,21 +179,17 @@
     summed = old_summed[...] * factor
     for side in range(CORES):
         summed = summed + dot_nt(terms[side].astype(BF16), new_columns(keyvalue, side, CHIPS // 2))
-    attended = (summed / total).astype(BF16)
-    odd = odd_ref[0]
-    for chunk in range(0, CHUNKS, 2):
-        wide = jnp.concatenate(
-            [
-                jnp.concatenate([part_of(out_w, odd, half, at)[...] for half in range(CORES)], axis=0)
-                for at in (chunk, chunk + 1)
-            ],
-            axis=1,
+    attended = summed / total
+    turned = pltpu.roll(attended, HALF, 1)
+    same = (core + odd_ref[0]) % CORES == 0
+    sides = (jnp.where(same, attended, turned).astype(BF16), jnp.where(same, turned, attended).astype(BF16))
+    for chunk in range(CHUNKS):
+        at = CHUNKS - 1 - chunk
+        square = jnp.concatenate(
+            [planes[at, WEIGHT_ROWS : WEIGHT_ROWS + HALF, :], peer[at, KV_ROWS : KV_ROWS + HALF, :]], axis=0
         )
-        part = dot(attended, wide)
-        for at in range(2):
-            result[:, OWN * (chunk + at) : OWN * (chunk + at + 1), :] = (
-                part[:, LANES * at : LANES * (at + 1)].reshape(CHIPS, OWN, LANES).astype(BF16)
-            )
+        part = dot(sides[chunk % 2], square)
+        result[:, OWN * chunk : OWN * (chunk + 1), :] = part.reshape(CHIPS, OWN, LANES).astype(BF16)
 
 
 def add_heads(parts, result):
@@ -274,30 +275,31 @@
     planes = lax.all_gather(weights, ("gx", "gy"), axis=0, tiled=False, axis_index_groups=COLUMNS)
     own, planes = lax.optimization_barrier((own, planes))
     inner = lax.all_gather(planes[:, :WEIGHT_ROWS], "gx", axis=0, tiled=False, axis_index_groups=ONE_CHIP)
-    (rows,) = call(project_keyvalue, [((CHIPS * CORES, CORES * OWN, LANES), BF16)], (odd, own, inner), scalars=1)
-    own, inner, planes, rows, length = lax.optimization_barrier((own, inner, planes, rows, cache_length))
+    rows, swapped = call(
+        project_keyvalue,
+        [((CHIPS * CORES, CORES * OWN, LANES), BF16), ((CHIPS, KV_ROWS + HALF, LANES), BF16)],
+        (odd, own, inner, planes),
+        scalars=1,
+    )
     keyvalue = lax.all_to_all(rows, "gx", 0, 0, tiled=True)
-    keys = lax.all_gather(own[:, :PAGE], "gx", axis=0, tiled=False, axis_index_groups=ONE_CHIP)
-    values = lax.all_gather(own[:, PAGE:KV_ROWS], "gx", axis=0, tiled=False, axis_index_groups=ONE_CHIP)
-    outer = lax.all_gather(planes[:, WEIGHT_ROWS:], "gx", axis=0, tiled=False, axis_index_groups=ONE_CHIP)
+    peer = lax.ppermute(swapped, "gx", SWAP)
     queries, largest, total, summed = call(
         attend_cached,
         [((LANES, LANES), BF16)] + [((LANES, LANES), F32)] * 3,
-        (length, odd, own, inner, keys, values),
-        scalars=2,
-    )
-    keyvalue, outer, summed = lax.optimization_barrier((keyvalue, outer, summed))
+        (cache_length, odd, core, own, inner, peer),
+        scalars=3,
+    )
     (parts,) = call(
         attend_new,
         [((CHIPS, LANES, LANES), BF16)],
-        (core, odd, queries, largest, total, summed, keyvalue, outer),
+        (core, odd, queries, largest, total, summed, keyvalue, planes, peer),
         scalars=2,
     )
     collected = lax.all_to_all(parts, "gx", 0, 0, tiled=True, axis_index_groups=SAME_CORE)
     new_key, new_value = call(
         write_pages,
         [((PAGE, LANES), BF16), ((PAGE, LANES), BF16)],
-        (length, place, keyvalue, key_cache[0], value_cache[0]),
+        (cache_length, place, keyvalue, key_cache[0], value_cache[0]),
         scalars=2,
     )
     (out,) = call(add_heads, [((OWN, FEATURES), BF16)], (collected,))

time: 81.3 us -> 80.7 us (level)
  blocking collectives: 43.6 us -> 37 us
  waiting for transfers between devices: 6.15 us -> 11.9 us
    all_gather x3 -> x0, blocking collectives: 6.63 us -> none  [the longest x1 2.23 us: body(): lax.all_gather(own[:, PAGE:KV_ROWS], 'gx', axis=0, tiled=False, axis_inde...]
    all_to_all x1, waiting for transfers between devices: 0.01 us -> 5.79 us  [body(): keyvalue = lax.all_to_all(rows, 'gx', 0, 0, tiled=True)]
    all_to_all x1, starting transfers between devices: 8.83 us -> 6.66 us  [body(): lax.all_to_all(parts, 'gx', 0, 0, tiled=True, axis_index_groups=SAME_CORE)]
    ppermute x0 -> x1, starting transfers between devices: none -> 2.05 us  [body(): peer = lax.ppermute(swapped, 'gx', SWAP)]
  transfers between devices with their start and end apart: 3 -> 4, of which waited for: 1 -> 2; matrix products, arithmetic and copies ran while one was open for 0% -> 0% of each run, Pallas kernels for 3% -> 3%
where the time goes in v9:
time: 80.7 us; the launch traced here: 80.3 us
  blocking collectives  37 us (46%)
  starting transfers between devices  22.3 us (28%)
  waiting for transfers between devices  11.9 us (15%)
  Pallas kernels  7.66 us (9%)
  between operations  1.34 us (2%)
    all_gather x1, blocking collectives, body(): lax.all_gather(weights, ('gx', 'gy'), axis=0, tiled=False, axis_index_gro...  34.8 us
    all_to_all x1, starting transfers between devices, body(): lax.all_to_all(send, 'gx', 0, 0, tiled=True, axis_index_groups=SAME_CORE)  9.73 us
    pallas_call x6, Pallas kernels, call(): pl.pallas_call(kernel, out_shape=[jax.ShapeDtypeStruct(shape, dtype) for...  7.66 us
    all_to_all x1, starting transfers between devices, body(): lax.all_to_all(parts, 'gx', 0, 0, tiled=True, axis_index_groups=SAME_CORE)  6.66 us
    all_to_all x1, waiting for transfers between devices, body(): lax.all_to_all(parts, 'gx', 0, 0, tiled=True, axis_index_groups=SAME_CORE)  6.1 us
    all_to_all x1, waiting for transfers between devices, body(): keyvalue = lax.all_to_all(rows, 'gx', 0, 0, tiled=True)  5.79 us
    all_to_all x1, starting transfers between devices, body(): keyvalue = lax.all_to_all(rows, 'gx', 0, 0, tiled=True)  3.88 us
    all_gather x1, blocking collectives, body(): lax.all_gather(planes[:, :WEIGHT_ROWS], 'gx', axis=0, tiled=False, axis_i...  2.23 us
  transfers between devices with their start and end apart: 4, of which 2 were waited for; matrix products, arithmetic and copies ran while one was open for 0% of the time, Pallas kernels for 3%

profile of v9, /device:TPU:1, one launch (start us, length us, event | category | flops | bytes accessed | tf_op | source)
XLA Modules:
  0.0 80.3 jit_solution(15368616316817076859)
XLA Ops:
  0.6 2.1 %shard_map.112 = (bf16[16,272,128]{2,1,0:T(8,128)(2,1)}, bf16[136,128]{1,0:T(8,128)(2,1)S(1)}) custom-call(bf16[8,2048]{1,0:T(8,128)(2,1)} %bitcast.24, f32[1,2048]{1,0:T(1,128)} %bitcast.26, f32[1,2048]{1,0:T(1,128)} %bitcast.27, bf16[64,128]{1,0:T(8,128)(2,1)} %bitcast.25, bf16[8,128]{1,0:T(8,128)(2,1)} %bitcast.28, bf16[64,128]{1,0:T(8,128)(2,1)} %out_w.1, ...), custom_call_target="tpu_custom_call" | custom-call | tf_op jit(solution)/shard_map/pallas_call | solution.py:229
  2.8 9.7 %all-to-all-start = ((bf16[16,272,128]{2,1,0:T(8,128)(2,1)}), bf16[16,272,128]{2,1,0:T(8,128)(2,1)S(1)}, u32[]{:S(2)}, u32[]{:S(2)}) async-start(bf16[16,272,128]{2,1,0:T(8,128)(2,1)} %get-tuple-element.15), calls=%async_computation | async-start | bytes 2228224 | tf_op jit(solution)/shard_map/all_to_all | solution.py:274
  12.5 34.8 %all-gather = bf16[2176,128]{1,0:T(8,128)(2,1)S(1)} all-gather(bf16[136,128]{1,0:T(8,128)(2,1)S(1)} %get-tuple-element.16), channel_id=2, replica_groups={{31,14,29,12,27,10,25,8,23,6,21,4,19,2,17,0},{15,30,13,28,11,26,9,24,7,..., dimensions={0}, use_global_device_ids=true | all-gather | bytes 591872 | tf_op jit(solution)/shard_map/all_gather | solution.py:275
  47.3 0.0 all-to-all-done.tokens.own
  47.3 2.2 %all-gather.1 = bf16[32,72,128]{2,1,0:T(8,128)(2,1)S(1)} all-gather(bf16[16,72,128]{2,1,0:T(8,128)(2,1)S(1)} %slice.3), channel_id=3, replica_groups={{0,16},{32,48},{64,80},{96,112},{128,144},{160,176},{192,208},{224,240}..., dimensions={0}, use_global_device_ids=true | all-gather | bytes 884736 | tf_op jit(solution)/shard_map/all_gather | solution.py:277
  49.5 1.1 %shard_map.113 = (bf16[32,16,128]{2,1,0:T(8,128)(2,1)}, bf16[16,208,128]{2,1,0:T(8,128)(2,1)}) custom-call(s32[1]{0:T(128)} %bitcast.1.odd_ref, bf16[16,272,128]{2,1,0:T(8,128)(2,1)S(1)} %all-to-all-done.tokens.own, bf16[2,16,72,128]{3,2,1,0:T(8,128)(2,1)S(1)} %bitcast.17, bf16[16,136,128]{2,1,0:T(8,128)(2,1)S(1)} %bitcast.15), custom_call_target="tpu_custom_call" | custom-call | tf_op jit(solution)/shard_map/pallas_call | solution.py:229
  50.6 2.0 %collective-permute-start = (bf16[16,208,128]{2,1,0:T(8,128)(2,1)}, bf16[16,208,128]{2,1,0:T(8,128)(2,1)S(1)}, u32[]{:S(2)}, u32[]{:S(2)}) collective-permute-start(bf16[16,208,128]{2,1,0:T(8,128)(2,1)} %get-tuple-element.19), channel_id=1, source_target_pairs={{0,16},{16,0},{32,48},{48,32},{64,80},{80,64},{96,112},{112,96},{1... | collective-permute-start | bytes 2555912 | tf_op jit(solution)/shard_map/ppermute | solution.py:285
  52.7 3.9 %all-to-all-start.1 = ((bf16[32,16,128]{2,1,0:T(8,128)(2,1)}), bf16[32,16,128]{2,1,0:T(8,128)(2,1)S(1)}, u32[]{:S(2)}, u32[]{:S(2)}) async-start(bf16[32,16,128]{2,1,0:T(8,128)(2,1)} %get-tuple-element.24), calls=%async_computation.1 | async-start | bytes 262144 | tf_op jit(solution)/shard_map/all_to_all | solution.py:284
  57.2 0.0 collective-permute-done.peer
  57.2 1.4 %shard_map.114 = (bf16[128,128]{1,0:T(8,128)(2,1)S(1)}, f32[128,128]{1,0:T(8,128)S(1)}, f32[128,128]{1,0:T(8,128)S(1)}, f32[128,128]{1,0:T(8,128)S(1)}) custom-call(s32[1]{0:T(128)S(6)} %copy.12.length_ref, s32[1]{0:T(128)} %bitcast.1.odd_ref, s32[1]{0:T(128)S(6)} %and.10.core_ref, bf16[16,272,128]{2,1,0:T(8,128)(2,1)S(1)} %all-to-all-done.tokens.own, ...), custom_call_target="tpu_custom_call" | custom-call | tf_op jit(solution)/shard_map/pallas_call | solution.py:229
  58.6 5.8 %all-to-all-done.1.keyvalue = bf16[32,16,128]{2,1,0:T(8,128)(2,1)S(1)} async-done(((bf16[32,16,128]{2,1,0:T(8,128)(2,1)}), bf16[32,16,128]{2,1,0:T(8,128)(2,1)S(1)}, u32[]{:S(2)}, u32[]{:S(2)}) %all-to-all-start.1) | async-done | bytes 131104 | tf_op jit(solution)/shard_map/all_to_all | solution.py:284
  64.4 0.0 copy-start
  64.4 0.0 copy-start.1
  64.4 1.6 %shard_map.115 = bf16[16,128,128]{2,1,0:T(8,128)(2,1)} custom-call(s32[1]{0:T(128)S(6)} %and.10.core_ref, s32[1]{0:T(128)} %bitcast.1.odd_ref, bf16[128,128]{1,0:T(8,128)(2,1)S(1)} %get-tuple-element.20.queries, f32[128,128]{1,0:T(8,128)S(1)} %get-tuple-element.21.old_largest, f32[128,128]{1,0:T(8,128)S(1)} %get-tuple-element.22.old_total, ...), custom_call_target="tpu_custom_call" | custom-call | tf_op jit(solution)/shard_map/pallas_call | solution.py:229
  66.0 6.7 %all-to-all-start.2 = ((bf16[16,128,128]{2,1,0:T(8,128)(2,1)}), bf16[16,128,128]{2,1,0:T(8,128)(2,1)S(1)}, u32[]{:S(2)}, u32[]{:S(2)}) async-start(bf16[16,128,128]{2,1,0:T(8,128)(2,1)} %shard_map.115), calls=%async_computation.2 | async-start | bytes 1048576 | tf_op jit(solution)/shard_map/all_to_all | solution.py:298
  72.6 0.0 copy-done
  72.6 0.0 copy-done.1
  72.6 0.8 %shard_map.117 = (bf16[72,128]{1,0:T(8,128)(2,1)}, bf16[72,128]{1,0:T(8,128)(2,1)}) custom-call(s32[1]{0:T(128)S(6)} %copy.12.length_ref, s32[1]{0:T(128)} %bitcast.place_ref, bf16[32,16,128]{2,1,0:T(8,128)(2,1)S(1)} %all-to-all-done.1.keyvalue, bf16[72,128]{1,0:T(8,128)(2,1)S(1)} %bitcast.20, bf16[72,128]{1,0:T(8,128)(2,1)S(1)} %bitcast.22), custom_call_target="tpu_custom_call" | custom-call | tf_op jit(solution)/shard_map/pallas_call | solution.py:229
  73.5 6.1 %all-to-all-done.2.parts = bf16[16,128,128]{2,1,0:T(8,128)(2,1)S(1)} async-done(((bf16[16,128,128]{2,1,0:T(8,128)(2,1)}), bf16[16,128,128]{2,1,0:T(8,128)(2,1)S(1)}, u32[]{:S(2)}, u32[]{:S(2)}) %all-to-all-start.2) | async-done | bytes 524320 | tf_op jit(solution)/shard_map/all_to_all | solution.py:298
  79.6 0.7 shard_map.116
  (1 shorter events, 0.0 us)
Async XLA Ops:
  2.8 44.5 %all-to-all-start = ((bf16[16,272,128]{2,1,0:T(8,128)(2,1)}), bf16[16,272,128]{2,1,0:T(8,128)(2,1)S(1)}, u32[]{:S(2)}, u32[]{:S(2)}) async-start(bf16[16,272,128]{2,1,0:T(8,128)(2,1)} %get-tuple-element.15), calls=%async_computation | async-start | bytes 2228224 | tf_op jit(solution)/shard_map/all_to_all | solution.py:274
  50.6 6.6 %collective-permute-start = (bf16[16,208,128]{2,1,0:T(8,128)(2,1)}, bf16[16,208,128]{2,1,0:T(8,128)(2,1)S(1)}, u32[]{:S(2)}, u32[]{:S(2)}) collective-permute-start(bf16[16,208,128]{2,1,0:T(8,128)(2,1)} %get-tuple-element.19), channel_id=1, source_target_pairs={{0,16},{16,0},{32,48},{48,32},{64,80},{80,64},{96,112},{112,96},{1... | collective-permute-start | bytes 2555912 | tf_op jit(solution)/shard_map/ppermute | solution.py:285
  52.7 11.7 %all-to-all-start.1 = ((bf16[32,16,128]{2,1,0:T(8,128)(2,1)}), bf16[32,16,128]{2,1,0:T(8,128)(2,1)S(1)}, u32[]{:S(2)}, u32[]{:S(2)}) async-start(bf16[32,16,128]{2,1,0:T(8,128)(2,1)} %get-tuple-element.24), calls=%async_computation.1 | async-start | bytes 262144 | tf_op jit(solution)/shard_map/all_to_all | solution.py:284
  64.4 8.2 %copy-start = (bf16[1,72,128]{2,1,0:T(8,128)(2,1)S(1)}, bf16[1,72,128]{2,1,0:T(8,128)(2,1)}, u32[]{:S(2)}) copy-start(bf16[1,72,128]{2,1,0:T(8,128)(2,1)} %param.15) | copy-start | bytes 55300
  64.4 8.2 %copy-start.1 = (bf16[1,72,128]{2,1,0:T(8,128)(2,1)S(1)}, bf16[1,72,128]{2,1,0:T(8,128)(2,1)}, u32[]{:S(2)}) copy-start(bf16[1,72,128]{2,1,0:T(8,128)(2,1)} %param.16) | copy-start | bytes 55300
  66.0 13.6 %all-to-all-start.2 = ((bf16[16,128,128]{2,1,0:T(8,128)(2,1)}), bf16[16,128,128]{2,1,0:T(8,128)(2,1)S(1)}, u32[]{:S(2)}, u32[]{:S(2)}) async-start(bf16[16,128,128]{2,1,0:T(8,128)(2,1)} %shard_map.115), calls=%async_computation.2 | async-start | bytes 1048576 | tf_op jit(solution)/shard_map/all_to_all | solution.py:298

commit v10 on v9

--- a/solution.py
+++ b/solution.py
@@ -46,35 +46,50 @@
 
 
 def prepare(hidden, gain, bias, query_w, keyvalue_w, out_w, key_page, value_page, send, weights, *scratch):
-    held, done = scratch[:-1], scratch[-1]
-    targets = held + (
-        weights.at[0:HALF],
-        weights.at[HALF:WEIGHT_ROWS],
-        weights.at[WEIGHT_ROWS : WEIGHT_ROWS + HALF],
-    )
-    sources = (hidden, gain, bias, key_page, value_page, query_w, keyvalue_w, out_w)
+    tokens, gains, biases, block, arrived, left = scratch
     copies = [
-        pltpu.make_async_copy(source, target, done.at[at])
-        for at, (source, target) in enumerate(zip(sources, targets))
+        pltpu.make_async_copy(source, target, arrived.at[at])
+        for at, (source, target) in enumerate(
+            (
+                (hidden, tokens),
+                (gain, gains),
+                (bias, biases),
+                (key_page, block.at[0:PAGE]),
+                (value_page, block.at[PAGE:KV_ROWS]),
+                (query_w, weights.at[0:HALF]),
+                (keyvalue_w, weights.at[HALF:WEIGHT_ROWS]),
+                (out_w, weights.at[WEIGHT_ROWS : WEIGHT_ROWS + HALF]),
+            )
+        )
     ]
     for copy in copies:
         copy.start()
-    for copy in copies:
+    copies[3].wait()
+    copies[4].wait()
+    sent = [
+        pltpu.make_async_copy(block.at[0:KV_ROWS], send.at[chip, 0:KV_ROWS], left.at[chip]) for chip in range(CHIPS)
+    ]
+    for copy in sent:
+        copy.start()
+    for copy in copies[:3]:
         copy.wait()
-    values = held[0][...].astype(F32)
+    values = tokens[...].astype(F32)
     average = jnp.mean(values, axis=-1, keepdims=True)
     centred = values - average
     spread = jnp.mean(centred * centred, axis=-1, keepdims=True)
-    normed = (centred * lax.rsqrt(spread + 1e-05) * held[1][...] + held[2][...]).astype(BF16)
-    key_rows = held[3][...]
-    value_rows = held[4][...]
-    for chip in range(CHIPS):
-        send[chip, 0:PAGE, :] = key_rows
-        send[chip, PAGE:KV_ROWS, :] = value_rows
-        for chunk in range(CHUNKS):
-            send[chip, KV_ROWS + OWN * chunk : KV_ROWS + OWN * (chunk + 1), :] = normed[
-                :, LANES * chunk : LANES * (chunk + 1)
-            ]
+    normed = (centred * lax.rsqrt(spread + 1e-05) * gains[...] + biases[...]).astype(BF16)
+    for chunk in range(CHUNKS):
+        block[KV_ROWS + OWN * chunk : KV_ROWS + OWN * (chunk + 1), :] = normed[:, LANES * chunk : LANES * (chunk + 1)]
+    more = [
+        pltpu.make_async_copy(
+            block.at[KV_ROWS:SEND_ROWS], send.at[chip, KV_ROWS:SEND_ROWS], left.at[CHIPS + chip]
+        )
+        for chip in range(CHIPS)
+    ]
+    for copy in more:
+        copy.start()
+    for copy in copies[5:] + sent + more:
+        copy.wait()
 
 
 def part_of(gathered, odd, core, chunk):
@@ -90,7 +105,15 @@
     return jnp.concatenate(pieces, axis=1)
 
 
-def project_keyvalue(odd_ref, tokens, weights, planes, keyvalue, swapped):
+def project_keyvalue(odd_ref, tokens, weights, planes, keyvalue, swapped, left):
+    copies = [
+        pltpu.make_async_copy(tokens.at[:, 0:KV_ROWS], swapped.at[:, 0:KV_ROWS], left.at[0]),
+        pltpu.make_async_copy(
+            planes.at[:, WEIGHT_ROWS : WEIGHT_ROWS + HALF], swapped.at[:, KV_ROWS : KV_ROWS + HALF], left.at[1]
+        ),
+    ]
+    for copy in copies:
+        copy.start()
     odd = odd_ref[0]
     narrow = jnp.concatenate(
         [
@@ -104,8 +127,8 @@
     rounded = dot_nt(narrow, gathered_tokens(tokens)).astype(BF16)
     for place in range(CHIPS * CORES):
         keyvalue[place] = rounded
-    swapped[:, 0:KV_ROWS, :] = tokens[:, 0:KV_ROWS, :]
-    swapped[:, KV_ROWS : KV_ROWS + HALF, :] = planes[:, WEIGHT_ROWS : WEIGHT_ROWS + HALF, :]
+    for copy in copies:
+        copy.wait()
 
 
 def project_queries(odd, tokens, weights):
@@ -183,13 +206,26 @@
     turned = pltpu.roll(attended, HALF, 1)
     same = (core + odd_ref[0]) % CORES == 0
     sides = (jnp.where(same, attended, turned).astype(BF16), jnp.where(same, turned, attended).astype(BF16))
-    for chunk in range(CHUNKS):
-        at = CHUNKS - 1 - chunk
-        square = jnp.concatenate(
-            [planes[at, WEIGHT_ROWS : WEIGHT_ROWS + HALF, :], peer[at, KV_ROWS : KV_ROWS + HALF, :]], axis=0
+    for parity in range(2):
+        chunks = range(parity, CHUNKS, 2)
+        wide = jnp.concatenate(
+            [
+                jnp.concatenate(
+                    [
+                        planes[CHUNKS - 1 - chunk, WEIGHT_ROWS : WEIGHT_ROWS + HALF, :],
+                        peer[CHUNKS - 1 - chunk, KV_ROWS : KV_ROWS + HALF, :],
+                    ],
+                    axis=0,
+                )
+                for chunk in chunks
+            ],
+            axis=1,
         )
-        part = dot(sides[chunk % 2], square)
-        result[:, OWN * chunk : OWN * (chunk + 1), :] = part.reshape(CHIPS, OWN, LANES).astype(BF16)
+        part = dot(sides[parity], wide)
+        for at, chunk in enumerate(chunks):
+            result[:, OWN * chunk : OWN * (chunk + 1), :] = (
+                part[:, LANES * at : LANES * (at + 1)].reshape(CHIPS, OWN, LANES).astype(BF16)
+            )
 
 
 def add_heads(parts, result):
@@ -215,23 +251,19 @@
     new_value[...] = jnp.where(inside, value_rows, value_page[...].astype(F32)).astype(BF16)
 
 
-def call(kernel, shapes, arguments, scalars=0, held=None):
-    space = pltpu.VMEM if held is None else pltpu.HBM
+def call(kernel, shapes, arguments, scalars=0, far=False, spaces=None, scratch=()):
+    space = pltpu.HBM if far else pltpu.VMEM
     specs = [
         pl.BlockSpec(memory_space=pltpu.SMEM if at < scalars else space) for at in range(len(arguments))
     ]
-    scratch = []
-    if held is not None:
-        scratch = [pltpu.VMEM(shape, dtype) for shape, dtype in held]
-        scratch.append(pltpu.SemaphoreType.DMA((len(arguments),)))
-    if held is not None:
+    if far:
         arguments = [pltpu.with_memory_space_constraint(argument, pltpu.HBM) for argument in arguments]
     return pl.pallas_call(
         kernel,
         out_shape=[jax.ShapeDtypeStruct(shape, dtype) for shape, dtype in shapes],
         in_specs=specs,
-        out_specs=[pl.BlockSpec(memory_space=pltpu.VMEM)] * len(shapes),
-        scratch_shapes=scratch,
+        out_specs=[pl.BlockSpec(memory_space=space) for space in spaces or [pltpu.VMEM] * len(shapes)],
+        scratch_shapes=list(scratch),
         compiler_params=pltpu.CompilerParams(vmem_limit_bytes=48 * 1024 * 1024),
     )(*arguments)
 
@@ -263,12 +295,15 @@
             key_cache[0],
             value_cache[0],
         ),
-        held=[
-            ((OWN, FEATURES), BF16),
-            ((1, FEATURES), F32),
-            ((1, FEATURES), F32),
-            ((PAGE, LANES), BF16),
-            ((PAGE, LANES), BF16),
+        far=True,
+        spaces=[pltpu.HBM, pltpu.VMEM],
+        scratch=[
+            pltpu.VMEM((OWN, FEATURES), BF16),
+            pltpu.VMEM((1, FEATURES), F32),
+            pltpu.VMEM((1, FEATURES), F32),
+            pltpu.VMEM((SEND_ROWS, LANES), BF16),
+            pltpu.SemaphoreType.DMA((8,)),
+            pltpu.SemaphoreType.DMA((2 * CHIPS,)),
         ],
     )
     own = lax.all_to_all(send, "gx", 0, 0, tiled=True, axis_index_groups=SAME_CORE)
@@ -280,6 +315,8 @@
         [((CHIPS * CORES, CORES * OWN, LANES), BF16), ((CHIPS, KV_ROWS + HALF, LANES), BF16)],
         (odd, own, inner, planes),
         scalars=1,
+        spaces=[pltpu.VMEM, pltpu.HBM],
+        scratch=[pltpu.SemaphoreType.DMA((2,))],
     )
     keyvalue = lax.all_to_all(rows, "gx", 0, 0, tiled=True)
     peer = lax.ppermute(swapped, "gx", SWAP)

time: 80.7 us -> 81.4 us (level)
  no operation moved by 1% of the time
where the time goes in v10:
time: 81.4 us; the launch traced here: 80.9 us
  blocking collectives  37 us (45%)
  starting transfers between devices  22.3 us (27%)
  waiting for transfers between devices  11.9 us (15%)
  Pallas kernels  8.29 us (10%)
  between operations  1.35 us (2%)
    all_gather x1, blocking collectives, body(): lax.all_gather(weights, ('gx', 'gy'), axis=0, tiled=False, axis_index_gro...  34.8 us
    all_to_all x1, starting transfers between devices, body(): lax.all_to_all(send, 'gx', 0, 0, tiled=True, axis_index_groups=SAME_CORE)  9.73 us
    pallas_call x6, Pallas kernels, call(): pl.pallas_call(kernel, out_shape=[jax.ShapeDtypeStruct(shape, dtype) for...  8.29 us
    all_to_all x1, starting transfers between devices, body(): lax.all_to_all(parts, 'gx', 0, 0, tiled=True, axis_index_groups=SAME_CORE)  6.66 us
    all_to_all x1, waiting for transfers between devices, body(): lax.all_to_all(parts, 'gx', 0, 0, tiled=True, axis_index_groups=SAME_CORE)  6.1 us
    all_to_all x1, waiting for transfers between devices, body(): keyvalue = lax.all_to_all(rows, 'gx', 0, 0, tiled=True)  5.79 us
    all_to_all x1, starting transfers between devices, body(): keyvalue = lax.all_to_all(rows, 'gx', 0, 0, tiled=True)  3.88 us
    all_gather x1, blocking collectives, body(): lax.all_gather(planes[:, :WEIGHT_ROWS], 'gx', axis=0, tiled=False, axis_i...  2.23 us
  transfers between devices with their start and end apart: 4, of which 2 were waited for; matrix products, arithmetic and copies ran while one was open for 0% of the time, Pallas kernels for 3%

profile of v10, /device:TPU:1, one launch (start us, length us, event | category | flops | bytes accessed | tf_op | source)
XLA Modules:
  0.0 80.9 jit_solution(14689306476761877756)
XLA Ops:
  0.6 2.2 %shard_map.112 = (bf16[16,272,128]{2,1,0:T(8,128)(2,1)}, bf16[136,128]{1,0:T(8,128)(2,1)S(1)}) custom-call(bf16[8,2048]{1,0:T(8,128)(2,1)} %bitcast.24, f32[1,2048]{1,0:T(1,128)} %bitcast.26, f32[1,2048]{1,0:T(1,128)} %bitcast.27, bf16[64,128]{1,0:T(8,128)(2,1)} %bitcast.25, bf16[8,128]{1,0:T(8,128)(2,1)} %bitcast.28, bf16[64,128]{1,0:T(8,128)(2,1)} %out_w.1, ...), custom_call_target="tpu_custom_call" | custom-call | tf_op jit(solution)/shard_map/pallas_call | solution.py:261
  2.8 9.7 %all-to-all-start = ((bf16[16,272,128]{2,1,0:T(8,128)(2,1)}), bf16[16,272,128]{2,1,0:T(8,128)(2,1)S(1)}, u32[]{:S(2)}, u32[]{:S(2)}) async-start(bf16[16,272,128]{2,1,0:T(8,128)(2,1)} %get-tuple-element.15), calls=%async_computation | async-start | bytes 2228224 | tf_op jit(solution)/shard_map/all_to_all | solution.py:309
  12.6 34.8 %all-gather = bf16[2176,128]{1,0:T(8,128)(2,1)S(1)} all-gather(bf16[136,128]{1,0:T(8,128)(2,1)S(1)} %get-tuple-element.16), channel_id=2, replica_groups={{31,14,29,12,27,10,25,8,23,6,21,4,19,2,17,0},{15,30,13,28,11,26,9,24,7,..., dimensions={0}, use_global_device_ids=true | all-gather | bytes 591872 | tf_op jit(solution)/shard_map/all_gather | solution.py:310
  47.3 0.0 all-to-all-done.tokens.own
  47.4 2.2 %all-gather.1 = bf16[32,72,128]{2,1,0:T(8,128)(2,1)S(1)} all-gather(bf16[16,72,128]{2,1,0:T(8,128)(2,1)S(1)} %slice.3), channel_id=3, replica_groups={{0,16},{32,48},{64,80},{96,112},{128,144},{160,176},{192,208},{224,240}..., dimensions={0}, use_global_device_ids=true | all-gather | bytes 884736 | tf_op jit(solution)/shard_map/all_gather | solution.py:312
  49.6 1.7 %shard_map.113 = (bf16[32,16,128]{2,1,0:T(8,128)(2,1)}, bf16[16,208,128]{2,1,0:T(8,128)(2,1)}) custom-call(s32[1]{0:T(128)} %bitcast.1.odd_ref, bf16[16,272,128]{2,1,0:T(8,128)(2,1)S(1)} %all-to-all-done.tokens.own, bf16[2,16,72,128]{3,2,1,0:T(8,128)(2,1)S(1)} %bitcast.17, bf16[16,136,128]{2,1,0:T(8,128)(2,1)S(1)} %bitcast.15), custom_call_target="tpu_custom_call" | custom-call | tf_op jit(solution)/shard_map/pallas_call | solution.py:261
  51.3 2.1 %collective-permute-start = (bf16[16,208,128]{2,1,0:T(8,128)(2,1)}, bf16[16,208,128]{2,1,0:T(8,128)(2,1)S(1)}, u32[]{:S(2)}, u32[]{:S(2)}) collective-permute-start(bf16[16,208,128]{2,1,0:T(8,128)(2,1)} %get-tuple-element.19), channel_id=1, source_target_pairs={{0,16},{16,0},{32,48},{48,32},{64,80},{80,64},{96,112},{112,96},{1... | collective-permute-start | bytes 2555912 | tf_op jit(solution)/shard_map/ppermute | solution.py:322
  53.3 3.9 %all-to-all-start.1 = ((bf16[32,16,128]{2,1,0:T(8,128)(2,1)}), bf16[32,16,128]{2,1,0:T(8,128)(2,1)S(1)}, u32[]{:S(2)}, u32[]{:S(2)}) async-start(bf16[32,16,128]{2,1,0:T(8,128)(2,1)} %get-tuple-element.24), calls=%async_computation.1 | async-start | bytes 262144 | tf_op jit(solution)/shard_map/all_to_all | solution.py:321
  57.9 0.0 collective-permute-done.peer
  57.9 1.4 %shard_map.114 = (bf16[128,128]{1,0:T(8,128)(2,1)S(1)}, f32[128,128]{1,0:T(8,128)S(1)}, f32[128,128]{1,0:T(8,128)S(1)}, f32[128,128]{1,0:T(8,128)S(1)}) custom-call(s32[1]{0:T(128)S(6)} %copy.12.length_ref, s32[1]{0:T(128)} %bitcast.1.odd_ref, s32[1]{0:T(128)S(6)} %and.10.core_ref, bf16[16,272,128]{2,1,0:T(8,128)(2,1)S(1)} %all-to-all-done.tokens.own, ...), custom_call_target="tpu_custom_call" | custom-call | tf_op jit(solution)/shard_map/pallas_call | solution.py:261
  59.2 5.8 %all-to-all-done.1.keyvalue = bf16[32,16,128]{2,1,0:T(8,128)(2,1)S(1)} async-done(((bf16[32,16,128]{2,1,0:T(8,128)(2,1)}), bf16[32,16,128]{2,1,0:T(8,128)(2,1)S(1)}, u32[]{:S(2)}, u32[]{:S(2)}) %all-to-all-start.1) | async-done | bytes 131104 | tf_op jit(solution)/shard_map/all_to_all | solution.py:321
  65.0 0.0 copy-start
  65.0 0.0 copy-start.1
  65.0 1.6 %shard_map.115 = bf16[16,128,128]{2,1,0:T(8,128)(2,1)} custom-call(s32[1]{0:T(128)S(6)} %and.10.core_ref, s32[1]{0:T(128)} %bitcast.1.odd_ref, bf16[128,128]{1,0:T(8,128)(2,1)S(1)} %get-tuple-element.20.queries, f32[128,128]{1,0:T(8,128)S(1)} %get-tuple-element.21.old_largest, f32[128,128]{1,0:T(8,128)S(1)} %get-tuple-element.22.old_total, ...), custom_call_target="tpu_custom_call" | custom-call | tf_op jit(solution)/shard_map/pallas_call | solution.py:261
  66.6 6.7 %all-to-all-start.2 = ((bf16[16,128,128]{2,1,0:T(8,128)(2,1)}), bf16[16,128,128]{2,1,0:T(8,128)(2,1)S(1)}, u32[]{:S(2)}, u32[]{:S(2)}) async-start(bf16[16,128,128]{2,1,0:T(8,128)(2,1)} %shard_map.115), calls=%async_computation.2 | async-start | bytes 1048576 | tf_op jit(solution)/shard_map/all_to_all | solution.py:335
  73.3 0.0 copy-done
  73.3 0.0 copy-done.1
  73.3 0.8 %shard_map.117 = (bf16[72,128]{1,0:T(8,128)(2,1)}, bf16[72,128]{1,0:T(8,128)(2,1)}) custom-call(s32[1]{0:T(128)S(6)} %copy.12.length_ref, s32[1]{0:T(128)} %bitcast.place_ref, bf16[32,16,128]{2,1,0:T(8,128)(2,1)S(1)} %all-to-all-done.1.keyvalue, bf16[72,128]{1,0:T(8,128)(2,1)S(1)} %bitcast.20, bf16[72,128]{1,0:T(8,128)(2,1)S(1)} %bitcast.22), custom_call_target="tpu_custom_call" | custom-call | tf_op jit(solution)/shard_map/pallas_call | solution.py:261
  74.1 6.1 %all-to-all-done.2.parts = bf16[16,128,128]{2,1,0:T(8,128)(2,1)S(1)} async-done(((bf16[16,128,128]{2,1,0:T(8,128)(2,1)}), bf16[16,128,128]{2,1,0:T(8,128)(2,1)S(1)}, u32[]{:S(2)}, u32[]{:S(2)}) %all-to-all-start.2) | async-done | bytes 524320 | tf_op jit(solution)/shard_map/all_to_all | solution.py:335
  80.2 0.7 shard_map.116
  (1 shorter events, 0.0 us)
Async XLA Ops:
  2.8 44.5 %all-to-all-start = ((bf16[16,272,128]{2,1,0:T(8,128)(2,1)}), bf16[16,272,128]{2,1,0:T(8,128)(2,1)S(1)}, u32[]{:S(2)}, u32[]{:S(2)}) async-start(bf16[16,272,128]{2,1,0:T(8,128)(2,1)} %get-tuple-element.15), calls=%async_computation | async-start | bytes 2228224 | tf_op jit(solution)/shard_map/all_to_all | solution.py:309
  51.3 6.6 %collective-permute-start = (bf16[16,208,128]{2,1,0:T(8,128)(2,1)}, bf16[16,208,128]{2,1,0:T(8,128)(2,1)S(1)}, u32[]{:S(2)}, u32[]{:S(2)}) collective-permute-start(bf16[16,208,128]{2,1,0:T(8,128)(2,1)} %get-tuple-element.19), channel_id=1, source_target_pairs={{0,16},{16,0},{32,48},{48,32},{64,80},{80,64},{96,112},{112,96},{1... | collective-permute-start | bytes 2555912 | tf_op jit(solution)/shard_map/ppermute | solution.py:322
  53.3 11.7 %all-to-all-start.1 = ((bf16[32,16,128]{2,1,0:T(8,128)(2,1)}), bf16[32,16,128]{2,1,0:T(8,128)(2,1)S(1)}, u32[]{:S(2)}, u32[]{:S(2)}) async-start(bf16[32,16,128]{2,1,0:T(8,128)(2,1)} %get-tuple-element.24), calls=%async_computation.1 | async-start | bytes 262144 | tf_op jit(solution)/shard_map/all_to_all | solution.py:321
  65.0 8.2 %copy-start = (bf16[1,72,128]{2,1,0:T(8,128)(2,1)S(1)}, bf16[1,72,128]{2,1,0:T(8,128)(2,1)}, u32[]{:S(2)}) copy-start(bf16[1,72,128]{2,1,0:T(8,128)(2,1)} %param.15) | copy-start | bytes 55300
  65.0 8.2 %copy-start.1 = (bf16[1,72,128]{2,1,0:T(8,128)(2,1)S(1)}, bf16[1,72,128]{2,1,0:T(8,128)(2,1)}, u32[]{:S(2)}) copy-start(bf16[1,72,128]{2,1,0:T(8,128)(2,1)} %param.16) | copy-start | bytes 55300
  66.6 13.6 %all-to-all-start.2 = ((bf16[16,128,128]{2,1,0:T(8,128)(2,1)}), bf16[16,128,128]{2,1,0:T(8,128)(2,1)S(1)}, u32[]{:S(2)}, u32[]{:S(2)}) async-start(bf16[16,128,128]{2,1,0:T(8,128)(2,1)} %shard_map.115), calls=%async_computation.2 | async-start | bytes 1048576 | tf_op jit(solution)/shard_map/all_to_all | solution.py:335

commit v11 on v9

--- a/solution.py
+++ b/solution.py
@@ -82,9 +82,9 @@
     return gathered.at[side, CHUNKS - 1 - chunk]
 
 
-def gathered_tokens(tokens):
+def gathered_tokens(tokens, chunks=range(CHUNKS)):
     pieces = []
-    for chunk in range(CHUNKS):
+    for chunk in chunks:
         first = KV_ROWS + OWN * chunk
         pieces.append(tokens[:, first : first + OWN, :].astype(F32).reshape(LANES, LANES).astype(BF16))
     return jnp.concatenate(pieces, axis=1)
@@ -95,7 +95,7 @@
     narrow = jnp.concatenate(
         [
             jnp.concatenate(
-                [part_of(weights, odd, core, chunk)[HALF:WEIGHT_ROWS, :].astype(F32) for core in range(CORES)], axis=0
+                [part_of(weights, odd, core, chunk)[...].astype(F32) for core in range(CORES)], axis=0
             )
             for chunk in range(CHUNKS)
         ],
@@ -106,17 +106,26 @@
         keyvalue[place] = rounded
     swapped[:, 0:KV_ROWS, :] = tokens[:, 0:KV_ROWS, :]
     swapped[:, KV_ROWS : KV_ROWS + HALF, :] = planes[:, WEIGHT_ROWS : WEIGHT_ROWS + HALF, :]
-
-
-def project_queries(odd, tokens, weights):
-    square = jnp.concatenate(
-        [
-            jnp.concatenate([part_of(weights, odd, core, chunk)[0:HALF, :] for core in range(CORES)], axis=0)
-            for chunk in range(CHUNKS)
-        ],
-        axis=1,
-    )
-    return dot_nt(gathered_tokens(tokens), square).astype(BF16)
+    swapped[:, KV_ROWS + HALF : SEND_ROWS, :] = planes[:, 0:HALF, :]
+
+
+def project_queries(same, tokens, planes, peer):
+    sums = []
+    for parity in range(2):
+        chunks = range(parity, CHUNKS, 2)
+        square = jnp.concatenate(
+            [
+                jnp.concatenate(
+                    [planes[CHUNKS - 1 - chunk, 0:HALF, :], peer[CHUNKS - 1 - chunk, KV_ROWS + HALF : SEND_ROWS, :]],
+                    axis=0,
+                )
+                for chunk in chunks
+            ],
+            axis=1,
+        )
+        sums.append(dot_nt(gathered_tokens(tokens, chunks), square))
+    total = sums[0] + pltpu.roll(sums[1], HALF, 1)
+    return jnp.where(same, total, pltpu.roll(total, HALF, 1)).astype(BF16)
 
 
 def new_columns(keyvalue, core, first):
@@ -129,12 +138,12 @@
 
 
 def attend_cached(
-    length_ref, odd_ref, core_ref, own, weights, peer, queries, largest_out, total_out, summed_out
+    length_ref, odd_ref, core_ref, own, planes, peer, queries, largest_out, total_out, summed_out
 ):
     length = length_ref[0]
     core = core_ref[0]
     scale = float(LANES) ** (-0.5)
-    query_rows = project_queries(odd_ref[0], own, weights)
+    query_rows = project_queries((core + odd_ref[0]) % CORES == 0, own, planes, peer)
     queries[...] = query_rows
     places = CHIPS * PAGE
     lane = iota((1, places), 1)
@@ -274,10 +283,10 @@
     own = lax.all_to_all(send, "gx", 0, 0, tiled=True, axis_index_groups=SAME_CORE)
     planes = lax.all_gather(weights, ("gx", "gy"), axis=0, tiled=False, axis_index_groups=COLUMNS)
     own, planes = lax.optimization_barrier((own, planes))
-    inner = lax.all_gather(planes[:, :WEIGHT_ROWS], "gx", axis=0, tiled=False, axis_index_groups=ONE_CHIP)
+    inner = lax.all_gather(planes[:, HALF:WEIGHT_ROWS], "gx", axis=0, tiled=False, axis_index_groups=ONE_CHIP)
     rows, swapped = call(
         project_keyvalue,
-        [((CHIPS * CORES, CORES * OWN, LANES), BF16), ((CHIPS, KV_ROWS + HALF, LANES), BF16)],
+        [((CHIPS * CORES, CORES * OWN, LANES), BF16), ((CHIPS, SEND_ROWS, LANES), BF16)],
         (odd, own, inner, planes),
         scalars=1,
     )
@@ -286,7 +295,7 @@
     queries, largest, total, summed = call(
         attend_cached,
         [((LANES, LANES), BF16)] + [((LANES, LANES), F32)] * 3,
-        (cache_length, odd, core, own, inner, peer),
+        (cache_length, odd, core, own, planes, peer),
         scalars=3,
     )
     (parts,) = call(

time: 80.7 us -> 80.4 us (level)
  no operation moved by 1% of the time
where the time goes in v11:
time: 80.4 us; the launch traced here: 80 us
  blocking collectives  36.6 us (46%)
  starting transfers between devices  22.3 us (28%)
  waiting for transfers between devices  12 us (15%)
  Pallas kernels  7.72 us (10%)
  between operations  1.34 us (2%)
    all_gather x1, blocking collectives, body(): lax.all_gather(weights, ('gx', 'gy'), axis=0, tiled=False, axis_index_gro...  34.8 us
    all_to_all x1, starting transfers between devices, body(): lax.all_to_all(send, 'gx', 0, 0, tiled=True, axis_index_groups=SAME_CORE)  9.73 us
    pallas_call x6, Pallas kernels, call(): pl.pallas_call(kernel, out_shape=[jax.ShapeDtypeStruct(shape, dtype) for...  7.72 us
    all_to_all x1, starting transfers between devices, body(): lax.all_to_all(parts, 'gx', 0, 0, tiled=True, axis_index_groups=SAME_CORE)  6.66 us
    all_to_all x1, waiting for transfers between devices, body(): lax.all_to_all(parts, 'gx', 0, 0, tiled=True, axis_index_groups=SAME_CORE)  6.1 us
    all_to_all x1, waiting for transfers between devices, body(): keyvalue = lax.all_to_all(rows, 'gx', 0, 0, tiled=True)  5.85 us
    all_to_all x1, starting transfers between devices, body(): keyvalue = lax.all_to_all(rows, 'gx', 0, 0, tiled=True)  3.86 us
    ppermute x1, starting transfers between devices, body(): peer = lax.ppermute(swapped, 'gx', SWAP)  2.06 us
  transfers between devices with their start and end apart: 4, of which 2 were waited for; matrix products, arithmetic and copies ran while one was open for 0% of the time, Pallas kernels for 3%

profile of v11, /device:TPU:1, one launch (start us, length us, event | category | flops | bytes accessed | tf_op | source)
XLA Modules:
  0.0 80.0 jit_solution(16912003283106311363)
XLA Ops:
  0.6 2.1 %shard_map.112 = (bf16[16,272,128]{2,1,0:T(8,128)(2,1)}, bf16[136,128]{1,0:T(8,128)(2,1)S(1)}) custom-call(bf16[8,2048]{1,0:T(8,128)(2,1)} %bitcast.24, f32[1,2048]{1,0:T(1,128)} %bitcast.26, f32[1,2048]{1,0:T(1,128)} %bitcast.27, bf16[64,128]{1,0:T(8,128)(2,1)} %bitcast.25, bf16[8,128]{1,0:T(8,128)(2,1)} %bitcast.28, bf16[64,128]{1,0:T(8,128)(2,1)} %out_w.1, ...), custom_call_target="tpu_custom_call" | custom-call | tf_op jit(solution)/shard_map/pallas_call | solution.py:238
  2.8 9.7 %all-to-all-start = ((bf16[16,272,128]{2,1,0:T(8,128)(2,1)}), bf16[16,272,128]{2,1,0:T(8,128)(2,1)S(1)}, u32[]{:S(2)}, u32[]{:S(2)}) async-start(bf16[16,272,128]{2,1,0:T(8,128)(2,1)} %get-tuple-element.15), calls=%async_computation | async-start | bytes 2228224 | tf_op jit(solution)/shard_map/all_to_all | solution.py:283
  12.5 34.8 %all-gather = bf16[2176,128]{1,0:T(8,128)(2,1)S(1)} all-gather(bf16[136,128]{1,0:T(8,128)(2,1)S(1)} %get-tuple-element.16), channel_id=2, replica_groups={{31,14,29,12,27,10,25,8,23,6,21,4,19,2,17,0},{15,30,13,28,11,26,9,24,7,..., dimensions={0}, use_global_device_ids=true | all-gather | bytes 591872 | tf_op jit(solution)/shard_map/all_gather | solution.py:284
  47.3 0.0 all-to-all-done.tokens.own
  47.3 1.8 %all-gather.1 = bf16[32,8,128]{2,1,0:T(8,128)(2,1)S(1)} all-gather(bf16[16,8,128]{2,1,0:T(8,128)(2,1)S(1)} %slice.3), channel_id=3, replica_groups={{0,16},{32,48},{64,80},{96,112},{128,144},{160,176},{192,208},{224,240}..., dimensions={0}, use_global_device_ids=true | all-gather | bytes 98304 | tf_op jit(solution)/shard_map/all_gather | solution.py:286
  49.1 1.2 %shard_map.113 = (bf16[32,16,128]{2,1,0:T(8,128)(2,1)}, bf16[16,272,128]{2,1,0:T(8,128)(2,1)}) custom-call(s32[1]{0:T(128)} %bitcast.1.odd_ref, bf16[16,272,128]{2,1,0:T(8,128)(2,1)S(1)} %all-to-all-done.tokens.own, bf16[2,16,8,128]{3,2,1,0:T(8,128)(2,1)S(1)} %bitcast.18, bf16[16,136,128]{2,1,0:T(8,128)(2,1)S(1)} %bitcast.15), custom_call_target="tpu_custom_call" | custom-call | tf_op jit(solution)/shard_map/pallas_call | solution.py:238
  50.4 2.1 %collective-permute-start = (bf16[16,272,128]{2,1,0:T(8,128)(2,1)}, bf16[16,272,128]{2,1,0:T(8,128)(2,1)S(1)}, u32[]{:S(2)}, u32[]{:S(2)}) collective-permute-start(bf16[16,272,128]{2,1,0:T(8,128)(2,1)} %get-tuple-element.19), channel_id=1, source_target_pairs={{0,16},{16,0},{32,48},{48,32},{64,80},{80,64},{96,112},{112,96},{1... | collective-permute-start | bytes 3342344 | tf_op jit(solution)/shard_map/ppermute | solution.py:294
  52.4 3.9 %all-to-all-start.1 = ((bf16[32,16,128]{2,1,0:T(8,128)(2,1)}), bf16[32,16,128]{2,1,0:T(8,128)(2,1)S(1)}, u32[]{:S(2)}, u32[]{:S(2)}) async-start(bf16[32,16,128]{2,1,0:T(8,128)(2,1)} %get-tuple-element.24), calls=%async_computation.1 | async-start | bytes 262144 | tf_op jit(solution)/shard_map/all_to_all | solution.py:293
  56.9 0.0 collective-permute-done.peer
  56.9 1.3 %shard_map.114 = (bf16[128,128]{1,0:T(8,128)(2,1)S(1)}, f32[128,128]{1,0:T(8,128)S(1)}, f32[128,128]{1,0:T(8,128)S(1)}, f32[128,128]{1,0:T(8,128)S(1)}) custom-call(s32[1]{0:T(128)S(6)} %copy.12.length_ref, s32[1]{0:T(128)} %bitcast.1.odd_ref, s32[1]{0:T(128)S(6)} %and.10.core_ref, bf16[16,272,128]{2,1,0:T(8,128)(2,1)S(1)} %all-to-all-done.tokens.own, ...), custom_call_target="tpu_custom_call" | custom-call | tf_op jit(solution)/shard_map/pallas_call | solution.py:238
  58.2 5.9 %all-to-all-done.1.keyvalue = bf16[32,16,128]{2,1,0:T(8,128)(2,1)S(1)} async-done(((bf16[32,16,128]{2,1,0:T(8,128)(2,1)}), bf16[32,16,128]{2,1,0:T(8,128)(2,1)S(1)}, u32[]{:S(2)}, u32[]{:S(2)}) %all-to-all-start.1) | async-done | bytes 131104 | tf_op jit(solution)/shard_map/all_to_all | solution.py:293
  64.1 0.0 copy-start
  64.1 0.0 copy-start.1
  64.1 1.6 %shard_map.115 = bf16[16,128,128]{2,1,0:T(8,128)(2,1)} custom-call(s32[1]{0:T(128)S(6)} %and.10.core_ref, s32[1]{0:T(128)} %bitcast.1.odd_ref, bf16[128,128]{1,0:T(8,128)(2,1)S(1)} %get-tuple-element.20.queries, f32[128,128]{1,0:T(8,128)S(1)} %get-tuple-element.21.old_largest, f32[128,128]{1,0:T(8,128)S(1)} %get-tuple-element.22.old_total, ...), custom_call_target="tpu_custom_call" | custom-call | tf_op jit(solution)/shard_map/pallas_call | solution.py:238
  65.7 6.7 %all-to-all-start.2 = ((bf16[16,128,128]{2,1,0:T(8,128)(2,1)}), bf16[16,128,128]{2,1,0:T(8,128)(2,1)S(1)}, u32[]{:S(2)}, u32[]{:S(2)}) async-start(bf16[16,128,128]{2,1,0:T(8,128)(2,1)} %shard_map.115), calls=%async_computation.2 | async-start | bytes 1048576 | tf_op jit(solution)/shard_map/all_to_all | solution.py:307
  72.3 0.0 copy-done
  72.3 0.0 copy-done.1
  72.3 0.8 %shard_map.117 = (bf16[72,128]{1,0:T(8,128)(2,1)}, bf16[72,128]{1,0:T(8,128)(2,1)}) custom-call(s32[1]{0:T(128)S(6)} %copy.12.length_ref, s32[1]{0:T(128)} %bitcast.place_ref, bf16[32,16,128]{2,1,0:T(8,128)(2,1)S(1)} %all-to-all-done.1.keyvalue, bf16[72,128]{1,0:T(8,128)(2,1)S(1)} %bitcast.20, bf16[72,128]{1,0:T(8,128)(2,1)S(1)} %bitcast.22), custom_call_target="tpu_custom_call" | custom-call | tf_op jit(solution)/shard_map/pallas_call | solution.py:238
  73.2 6.1 %all-to-all-done.2.parts = bf16[16,128,128]{2,1,0:T(8,128)(2,1)S(1)} async-done(((bf16[16,128,128]{2,1,0:T(8,128)(2,1)}), bf16[16,128,128]{2,1,0:T(8,128)(2,1)S(1)}, u32[]{:S(2)}, u32[]{:S(2)}) %all-to-all-start.2) | async-done | bytes 524320 | tf_op jit(solution)/shard_map/all_to_all | solution.py:307
  79.3 0.7 shard_map.116
  (1 shorter events, 0.0 us)
Async XLA Ops:
  2.8 44.5 %all-to-all-start = ((bf16[16,272,128]{2,1,0:T(8,128)(2,1)}), bf16[16,272,128]{2,1,0:T(8,128)(2,1)S(1)}, u32[]{:S(2)}, u32[]{:S(2)}) async-start(bf16[16,272,128]{2,1,0:T(8,128)(2,1)} %get-tuple-element.15), calls=%async_computation | async-start | bytes 2228224 | tf_op jit(solution)/shard_map/all_to_all | solution.py:283
  50.4 6.6 %collective-permute-start = (bf16[16,272,128]{2,1,0:T(8,128)(2,1)}, bf16[16,272,128]{2,1,0:T(8,128)(2,1)S(1)}, u32[]{:S(2)}, u32[]{:S(2)}) collective-permute-start(bf16[16,272,128]{2,1,0:T(8,128)(2,1)} %get-tuple-element.19), channel_id=1, source_target_pairs={{0,16},{16,0},{32,48},{48,32},{64,80},{80,64},{96,112},{112,96},{1... | collective-permute-start | bytes 3342344 | tf_op jit(solution)/shard_map/ppermute | solution.py:294
  52.4 11.7 %all-to-all-start.1 = ((bf16[32,16,128]{2,1,0:T(8,128)(2,1)}), bf16[32,16,128]{2,1,0:T(8,128)(2,1)S(1)}, u32[]{:S(2)}, u32[]{:S(2)}) async-start(bf16[32,16,128]{2,1,0:T(8,128)(2,1)} %get-tuple-element.24), calls=%async_computation.1 | async-start | bytes 262144 | tf_op jit(solution)/shard_map/all_to_all | solution.py:293
  64.1 8.2 %copy-start = (bf16[1,72,128]{2,1,0:T(8,128)(2,1)S(1)}, bf16[1,72,128]{2,1,0:T(8,128)(2,1)}, u32[]{:S(2)}) copy-start(bf16[1,72,128]{2,1,0:T(8,128)(2,1)} %param.15) | copy-start | bytes 55300
  64.1 8.2 %copy-start.1 = (bf16[1,72,128]{2,1,0:T(8,128)(2,1)S(1)}, bf16[1,72,128]{2,1,0:T(8,128)(2,1)}, u32[]{:S(2)}) copy-start(bf16[1,72,128]{2,1,0:T(8,128)(2,1)} %param.16) | copy-start | bytes 55300
  65.7 13.6 %all-to-all-start.2 = ((bf16[16,128,128]{2,1,0:T(8,128)(2,1)}), bf16[16,128,128]{2,1,0:T(8,128)(2,1)S(1)}, u32[]{:S(2)}, u32[]{:S(2)}) async-start(bf16[16,128,128]{2,1,0:T(8,128)(2,1)} %shard_map.115), calls=%async_computation.2 | async-start | bytes 1048576 | tf_op jit(solution)/shard_map/all_to_all | solution.py:307

commit v12 on v11

--- a/solution.py
+++ b/solution.py
@@ -15,7 +15,7 @@
 CHUNKS = FEATURES // LANES
 KV_ROWS = 2 * PAGE
 SEND_ROWS = KV_ROWS + OWN * CHUNKS
-WEIGHT_ROWS = HALF + OWN
+WEIGHT_ROWS = HALF + CORES * OWN
 NEW = 256
 NEGATIVE = -1e30
 
@@ -77,11 +77,6 @@
             ]
 
 
-def part_of(gathered, odd, core, chunk):
-    side = odd if (core + chunk) % CORES == 0 else 1 - odd
-    return gathered.at[side, CHUNKS - 1 - chunk]
-
-
 def gathered_tokens(tokens, chunks=range(CHUNKS)):
     pieces = []
     for chunk in chunks:
@@ -90,17 +85,8 @@
     return jnp.concatenate(pieces, axis=1)
 
 
-def project_keyvalue(odd_ref, tokens, weights, planes, keyvalue, swapped):
-    odd = odd_ref[0]
-    narrow = jnp.concatenate(
-        [
-            jnp.concatenate(
-                [part_of(weights, odd, core, chunk)[...].astype(F32) for core in range(CORES)], axis=0
-            )
-            for chunk in range(CHUNKS)
-        ],
-        axis=1,
-    ).astype(BF16)
+def project_keyvalue(tokens, planes, keyvalue, swapped):
+    narrow = jnp.concatenate([planes[CHUNKS - 1 - chunk, HALF:WEIGHT_ROWS, :] for chunk in range(CHUNKS)], axis=1)
     rounded = dot_nt(narrow, gathered_tokens(tokens)).astype(BF16)
     for place in range(CHIPS * CORES):
         keyvalue[place] = rounded
@@ -259,6 +245,7 @@
     place = lax.axis_index("gx").astype(jnp.int32).reshape(1)
     core = place & 1
     odd = lax.axis_index("gy").astype(jnp.int32).reshape(1) & 1
+    both = lax.all_gather(keyvalue_weight.T, "gx", axis=0, tiled=True, axis_index_groups=ONE_CHIP)
     send, weights = call(
         prepare,
         [((CHIPS, SEND_ROWS, LANES), BF16), ((WEIGHT_ROWS + HALF, LANES), BF16)],
@@ -267,7 +254,7 @@
             norm_gain.reshape(1, FEATURES),
             norm_bias.reshape(1, FEATURES),
             query_weight.T,
-            keyvalue_weight.T,
+            both,
             out_weight,
             key_cache[0],
             value_cache[0],
@@ -283,12 +270,10 @@
     own = lax.all_to_all(send, "gx", 0, 0, tiled=True, axis_index_groups=SAME_CORE)
     planes = lax.all_gather(weights, ("gx", "gy"), axis=0, tiled=False, axis_index_groups=COLUMNS)
     own, planes = lax.optimization_barrier((own, planes))
-    inner = lax.all_gather(planes[:, HALF:WEIGHT_ROWS], "gx", axis=0, tiled=False, axis_index_groups=ONE_CHIP)
     rows, swapped = call(
         project_keyvalue,
         [((CHIPS * CORES, CORES * OWN, LANES), BF16), ((CHIPS, SEND_ROWS, LANES), BF16)],
-        (odd, own, inner, planes),
-        scalars=1,
+        (own, planes),
     )
     keyvalue = lax.all_to_all(rows, "gx", 0, 0, tiled=True)
     peer = lax.ppermute(swapped, "gx", SWAP)

time: 80.4 us -> 82.3 us (1.024)
  blocking collectives: 36.6 us -> 41.5 us
  starting transfers between devices: 22.3 us -> 19.3 us
    all_gather x1, blocking collectives: 1.84 us -> 9.75 us  [body(): lax.all_gather(keyvalue_weight.T, 'gx', axis=0, tiled=True, axis_index_gr...]
    all_to_all x1, starting transfers between devices: 9.73 us -> 6.68 us  [body(): lax.all_to_all(send, 'gx', 0, 0, tiled=True, axis_index_groups=SAME_CORE)]
    all_gather x1, blocking collectives: 34.8 us -> 31.7 us  [body(): lax.all_gather(weights, ('gx', 'gy'), axis=0, tiled=False, axis_index_gro...]
where the time goes in v12:
time: 82.3 us; the launch traced here: 81.8 us
  blocking collectives  41.5 us (50%)
  starting transfers between devices  19.3 us (23%)
  waiting for transfers between devices  11.9 us (14%)
  Pallas kernels  7.7 us (9%)
  between operations  1.34 us (2%)
    all_gather x1, blocking collectives, body(): lax.all_gather(weights, ('gx', 'gy'), axis=0, tiled=False, axis_index_gro...  31.7 us
    all_gather x1, blocking collectives, body(): lax.all_gather(keyvalue_weight.T, 'gx', axis=0, tiled=True, axis_index_gr...  9.75 us
    pallas_call x6, Pallas kernels, call(): pl.pallas_call(kernel, out_shape=[jax.ShapeDtypeStruct(shape, dtype) for...  7.7 us
    all_to_all x1, starting transfers between devices, body(): lax.all_to_all(send, 'gx', 0, 0, tiled=True, axis_index_groups=SAME_CORE)  6.68 us
    all_to_all x1, starting transfers between devices, body(): lax.all_to_all(parts, 'gx', 0, 0, tiled=True, axis_index_groups=SAME_CORE)  6.66 us
    all_to_all x1, waiting for transfers between devices, body(): lax.all_to_all(parts, 'gx', 0, 0, tiled=True, axis_index_groups=SAME_CORE)  6.1 us
    all_to_all x1, waiting for transfers between devices, body(): keyvalue = lax.all_to_all(rows, 'gx', 0, 0, tiled=True)  5.83 us
    all_to_all x1, starting transfers between devices, body(): keyvalue = lax.all_to_all(rows, 'gx', 0, 0, tiled=True)  3.64 us
  transfers between devices with their start and end apart: 4, of which 2 were waited for; matrix products, arithmetic and copies ran while one was open for 0% of the time, Pallas kernels for 3%

profile of v12, /device:TPU:1, one launch (start us, length us, event | category | flops | bytes accessed | tf_op | source)
XLA Modules:
  0.0 81.8 jit_solution(8390115800972675683)
XLA Ops:
  0.6 9.8 %all_gather.9.keyvalue_w = bf16[16,128]{1,0:T(8,128)(2,1)} all-gather(bf16[8,128]{1,0:T(8,128)(2,1)} %bitcast.25), channel_id=1, replica_groups={{0,16},{32,48},{64,80},{96,112},{128,144},{160,176},{192,208},{224,240}..., dimensions={0}, use_global_device_ids=true | all-gather | bytes 6144 | tf_op jit(solution)/shard_map/all_gather | solution.py:248
  10.4 2.1 %shard_map.112 = (bf16[16,272,128]{2,1,0:T(8,128)(2,1)}, bf16[144,128]{1,0:T(8,128)(2,1)S(1)}) custom-call(bf16[8,2048]{1,0:T(8,128)(2,1)} %bitcast.21, f32[1,2048]{1,0:T(1,128)} %bitcast.23, f32[1,2048]{1,0:T(1,128)} %bitcast.24, bf16[64,128]{1,0:T(8,128)(2,1)} %bitcast.22, bf16[16,128]{1,0:T(8,128)(2,1)} %all_gather.9.keyvalue_w, bf16[64,128]{1,0:T(8,128)(2,1)} %out_w.1, ...), custom_call_target="tpu_custom_call" | custom-call | tf_op jit(solution)/shard_map/pallas_call | solution.py:224
  12.5 6.7 %all-to-all-start = ((bf16[16,272,128]{2,1,0:T(8,128)(2,1)}), bf16[16,272,128]{2,1,0:T(8,128)(2,1)S(1)}, u32[]{:S(2)}, u32[]{:S(2)}) async-start(bf16[16,272,128]{2,1,0:T(8,128)(2,1)} %get-tuple-element.15), calls=%async_computation | async-start | bytes 2228224 | tf_op jit(solution)/shard_map/all_to_all | solution.py:270
  19.2 31.7 %all-gather = bf16[2304,128]{1,0:T(8,128)(2,1)S(1)} all-gather(bf16[144,128]{1,0:T(8,128)(2,1)S(1)} %get-tuple-element.16), channel_id=2, replica_groups={{31,14,29,12,27,10,25,8,23,6,21,4,19,2,17,0},{15,30,13,28,11,26,9,24,7,..., dimensions={0}, use_global_device_ids=true | all-gather | bytes 626688 | tf_op jit(solution)/shard_map/all_gather | solution.py:271
  50.9 0.0 all-to-all-done.tokens.own
  50.9 1.2 %shard_map.113 = (bf16[32,16,128]{2,1,0:T(8,128)(2,1)}, bf16[16,272,128]{2,1,0:T(8,128)(2,1)}) custom-call(bf16[16,272,128]{2,1,0:T(8,128)(2,1)S(1)} %all-to-all-done.tokens.own, bf16[16,144,128]{2,1,0:T(8,128)(2,1)S(1)} %bitcast.13), custom_call_target="tpu_custom_call" | custom-call | tf_op jit(solution)/shard_map/pallas_call | solution.py:224
  52.1 2.3 %collective-permute-start = (bf16[16,272,128]{2,1,0:T(8,128)(2,1)}, bf16[16,272,128]{2,1,0:T(8,128)(2,1)S(1)}, u32[]{:S(2)}, u32[]{:S(2)}) collective-permute-start(bf16[16,272,128]{2,1,0:T(8,128)(2,1)} %get-tuple-element.19), channel_id=1, source_target_pairs={{0,16},{16,0},{32,48},{48,32},{64,80},{80,64},{96,112},{112,96},{1... | collective-permute-start | bytes 3342344 | tf_op jit(solution)/shard_map/ppermute | solution.py:279
  54.4 3.6 %all-to-all-start.1 = ((bf16[32,16,128]{2,1,0:T(8,128)(2,1)}), bf16[32,16,128]{2,1,0:T(8,128)(2,1)S(1)}, u32[]{:S(2)}, u32[]{:S(2)}) async-start(bf16[32,16,128]{2,1,0:T(8,128)(2,1)} %get-tuple-element.24), calls=%async_computation.1 | async-start | bytes 262144 | tf_op jit(solution)/shard_map/all_to_all | solution.py:278
  58.7 0.0 collective-permute-done.peer
  58.8 1.3 %shard_map.114 = (bf16[128,128]{1,0:T(8,128)(2,1)S(1)}, f32[128,128]{1,0:T(8,128)S(1)}, f32[128,128]{1,0:T(8,128)S(1)}, f32[128,128]{1,0:T(8,128)S(1)}) custom-call(s32[1]{0:T(128)S(6)} %copy.12.length_ref, s32[1]{0:T(128)} %bitcast.1.odd_ref, s32[1]{0:T(128)S(6)} %and.10.core_ref, bf16[16,272,128]{2,1,0:T(8,128)(2,1)S(1)} %all-to-all-done.tokens.own, ...), custom_call_target="tpu_custom_call" | custom-call | tf_op jit(solution)/shard_map/pallas_call | solution.py:224
  60.0 5.8 %all-to-all-done.1.keyvalue = bf16[32,16,128]{2,1,0:T(8,128)(2,1)S(1)} async-done(((bf16[32,16,128]{2,1,0:T(8,128)(2,1)}), bf16[32,16,128]{2,1,0:T(8,128)(2,1)S(1)}, u32[]{:S(2)}, u32[]{:S(2)}) %all-to-all-start.1) | async-done | bytes 131104 | tf_op jit(solution)/shard_map/all_to_all | solution.py:278
  65.9 0.0 copy-start
  65.9 0.0 copy-start.1
  65.9 1.6 %shard_map.115 = bf16[16,128,128]{2,1,0:T(8,128)(2,1)} custom-call(s32[1]{0:T(128)S(6)} %and.10.core_ref, s32[1]{0:T(128)} %bitcast.1.odd_ref, bf16[128,128]{1,0:T(8,128)(2,1)S(1)} %get-tuple-element.20.queries, f32[128,128]{1,0:T(8,128)S(1)} %get-tuple-element.21.old_largest, f32[128,128]{1,0:T(8,128)S(1)} %get-tuple-element.22.old_total, ...), custom_call_target="tpu_custom_call" | custom-call | tf_op jit(solution)/shard_map/pallas_call | solution.py:224
  67.5 6.7 %all-to-all-start.2 = ((bf16[16,128,128]{2,1,0:T(8,128)(2,1)}), bf16[16,128,128]{2,1,0:T(8,128)(2,1)S(1)}, u32[]{:S(2)}, u32[]{:S(2)}) async-start(bf16[16,128,128]{2,1,0:T(8,128)(2,1)} %shard_map.115), calls=%async_computation.2 | async-start | bytes 1048576 | tf_op jit(solution)/shard_map/all_to_all | solution.py:292
  74.1 0.0 copy-done
  74.1 0.0 copy-done.1
  74.1 0.8 %shard_map.117 = (bf16[72,128]{1,0:T(8,128)(2,1)}, bf16[72,128]{1,0:T(8,128)(2,1)}) custom-call(s32[1]{0:T(128)S(6)} %copy.12.length_ref, s32[1]{0:T(128)} %bitcast.place_ref, bf16[32,16,128]{2,1,0:T(8,128)(2,1)S(1)} %all-to-all-done.1.keyvalue, bf16[72,128]{1,0:T(8,128)(2,1)S(1)} %bitcast.17, bf16[72,128]{1,0:T(8,128)(2,1)S(1)} %bitcast.19), custom_call_target="tpu_custom_call" | custom-call | tf_op jit(solution)/shard_map/pallas_call | solution.py:224
  75.0 6.1 %all-to-all-done.2.parts = bf16[16,128,128]{2,1,0:T(8,128)(2,1)S(1)} async-done(((bf16[16,128,128]{2,1,0:T(8,128)(2,1)}), bf16[16,128,128]{2,1,0:T(8,128)(2,1)S(1)}, u32[]{:S(2)}, u32[]{:S(2)}) %all-to-all-start.2) | async-done | bytes 524320 | tf_op jit(solution)/shard_map/all_to_all | solution.py:292
  81.1 0.7 shard_map.116
Async XLA Ops:
  12.5 38.4 %all-to-all-start = ((bf16[16,272,128]{2,1,0:T(8,128)(2,1)}), bf16[16,272,128]{2,1,0:T(8,128)(2,1)S(1)}, u32[]{:S(2)}, u32[]{:S(2)}) async-start(bf16[16,272,128]{2,1,0:T(8,128)(2,1)} %get-tuple-element.15), calls=%async_computation | async-start | bytes 2228224 | tf_op jit(solution)/shard_map/all_to_all | solution.py:270
  52.1 6.6 %collective-permute-start = (bf16[16,272,128]{2,1,0:T(8,128)(2,1)}, bf16[16,272,128]{2,1,0:T(8,128)(2,1)S(1)}, u32[]{:S(2)}, u32[]{:S(2)}) collective-permute-start(bf16[16,272,128]{2,1,0:T(8,128)(2,1)} %get-tuple-element.19), channel_id=1, source_target_pairs={{0,16},{16,0},{32,48},{48,32},{64,80},{80,64},{96,112},{112,96},{1... | collective-permute-start | bytes 3342344 | tf_op jit(solution)/shard_map/ppermute | solution.py:279
  54.4 11.4 %all-to-all-start.1 = ((bf16[32,16,128]{2,1,0:T(8,128)(2,1)}), bf16[32,16,128]{2,1,0:T(8,128)(2,1)S(1)}, u32[]{:S(2)}, u32[]{:S(2)}) async-start(bf16[32,16,128]{2,1,0:T(8,128)(2,1)} %get-tuple-element.24), calls=%async_computation.1 | async-start | bytes 262144 | tf_op jit(solution)/shard_map/all_to_all | solution.py:278
  65.9 8.2 %copy-start = (bf16[1,72,128]{2,1,0:T(8,128)(2,1)S(1)}, bf16[1,72,128]{2,1,0:T(8,128)(2,1)}, u32[]{:S(2)}) copy-start(bf16[1,72,128]{2,1,0:T(8,128)(2,1)} %param.15) | copy-start | bytes 55300
  65.9 8.2 %copy-start.1 = (bf16[1,72,128]{2,1,0:T(8,128)(2,1)S(1)}, bf16[1,72,128]{2,1,0:T(8,128)(2,1)}, u32[]{:S(2)}) copy-start(bf16[1,72,128]{2,1,0:T(8,128)(2,1)} %param.16) | copy-start | bytes 55300
  67.5 13.6 %all-to-all-start.2 = ((bf16[16,128,128]{2,1,0:T(8,128)(2,1)}), bf16[16,128,128]{2,1,0:T(8,128)(2,1)S(1)}, u32[]{:S(2)}, u32[]{:S(2)}) async-start(bf16[16,128,128]{2,1,0:T(8,128)(2,1)} %shard_map.115), calls=%async_computation.2 | async-start | bytes 1048576 | tf_op jit(solution)/shard_map/all_to_all | solution.py:292

commit v13 on v11

--- a/solution.py
+++ b/solution.py
@@ -192,13 +192,26 @@
     turned = pltpu.roll(attended, HALF, 1)
     same = (core + odd_ref[0]) % CORES == 0
     sides = (jnp.where(same, attended, turned).astype(BF16), jnp.where(same, turned, attended).astype(BF16))
-    for chunk in range(CHUNKS):
-        at = CHUNKS - 1 - chunk
-        square = jnp.concatenate(
-            [planes[at, WEIGHT_ROWS : WEIGHT_ROWS + HALF, :], peer[at, KV_ROWS : KV_ROWS + HALF, :]], axis=0
+    for parity in range(2):
+        chunks = range(parity, CHUNKS, 2)
+        wide = jnp.concatenate(
+            [
+                jnp.concatenate(
+                    [
+                        planes[CHUNKS - 1 - chunk, WEIGHT_ROWS : WEIGHT_ROWS + HALF, :],
+                        peer[CHUNKS - 1 - chunk, KV_ROWS : KV_ROWS + HALF, :],
+                    ],
+                    axis=0,
+                )
+                for chunk in chunks
+            ],
+            axis=1,
         )
-        part = dot(sides[chunk % 2], square)
-        result[:, OWN * chunk : OWN * (chunk + 1), :] = part.reshape(CHIPS, OWN, LANES).astype(BF16)
+        part = dot(sides[parity], wide)
+        for at, chunk in enumerate(chunks):
+            result[:, OWN * chunk : OWN * (chunk + 1), :] = (
+                part[:, LANES * at : LANES * (at + 1)].reshape(CHIPS, OWN, LANES).astype(BF16)
+            )
 
 
 def add_heads(parts, result):

time: 80.4 us -> 80.4 us (level)
  no operation moved by 1% of the time
where the time goes in v13:
time: 80.4 us; the launch traced here: 80 us
  blocking collectives  36.6 us (46%)
  starting transfers between devices  22.3 us (28%)
  waiting for transfers between devices  12 us (15%)
  Pallas kernels  7.71 us (10%)
  between operations  1.34 us (2%)
    all_gather x1, blocking collectives, body(): lax.all_gather(weights, ('gx', 'gy'), axis=0, tiled=False, axis_index_gro...  34.8 us
    all_to_all x1, starting transfers between devices, body(): lax.all_to_all(send, 'gx', 0, 0, tiled=True, axis_index_groups=SAME_CORE)  9.73 us
    pallas_call x6, Pallas kernels, call(): pl.pallas_call(kernel, out_shape=[jax.ShapeDtypeStruct(shape, dtype) for...  7.71 us
    all_to_all x1, starting transfers between devices, body(): lax.all_to_all(parts, 'gx', 0, 0, tiled=True, axis_index_groups=SAME_CORE)  6.66 us
    all_to_all x1, waiting for transfers between devices, body(): lax.all_to_all(parts, 'gx', 0, 0, tiled=True, axis_index_groups=SAME_CORE)  6.1 us
    all_to_all x1, waiting for transfers between devices, body(): keyvalue = lax.all_to_all(rows, 'gx', 0, 0, tiled=True)  5.85 us
    all_to_all x1, starting transfers between devices, body(): keyvalue = lax.all_to_all(rows, 'gx', 0, 0, tiled=True)  3.86 us
    ppermute x1, starting transfers between devices, body(): peer = lax.ppermute(swapped, 'gx', SWAP)  2.06 us
  transfers between devices with their start and end apart: 4, of which 2 were waited for; matrix products, arithmetic and copies ran while one was open for 0% of the time, Pallas kernels for 3%

profile of v13, /device:TPU:1, one launch (start us, length us, event | category | flops | bytes accessed | tf_op | source)
XLA Modules:
  0.0 80.0 jit_solution(12969369296736403572)
XLA Ops:
  0.6 2.1 %shard_map.112 = (bf16[16,272,128]{2,1,0:T(8,128)(2,1)}, bf16[136,128]{1,0:T(8,128)(2,1)S(1)}) custom-call(bf16[8,2048]{1,0:T(8,128)(2,1)} %bitcast.24, f32[1,2048]{1,0:T(1,128)} %bitcast.26, f32[1,2048]{1,0:T(1,128)} %bitcast.27, bf16[64,128]{1,0:T(8,128)(2,1)} %bitcast.25, bf16[8,128]{1,0:T(8,128)(2,1)} %bitcast.28, bf16[64,128]{1,0:T(8,128)(2,1)} %out_w.1, ...), custom_call_target="tpu_custom_call" | custom-call | tf_op jit(solution)/shard_map/pallas_call | solution.py:251
  2.8 9.7 %all-to-all-start = ((bf16[16,272,128]{2,1,0:T(8,128)(2,1)}), bf16[16,272,128]{2,1,0:T(8,128)(2,1)S(1)}, u32[]{:S(2)}, u32[]{:S(2)}) async-start(bf16[16,272,128]{2,1,0:T(8,128)(2,1)} %get-tuple-element.15), calls=%async_computation | async-start | bytes 2228224 | tf_op jit(solution)/shard_map/all_to_all | solution.py:296
  12.5 34.8 %all-gather = bf16[2176,128]{1,0:T(8,128)(2,1)S(1)} all-gather(bf16[136,128]{1,0:T(8,128)(2,1)S(1)} %get-tuple-element.16), channel_id=2, replica_groups={{31,14,29,12,27,10,25,8,23,6,21,4,19,2,17,0},{15,30,13,28,11,26,9,24,7,..., dimensions={0}, use_global_device_ids=true | all-gather | bytes 591872 | tf_op jit(solution)/shard_map/all_gather | solution.py:297
  47.3 0.0 all-to-all-done.tokens.own
  47.3 1.8 %all-gather.1 = bf16[32,8,128]{2,1,0:T(8,128)(2,1)S(1)} all-gather(bf16[16,8,128]{2,1,0:T(8,128)(2,1)S(1)} %slice.3), channel_id=3, replica_groups={{0,16},{32,48},{64,80},{96,112},{128,144},{160,176},{192,208},{224,240}..., dimensions={0}, use_global_device_ids=true | all-gather | bytes 98304 | tf_op jit(solution)/shard_map/all_gather | solution.py:299
  49.1 1.2 %shard_map.113 = (bf16[32,16,128]{2,1,0:T(8,128)(2,1)}, bf16[16,272,128]{2,1,0:T(8,128)(2,1)}) custom-call(s32[1]{0:T(128)} %bitcast.1.odd_ref, bf16[16,272,128]{2,1,0:T(8,128)(2,1)S(1)} %all-to-all-done.tokens.own, bf16[2,16,8,128]{3,2,1,0:T(8,128)(2,1)S(1)} %bitcast.18, bf16[16,136,128]{2,1,0:T(8,128)(2,1)S(1)} %bitcast.15), custom_call_target="tpu_custom_call" | custom-call | tf_op jit(solution)/shard_map/pallas_call | solution.py:251
  50.4 2.1 %collective-permute-start = (bf16[16,272,128]{2,1,0:T(8,128)(2,1)}, bf16[16,272,128]{2,1,0:T(8,128)(2,1)S(1)}, u32[]{:S(2)}, u32[]{:S(2)}) collective-permute-start(bf16[16,272,128]{2,1,0:T(8,128)(2,1)} %get-tuple-element.19), channel_id=1, source_target_pairs={{0,16},{16,0},{32,48},{48,32},{64,80},{80,64},{96,112},{112,96},{1... | collective-permute-start | bytes 3342344 | tf_op jit(solution)/shard_map/ppermute | solution.py:307
  52.4 3.9 %all-to-all-start.1 = ((bf16[32,16,128]{2,1,0:T(8,128)(2,1)}), bf16[32,16,128]{2,1,0:T(8,128)(2,1)S(1)}, u32[]{:S(2)}, u32[]{:S(2)}) async-start(bf16[32,16,128]{2,1,0:T(8,128)(2,1)} %get-tuple-element.24), calls=%async_computation.1 | async-start | bytes 262144 | tf_op jit(solution)/shard_map/all_to_all | solution.py:306
  56.9 0.0 collective-permute-done.peer
  56.9 1.3 %shard_map.114 = (bf16[128,128]{1,0:T(8,128)(2,1)S(1)}, f32[128,128]{1,0:T(8,128)S(1)}, f32[128,128]{1,0:T(8,128)S(1)}, f32[128,128]{1,0:T(8,128)S(1)}) custom-call(s32[1]{0:T(128)S(6)} %copy.12.length_ref, s32[1]{0:T(128)} %bitcast.1.odd_ref, s32[1]{0:T(128)S(6)} %and.10.core_ref, bf16[16,272,128]{2,1,0:T(8,128)(2,1)S(1)} %all-to-all-done.tokens.own, ...), custom_call_target="tpu_custom_call" | custom-call | tf_op jit(solution)/shard_map/pallas_call | solution.py:251
  58.2 5.9 %all-to-all-done.1.keyvalue = bf16[32,16,128]{2,1,0:T(8,128)(2,1)S(1)} async-done(((bf16[32,16,128]{2,1,0:T(8,128)(2,1)}), bf16[32,16,128]{2,1,0:T(8,128)(2,1)S(1)}, u32[]{:S(2)}, u32[]{:S(2)}) %all-to-all-start.1) | async-done | bytes 131104 | tf_op jit(solution)/shard_map/all_to_all | solution.py:306
  64.1 0.0 copy-start
  64.1 0.0 copy-start.1
  64.1 1.6 %shard_map.115 = bf16[16,128,128]{2,1,0:T(8,128)(2,1)} custom-call(s32[1]{0:T(128)S(6)} %and.10.core_ref, s32[1]{0:T(128)} %bitcast.1.odd_ref, bf16[128,128]{1,0:T(8,128)(2,1)S(1)} %get-tuple-element.20.queries, f32[128,128]{1,0:T(8,128)S(1)} %get-tuple-element.21.old_largest, f32[128,128]{1,0:T(8,128)S(1)} %get-tuple-element.22.old_total, ...), custom_call_target="tpu_custom_call" | custom-call | tf_op jit(solution)/shard_map/pallas_call | solution.py:251
  65.7 6.7 %all-to-all-start.2 = ((bf16[16,128,128]{2,1,0:T(8,128)(2,1)}), bf16[16,128,128]{2,1,0:T(8,128)(2,1)S(1)}, u32[]{:S(2)}, u32[]{:S(2)}) async-start(bf16[16,128,128]{2,1,0:T(8,128)(2,1)} %shard_map.115), calls=%async_computation.2 | async-start | bytes 1048576 | tf_op jit(solution)/shard_map/all_to_all | solution.py:320
  72.3 0.0 copy-done
  72.3 0.0 copy-done.1
  72.3 0.8 %shard_map.117 = (bf16[72,128]{1,0:T(8,128)(2,1)}, bf16[72,128]{1,0:T(8,128)(2,1)}) custom-call(s32[1]{0:T(128)S(6)} %copy.12.length_ref, s32[1]{0:T(128)} %bitcast.place_ref, bf16[32,16,128]{2,1,0:T(8,128)(2,1)S(1)} %all-to-all-done.1.keyvalue, bf16[72,128]{1,0:T(8,128)(2,1)S(1)} %bitcast.20, bf16[72,128]{1,0:T(8,128)(2,1)S(1)} %bitcast.22), custom_call_target="tpu_custom_call" | custom-call | tf_op jit(solution)/shard_map/pallas_call | solution.py:251
  73.2 6.1 %all-to-all-done.2.parts = bf16[16,128,128]{2,1,0:T(8,128)(2,1)S(1)} async-done(((bf16[16,128,128]{2,1,0:T(8,128)(2,1)}), bf16[16,128,128]{2,1,0:T(8,128)(2,1)S(1)}, u32[]{:S(2)}, u32[]{:S(2)}) %all-to-all-start.2) | async-done | bytes 524320 | tf_op jit(solution)/shard_map/all_to_all | solution.py:320
  79.3 0.7 shard_map.116
  (1 shorter events, 0.0 us)
Async XLA Ops:
  2.8 44.5 %all-to-all-start = ((bf16[16,272,128]{2,1,0:T(8,128)(2,1)}), bf16[16,272,128]{2,1,0:T(8,128)(2,1)S(1)}, u32[]{:S(2)}, u32[]{:S(2)}) async-start(bf16[16,272,128]{2,1,0:T(8,128)(2,1)} %get-tuple-element.15), calls=%async_computation | async-start | bytes 2228224 | tf_op jit(solution)/shard_map/all_to_all | solution.py:296
  50.4 6.6 %collective-permute-start = (bf16[16,272,128]{2,1,0:T(8,128)(2,1)}, bf16[16,272,128]{2,1,0:T(8,128)(2,1)S(1)}, u32[]{:S(2)}, u32[]{:S(2)}) collective-permute-start(bf16[16,272,128]{2,1,0:T(8,128)(2,1)} %get-tuple-element.19), channel_id=1, source_target_pairs={{0,16},{16,0},{32,48},{48,32},{64,80},{80,64},{96,112},{112,96},{1... | collective-permute-start | bytes 3342344 | tf_op jit(solution)/shard_map/ppermute | solution.py:307
  52.4 11.7 %all-to-all-start.1 = ((bf16[32,16,128]{2,1,0:T(8,128)(2,1)}), bf16[32,16,128]{2,1,0:T(8,128)(2,1)S(1)}, u32[]{:S(2)}, u32[]{:S(2)}) async-start(bf16[32,16,128]{2,1,0:T(8,128)(2,1)} %get-tuple-element.24), calls=%async_computation.1 | async-start | bytes 262144 | tf_op jit(solution)/shard_map/all_to_all | solution.py:306
  64.1 8.2 %copy-start = (bf16[1,72,128]{2,1,0:T(8,128)(2,1)S(1)}, bf16[1,72,128]{2,1,0:T(8,128)(2,1)}, u32[]{:S(2)}) copy-start(bf16[1,72,128]{2,1,0:T(8,128)(2,1)} %param.15) | copy-start | bytes 55300
  64.1 8.2 %copy-start.1 = (bf16[1,72,128]{2,1,0:T(8,128)(2,1)S(1)}, bf16[1,72,128]{2,1,0:T(8,128)(2,1)}, u32[]{:S(2)}) copy-start(bf16[1,72,128]{2,1,0:T(8,128)(2,1)} %param.16) | copy-start | bytes 55300
  65.7 13.6 %all-to-all-start.2 = ((bf16[16,128,128]{2,1,0:T(8,128)(2,1)}), bf16[16,128,128]{2,1,0:T(8,128)(2,1)S(1)}, u32[]{:S(2)}, u32[]{:S(2)}) async-start(bf16[16,128,128]{2,1,0:T(8,128)(2,1)} %shard_map.115), calls=%async_computation.2 | async-start | bytes 1048576 | tf_op jit(solution)/shard_map/all_to_all | solution.py:320
